TPU v7x, 128 devices: a whole 4x4x4 slice. The times are simulated.
128 devices in a mesh: rep: 4 (over z_lo, core), shard: 32 (over z_hi, y, x).
Axes of the slice: x: 4, y: 4, z: 4 (z_hi: 2, z_lo: 2; z = z_hi * 2 + z_lo), core: 2. Of those that a mesh axis runs over, the one named last changes fastest.
Arguments:
- inputs: float32 [32, 512, 1024], P('shard', 'rep'), may hold values from -6 to 6
- segment_ids: int32 [32, 512], P('shard', 'rep'), may hold values from 0 to 3, never falling along the last dimension, each value on 1 to 200 neighbouring positions
- cotangent: float32 [32, 512, 1024], P('shard', 'rep'), may hold values from -6 to 6
- w_qkv: bfloat16 [1, 1024, 3072], P(None, 'shard'), may hold values from -0.1875 to 0.1875
- w_out: bfloat16 [1, 1024, 1024], P(None, 'shard'), may hold values from -0.75 to 0.75
- w_up: bfloat16 [1, 1024, 4096], P(None, 'shard'), may hold values from -0.1875 to 0.1875
- w_down: bfloat16 [1, 4096, 1024], P(None, 'shard'), may hold values from -0.09375 to 0.09375
- biases: bfloat16 [1, 6, 1024], P(None, None, 'shard'), may hold values from -3 to 3
- norm_gains: bfloat16 [1, 2, 1024], P(None, None, 'shard'), may hold values from 0.5 to 1.5
- up_bias: bfloat16 [1, 4096], P(None, 'shard'), may hold values from -3 to 3
Outputs:
- outputs: float32 [32, 512, 1024], P('shard', 'rep')
- input_grad: float32 [32, 512, 1024], P('shard', 'rep')
- grad_w_qkv: float32 [1, 1024, 3072], P(None, 'shard')
- grad_w_out: float32 [1, 1024, 1024], P(None, 'shard')
- grad_w_up: float32 [1, 1024, 4096], P(None, 'shard')
- grad_w_down: float32 [1, 4096, 1024], P(None, 'shard')
- grad_biases: float32 [1, 6, 1024], P(None, None, 'shard')
- grad_norm_gains: float32 [1, 2, 1024], P(None, None, 'shard')
- grad_up_bias: float32 [1, 4096], P(None, 'shard')
Inputs may be any that keep to these rules, and one draw needn't show every extreme that they name: `segment_ids`: within each sequence the id never falls along the positions; ids of different sequences are unrelated.
All inputs are finite; a program needn't handle non-finite values.
Results may differ from a plain program's by a relative error of at most 0.025.
Values may be sent and summed in bfloat16 or wider, within the bound.
A program may use at most 128 MiB of HBM per device.

v0:
```python
import math

import jax
import jax.numpy as jnp
from jax import lax
from jax.sharding import PartitionSpec as P

D = 1024
HEADS = 16
HEAD_DIM = 64
LAYERS = 1


epsilon = 1e-06


def normalize(residual):
    center = residual - jnp.mean(residual, axis=-1, keepdims=True)
    rstd_val = lax.rsqrt(jnp.mean(center * center, axis=-1, keepdims=True) + epsilon)
    return (center * rstd_val, rstd_val)


def norm_back(grad_out, x_hat, rstd_val, gain_row):
    d_hat = grad_out * gain_row
    return rstd_val * (
        d_hat
        - jnp.mean(d_hat, axis=-1, keepdims=True)
        - x_hat * jnp.mean(d_hat * x_hat, axis=-1, keepdims=True)
    )


def gelu_pair(pre_act):
    normal_cdf = 0.5 * (1.0 + lax.erf(pre_act * (1.0 / math.sqrt(2.0))))
    density = jnp.exp(-0.5 * pre_act * pre_act) * (1.0 / math.sqrt(2.0 * math.pi))
    return (pre_act * normal_cdf, normal_cdf + pre_act * density)


def matmul(first_op, second_op):
    return jnp.dot(first_op, second_op, preferred_element_type=jnp.float32)


def matmul_lt(first_op, second_op):
    return lax.dot_general(
        first_op, second_op, (((0,), (0,)), ((), ())), preferred_element_type=jnp.float32
    )


def matmul_rt(first_op, second_op):
    return lax.dot_general(
        first_op, second_op, (((1,), (1,)), ((), ())), preferred_element_type=jnp.float32
    )


def attention_scores(queries, keys_all, seg_rows, seg_cols):
    scores = jnp.einsum(
        "sqhe,skhe->shqk", queries, keys_all, preferred_element_type=jnp.float32
    ) * (1.0 / math.sqrt(HEAD_DIM))
    allowed = seg_rows[:, None, :, None] == seg_cols[:, None, None, :]
    return (scores, allowed)


def forward_layer(hidden, seg_rows, weights):
    w_qkv, w_out, w_up, w_down, biases, norm_gains, up_bias = weights
    seq_count = hidden.shape[0]
    rows_f32 = hidden.reshape(-1, D)
    rows_bf = rows_f32.astype(jnp.bfloat16)
    qkv_rows = matmul(rows_bf, w_qkv)
    queries = (
        (qkv_rows[:, :D] + biases[0]).astype(jnp.bfloat16).reshape(seq_count, -1, HEADS, HEAD_DIM)
    )
    keys_local = qkv_rows[:, D : 2 * D].astype(jnp.bfloat16)
    values_local = (qkv_rows[:, 2 * D :] + biases[1]).astype(jnp.bfloat16)
    local_pair = jnp.concatenate([keys_local, values_local], axis=-1).reshape(seq_count, -1, 2 * D)
    pair_all, seg_cols = (
        lax.all_gather(local_pair, "rep", axis=1, tiled=True),
        lax.all_gather(seg_rows, "rep", axis=1, tiled=True),
    )
    keys_all = pair_all[:, :, :D].reshape(seq_count, -1, HEADS, HEAD_DIM)
    values_all = pair_all[:, :, D:].reshape(seq_count, -1, HEADS, HEAD_DIM)
    scores, allowed = attention_scores(queries, keys_all, seg_rows, seg_cols)
    expo_all = jnp.where(allowed, jnp.exp(scores), 0.0)
    row_total = jnp.sum(expo_all, axis=-1, keepdims=True)
    log_total = jnp.log(row_total)
    attn_probs = (expo_all / row_total).astype(jnp.bfloat16)
    context = (
        jnp.einsum("shqk,skhe->sqhe", attn_probs, values_all, preferred_element_type=jnp.float32)
        .astype(jnp.bfloat16)
        .reshape(-1, D)
    )
    first_sum = rows_f32 + matmul(context, w_out) + biases[2]
    norm_one, rstd_one = normalize(first_sum)
    mid_norm = norm_one * norm_gains[0] + biases[3]
    mid_b = mid_norm.astype(jnp.bfloat16)
    pre_act = matmul(mid_b, w_up) + up_bias
    act_f32, gelu_slope = gelu_pair(pre_act)
    act_b = act_f32.astype(jnp.bfloat16)
    second_sum = mid_norm + matmul(act_b, w_down) + biases[4]
    norm_two, rstd_two = normalize(second_sum)
    layer_out = norm_two * norm_gains[1] + biases[5]
    saved = (
        rows_bf,
        queries,
        keys_all,
        values_all,
        seg_cols,
        log_total,
        context,
        norm_one,
        rstd_one,
        mid_b,
        gelu_slope,
        act_b,
        norm_two,
        rstd_two,
    )
    return (layer_out.reshape(hidden.shape), saved)


def backward_layer(grad_rows, seg_rows, weights, saved):
    w_qkv, w_out, w_up, w_down, biases, norm_gains, up_bias = weights
    (
        rows_bf,
        queries,
        keys_all,
        values_all,
        seg_cols,
        log_total,
        context,
        norm_one,
        rstd_one,
        mid_b,
        gelu_slope,
        act_b,
        norm_two,
        rstd_two,
    ) = saved
    seq_count = queries.shape[0]
    d_gain_two = jnp.sum(grad_rows * norm_two, axis=0)
    d_bias_two = jnp.sum(grad_rows, axis=0)
    d_second = norm_back(grad_rows, norm_two, rstd_two, norm_gains[1])
    d_second_b = d_second.astype(jnp.bfloat16)
    d_bdown = jnp.sum(d_second, axis=0)
    d_wdown = matmul_lt(act_b, d_second_b)
    d_pre = matmul_rt(d_second_b, w_down) * gelu_slope
    d_bup = jnp.sum(d_pre, axis=0)
    d_pre_b = d_pre.astype(jnp.bfloat16)
    d_wup = matmul_lt(mid_b, d_pre_b)
    d_mid = d_second + matmul_rt(d_pre_b, w_up)
    d_gain_one = jnp.sum(d_mid * norm_one, axis=0)
    d_bias_one = jnp.sum(d_mid, axis=0)
    d_first = norm_back(d_mid, norm_one, rstd_one, norm_gains[0])
    d_first_b = d_first.astype(jnp.bfloat16)
    d_bout = jnp.sum(d_first, axis=0)
    d_wout = matmul_lt(context, d_first_b)
    d_context = (
        matmul_rt(d_first_b, w_out).astype(jnp.bfloat16).reshape(seq_count, -1, HEADS, HEAD_DIM)
    )
    scores, allowed = attention_scores(queries, keys_all, seg_rows, seg_cols)
    probs_again = jnp.where(allowed, jnp.exp(scores - log_total), 0.0)
    d_probs = jnp.einsum(
        "sqhe,skhe->shqk", d_context, values_all, preferred_element_type=jnp.float32
    )
    d_scores = (
        probs_again
        * (d_probs - jnp.sum(probs_again * d_probs, axis=-1, keepdims=True))
        * (1.0 / math.sqrt(HEAD_DIM))
    ).astype(jnp.bfloat16)
    d_queries = jnp.einsum(
        "shqk,skhe->sqhe", d_scores, keys_all, preferred_element_type=jnp.float32
    ).reshape(-1, D)
    d_keys = jnp.einsum(
        "shqk,sqhe->skhe", d_scores, queries, preferred_element_type=jnp.float32
    ).reshape(seq_count, -1, D)
    d_values = jnp.einsum(
        "shqk,sqhe->skhe",
        probs_again.astype(jnp.bfloat16),
        d_context,
        preferred_element_type=jnp.float32,
    ).reshape(seq_count, -1, D)
    d_pair = (
        lax.psum_scatter(
            jnp.concatenate([d_keys, d_values], axis=-1).astype(jnp.bfloat16),
            "rep",
            scatter_dimension=1,
            tiled=True,
        )
        .astype(jnp.float32)
        .reshape(-1, 2 * D)
    )
    d_qkv = jnp.concatenate([d_queries, d_pair], axis=-1).astype(jnp.bfloat16)
    d_wqkv = matmul_lt(rows_bf, d_qkv)
    d_hidden = d_first + matmul_rt(d_qkv, w_qkv)
    d_biases = jnp.stack(
        [
            jnp.sum(d_queries, axis=0),
            jnp.sum(d_pair[:, D:], axis=0),
            d_bout,
            d_bias_one,
            d_bdown,
            d_bias_two,
        ]
    )
    d_gains = jnp.stack([d_gain_one, d_gain_two])
    return (d_hidden, (d_wqkv, d_wout, d_wup, d_wdown, d_biases, d_gains, d_bup))


def local(inputs, segment_ids, cotangent, w_qkv, w_out, w_up, w_down, biases, norm_gains, up_bias):
    hidden = inputs
    layer_id = 0
    weights = (
        lax.all_gather(w_qkv[layer_id], "shard", axis=0, tiled=True),
        lax.all_gather(w_out[layer_id], "shard", axis=0, tiled=True),
        lax.all_gather(w_up[layer_id], "shard", axis=0, tiled=True),
        lax.all_gather(w_down[layer_id], "shard", axis=0, tiled=True),
        lax.all_gather(biases[layer_id], "shard", axis=1, tiled=True),
        lax.all_gather(norm_gains[layer_id], "shard", axis=1, tiled=True),
        lax.all_gather(up_bias[layer_id], "shard", axis=0, tiled=True),
    )
    kept_weights = [weights]
    hidden, saved = forward_layer(hidden, segment_ids, weights)
    saved_list = [saved]
    grad_rows = cotangent.reshape(-1, cotangent.shape[-1])
    layer_shares = [None] * LAYERS
    for layer_id in reversed(range(LAYERS)):
        weights = kept_weights[layer_id]
        grad_rows, grads = backward_layer(grad_rows, segment_ids, weights, saved_list[layer_id])
        shares = (
            lax.psum_scatter(
                grads[0].astype(jnp.bfloat16), "shard", scatter_dimension=0, tiled=True
            ).astype(jnp.float32),
            lax.psum_scatter(
                grads[1].astype(jnp.bfloat16), "shard", scatter_dimension=0, tiled=True
            ).astype(jnp.float32),
            lax.psum_scatter(
                grads[2].astype(jnp.bfloat16), "shard", scatter_dimension=0, tiled=True
            ).astype(jnp.float32),
            lax.psum_scatter(
                grads[3].astype(jnp.bfloat16), "shard", scatter_dimension=0, tiled=True
            ).astype(jnp.float32),
            lax.psum_scatter(
                grads[4].astype(jnp.bfloat16), "shard", scatter_dimension=1, tiled=True
            ).astype(jnp.float32),
            lax.psum_scatter(
                grads[5].astype(jnp.bfloat16), "shard", scatter_dimension=1, tiled=True
            ).astype(jnp.float32),
            lax.psum_scatter(
                grads[6].astype(jnp.bfloat16), "shard", scatter_dimension=0, tiled=True
            ).astype(jnp.float32),
        )
        shares = (
            lax.psum(shares[0].astype(jnp.bfloat16), "rep").astype(jnp.float32),
            lax.psum(shares[1].astype(jnp.bfloat16), "rep").astype(jnp.float32),
            lax.psum(shares[2].astype(jnp.bfloat16), "rep").astype(jnp.float32),
            lax.psum(shares[3].astype(jnp.bfloat16), "rep").astype(jnp.float32),
            lax.psum(shares[4].astype(jnp.bfloat16), "rep").astype(jnp.float32),
            lax.psum(shares[5].astype(jnp.bfloat16), "rep").astype(jnp.float32),
            lax.psum(shares[6].astype(jnp.bfloat16), "rep").astype(jnp.float32),
        )
        layer_shares[layer_id] = shares
    totals = tuple((jnp.stack([layer_shares[0][kind_id]]) for kind_id in range(7)))
    return (
        hidden,
        grad_rows.reshape(inputs.shape),
        totals[0],
        totals[1],
        totals[2],
        totals[3],
        totals[4],
        totals[5],
        totals[6],
    )


def solution(mesh):
    in_specs = (
        P("shard", "rep", None),
        P("shard", "rep"),
        P("shard", "rep", None),
        P(None, "shard", None),
        P(None, "shard", None),
        P(None, "shard", None),
        P(None, "shard", None),
        P(None, None, "shard"),
        P(None, None, "shard"),
        P(None, "shard"),
    )
    out_specs = (
        P("shard", "rep", None),
        P("shard", "rep", None),
        P(None, "shard", None),
        P(None, "shard", None),
        P(None, "shard", None),
        P(None, "shard", None),
        P(None, None, "shard"),
        P(None, None, "shard"),
        P(None, "shard"),
    )
    return jax.shard_map(local, mesh=mesh, in_specs=in_specs, out_specs=out_specs, check_vma=False)
```

profile of v0, /device:TPU:1, one launch (start us, length us, event | category | flops | bytes accessed | tf_op | source)
XLA Modules:
  0.0 1791.1 jit_solution(6566640944744495141)
XLA Ops:
  8.7 86.7 %all-gather.1 = bf16[1,6,1024]{1,0,2:T(2,128)(2,1)S(1)} all-gather(bf16[1,6,32]{1,0,2:T(2,128)(2,1)S(1)} %copy.41), channel_id=3, replica_groups=mesh['rep'=4,'shard'=32] {'shard'}, dimensions={2}, use_global_device_ids=true | all-gather | bytes 12672 | tf_op jit(solution)/shard_map/all_gather | solution.py:215
  95.4 18.0 %fusion.76 = (f32[1024]{0:T(1024)S(1)}, f32[1024]{0:T(1024)S(1)}, f32[1024]{0:T(1024)S(1)}, f32[1024]{0:T(1024)S(1)}, f32[1024]{0:T(1024)S(1)}, /*index=5*/f32[1024]{0:T(1024)S(1)}) fusion(bf16[1,6,1024]{1,0,2:T(2,128)(2,1)S(1)} %all-gather.1), kind=kLoop, calls=%fused_computation.61 | loop fusion | flops 6144 | bytes 36864 | tf_op jit(solution)/shard_map/add | solution.py:99
  113.4 3.8 fusion.11
  120.3 73.0 %all-gather.6 = bf16[1,4096]{1,0:T(2,128)(2,1)S(1)} all-gather(bf16[1,128]{1,0:T(2,128)(2,1)S(1)} %copy-done.16), channel_id=8, replica_groups=mesh['rep'=4,'shard'=32] {'shard'}, dimensions={1}, use_global_device_ids=true | all-gather | bytes 8448 | tf_op jit(solution)/shard_map/all_gather | solution.py:217
  193.3 33.2 %all_gather.32 = s32[1,512]{1,0:T(1,128)S(1)} all-gather(s32[1,128]{1,0:T(1,128)S(1)} %copy-done.14), channel_id=1, replica_groups=mesh['rep'=4,'shard'=32] {'rep'}, dimensions={1}, use_global_device_ids=true | all-gather | bytes 2560 | tf_op jit(solution)/shard_map/all_gather | solution.py:76
  226.6 79.5 %all-gather.4 = bf16[1,2,1024]{1,0,2:T(2,128)(2,1)S(1)} all-gather(bf16[1,2,32]{1,0,2:T(2,128)(2,1)S(1)} %copy.45), channel_id=6, replica_groups=mesh['rep'=4,'shard'=32] {'shard'}, dimensions={2}, use_global_device_ids=true | all-gather | bytes 4224 | tf_op jit(solution)/shard_map/all_gather | solution.py:216
  306.1 6.3 fusion.77
  312.6 1.8 fusion.115
  314.4 1.6 copy.44
  316.6 2.8 fusion.20
  319.5 2.0 copy-done.18
  322.8 2.2 fusion.117
  325.2 12.1 all-gather.20.cloned.1.call-done
  337.3 4.7 fusion.13
  342.1 101.8 %all-gather.22.cloned.1.call-done = bf16[1,4096,1024]{2,1,0:T(8,128)(2,1)} async-done(((bf16[1,128,1024]{2,1,0:T(8,128)(2,1)}), bf16[1,4096,1024]{2,1,0:T(8,128)(2,1)}) %all-gather.22.cloned.1.call-update) | async-done | bytes 8388624 | tf_op jit(solution)/shard_map/all_gather | solution.py:214
  443.8 5.0 fusion.118
  450.4 3.7 fusion.121
  454.2 3.0 multiply_reduce_fusion.1
  459.2 4.1 fusion.126
  463.3 2.1 fusion.42
  465.4 18.3 %fusion.45 = bf16[16,64,512]{2,1,0:T(8,128)(2,1)} fusion(bf16[128,16,64]{0,2,1:T(8,128)(2,1)S(1)} %bitcast.175, f32[16,128,512]{2,1,0:T(8,128)} %fusion.126, f32[16,128,512]{2,1,0:T(8,128)} %copy-done.18, f32[16,128]{1,0:T(8,128)S(1)} %log.8, pred[128,512]{1,0:T(8,128)(4,1)S(1)} %broadcast_compare_fusion), kind=kOutput, calls=%fused_computation.47 | convolution fusion | flops 146278912 | bytes 9773056 | tf_op jit(solution)/shard_map/shqk,sqhe->skhe/dot_general | solution.py:171
  483.8 3.1 pad_maximum_fusion
  486.8 10.9 copy.49
  497.7 4.9 copy.59
  502.8 18.1 %fusion.116 = (bf16[16,64]{1,0:T(8,128)(2,1)S(1)}, bf16[1,128,16,64]{1,3,2,0:T(8,128)(2,1)S(1)}) fusion(bf16[512,16,64]{0,2,1:T(8,128)(2,1)} %bitcast.165, f32[16,128,512]{2,1,0:T(8,128)} %fusion.126, f32[16,128]{1,0:T(8,128)S(1)} %log.8, f32[16,128,512]{2,1,0:T(8,128)} %copy-done.18, pred[128,512]{1,0:T(8,128)(4,1)S(1)} %broadcast_compare_fusion), kind=kOutput, calls=%fused_computation.131 | convolution fusion | flops 146015744 | bytes 9775104 | tf_op jit(solution)/shard_map/shqk,skhe->sqhe/dot_general | solution.py:168
  520.9 8.4 reduce-scatter.22.cloned.1.call-done
  529.3 2.6 reshape_bitcast_fusion
  532.0 3.5 copy.50
  535.5 5.6 convert_bitcast_fusion
  541.1 8.6 copy.51
  549.8 3.0 convolution_convert_fusion.2
  552.9 6.9 convolution_convert_fusion.1
  560.9 4.6 convolution_convert_fusion
  568.8 211.7 %reduce-scatter.24.cloned.1.call-done = bf16[32,3072]{1,0:T(8,128)(2,1)} async-done(((bf16[1024,3072]{1,0:T(8,128)(2,1)}), bf16[32,3072]{1,0:T(8,128)(2,1)}) %reduce-scatter.24.cloned.1.call-update) | async-done | bytes 196624
  780.6 2.1 copy.52
  782.7 162.6 %reduce-scatter.16.cloned.1.call-done = bf16[32,1024]{1,0:T(8,128)(2,1)} async-done(((bf16[1024,1024]{1,0:T(8,128)(2,1)}), bf16[32,1024]{1,0:T(8,128)(2,1)}) %reduce-scatter.16.cloned.1.call-update) | async-done | bytes 65552 | tf_op jit(solution)/shard_map/reduce_scatter | solution.py:231
  945.3 200.4 %reduce-scatter.18.cloned.1.call-done = bf16[32,4096]{1,0:T(8,128)(2,1)} async-done(((bf16[1024,4096]{1,0:T(8,128)(2,1)}), bf16[32,4096]{1,0:T(8,128)(2,1)}) %reduce-scatter.18.cloned.1.call-update) | async-done | bytes 262160 | tf_op jit(solution)/shard_map/reduce_scatter | solution.py:234
  1145.7 200.2 %reduce-scatter.20.cloned.1.call-done = bf16[128,1024]{1,0:T(8,128)(2,1)} async-done(((bf16[4096,1024]{1,0:T(8,128)(2,1)}), bf16[128,1024]{1,0:T(8,128)(2,1)}) %reduce-scatter.20.cloned.1.call-update) | async-done | bytes 262160 | tf_op jit(solution)/shard_map/reduce_scatter | solution.py:237
  1347.2 79.5 %all-reduce = bf16[4096]{0:T(1024)(128)(2,1)S(1)} all-reduce(bf16[4096]{0:T(1024)(128)(2,1)S(1)} %get-tuple-element.86), channel_id=17, replica_groups=mesh['rep'=4,'shard'=32] {'shard'}, use_global_device_ids=true, to_apply=%region_32.33.clone | all-reduce | flops 4096 | bytes 16384
  1426.8 99.6 %reduce-scatter.28.cloned.1.call-done = bf16[32,2]{1,0:T(8,128)(2,1)} async-done(((bf16[1024,2]{1,0:T(8,128)(2,1)}), bf16[32,2]{1,0:T(8,128)(2,1)}) %reduce-scatter.28.cloned.1.call-update) | async-done | bytes 144
  1527.2 5.8 fusion.69
  1533.0 174.2 %reduce-scatter.26.cloned.1.call-done = bf16[32,6]{1,0:T(8,128)(2,1)} async-done(((bf16[1024,6]{1,0:T(8,128)(2,1)}), bf16[32,6]{1,0:T(8,128)(2,1)}) %reduce-scatter.26.cloned.1.call-update) | async-done | bytes 400
  1708.0 31.4 %all-reduce.1 = (bf16[1,6,32]{2,1,0:T(8,128)(2,1)S(1)}, bf16[1,2,32]{2,1,0:T(2,128)(2,1)S(1)}, bf16[1,128]{1,0:T(2,128)(2,1)S(1)}) all-reduce(bf16[1,6,32]{2,1,0:T(8,128)(2,1)S(1)} %bitcast.182, bf16[1,2,32]{2,1,0:T(2,128)(2,1)S(1)} %bitcast.185, ...), channel_id=1, replica_groups=mesh['rep'=4,'shard'=32] {'rep'}, use_global_device_ids=true, to_apply=%region_26.27 | all-reduce | flops 384 | bytes 1536 | tf_op jit(solution)/shard_map/psum | solution.py:255
  1741.0 36.1 %all-reduce.5.cloned.1.call-done = (bf16[1,32,3072]{1,2,0:T(8,128)(2,1)}, bf16[1,32,1024]{2,1,0:T(8,128)(2,1)}, bf16[1,32,4096]{2,1,0:T(8,128)(2,1)}, bf16[1,128,1024]{2,1,0:T(8,128)(2,1)}) async-done(((bf16[1,32,3072]{1,2,0:T(8,128)(2,1)}, bf16[1,32,1024]{2,1,0:T(8,128)(2,1)}, bf16[1,32,4096]{2,1,0:T(8,128)(2,1)}, bf16[1,128,1024]{2,1,0:T(8,128)(2,1)}), (bf16[1,32,3072]{1,2,0:T(8,128)(2,1)}, ...) | async-done | bytes 786448 | tf_op jit(solution)/shard_map/psum | solution.py:251
  1777.2 1.8 stack.87
  1778.9 1.8 stack.89
  1780.7 2.1 copy.47
  1782.9 1.5 stack.85
  (119 shorter events, 19.0 us)
Async XLA Ops:
  7.2 106.2 %copy-start.2 = (f32[1,128,1024]{2,1,0:T(8,128)S(1)}, f32[1,128,1024]{2,1,0:T(8,128)}, u32[]{:S(2)}) copy-start(f32[1,128,1024]{2,1,0:T(8,128)} %param.10) | copy-start | bytes 1572868
  7.2 106.2 %all-gather.14.cloned.1.call-start = ((), (), s32[]{:S(2)}) async-start(), calls=%async_computation.10 | async-start | bytes 6488064 | tf_op jit(solution)/shard_map/all_gather | solution.py:211
  7.9 304.7 %all-gather.16.cloned.1.call-start = ((), (), s32[]{:S(2)}) async-start(), calls=%async_computation.11 | async-start | bytes 2621440 | tf_op jit(solution)/shard_map/all_gather | solution.py:75
  117.2 3.0 copy-start.15
  117.2 3.1 copy-start.16
  117.2 76.1 %copy-start.14 = (s32[1,128]{1,0:T(1,128)S(1)}, s32[1,128]{1,0:T(1,128)}, u32[]{:S(2)}) copy-start(s32[1,128]{1,0:T(1,128)} %param.11) | copy-start | bytes 1540
  118.2 204.5 %all-gather.18.cloned.1.call-start = ((), (), s32[]{:S(2)}) async-start(), calls=%async_computation.12 | async-start | bytes 2162688 | tf_op jit(solution)/shard_map/all_gather | solution.py:212
  119.0 218.3 %all-gather.20.cloned.1.call-start = ((), (), s32[]{:S(2)}) async-start(), calls=%async_computation.13 | async-start | bytes 8650752 | tf_op jit(solution)/shard_map/all_gather | solution.py:213
  119.6 324.2 %all-gather.22.cloned.1.call-start = ((), (), s32[]{:S(2)}) async-start(), calls=%async_computation.14 | async-start | bytes 8650752 | tf_op jit(solution)/shard_map/all_gather | solution.py:214
  120.2 409.2 %reduce-scatter.22.cloned.1.call-start = ((), (), s32[]{:S(2)}) async-start(), calls=%async_computation.15 | async-start | bytes 2621440
  312.6 4.0 copy-start.12
  316.6 6.2 copy-start.8
  319.4 2.0 copy-start.18
  322.7 14.6 copy-start.10
  443.8 5.3 copy-start.4
  443.8 6.6 copy-start
  449.3 4.8 slice-start
  450.4 3.8 copy-start.6
  450.4 3.8 slice-start.1
  454.2 3.1 copy-start.9
  454.2 3.3 copy-start.1
  459.2 4.1 copy-start.11
  459.2 4.1 copy-start.19
  463.3 2.1 copy-start.13
  502.6 278.0 %reduce-scatter.24.cloned.1.call-start = ((), (), s32[]{:S(2)}) async-start(), calls=%async_computation.16 | async-start | bytes 6488064
  549.8 395.5 %reduce-scatter.16.cloned.1.call-start = ((), (), s32[]{:S(2)}) async-start(), calls=%async_computation.7 | async-start | bytes 2162688 | tf_op jit(solution)/shard_map/reduce_scatter | solution.py:231
  552.8 592.9 %reduce-scatter.18.cloned.1.call-start = ((), (), s32[]{:S(2)}) async-start(), calls=%async_computation.8 | async-start | bytes 8650752 | tf_op jit(solution)/shard_map/reduce_scatter | solution.py:234
  559.8 1.1 copy-start.7
  559.8 786.1 %reduce-scatter.20.cloned.1.call-start = ((), (), s32[]{:S(2)}) async-start(), calls=%async_computation.9 | async-start | bytes 8650752 | tf_op jit(solution)/shard_map/reduce_scatter | solution.py:237
  565.4 1.0 copy-start.5
  565.4 2.2 copy-start.3
  565.5 780.5 %copy-start.17 = (u32[128]{0:T(128)S(1)}, u32[128]{0:T(128)}, u32[]{:S(2)}) copy-start(u32[128]{0:T(128)} %constant.32) | copy-start | bytes 1540
  565.5 961.0 %reduce-scatter.28.cloned.1.call-start = ((), (), s32[]{:S(2)}) async-start(), calls=%async_computation.18 | async-start | bytes 270336
  567.6 1139.6 %reduce-scatter.26.cloned.1.call-start = ((), (), s32[]{:S(2)}) async-start(), calls=%async_computation.17 | async-start | bytes 270336
  568.8 1208.4 %all-reduce.5.cloned.1.call-start = ((), (), s32[]{:S(2)}) async-start(), calls=%async_computation.19 | async-start | bytes 2752512 | tf_op jit(solution)/shard_map/psum | solution.py:251
Sparse Core Ops, SparseCore 0:
  11.1 95.8 all-gather.13
  118.4 38.3 all-gather.15
  159.9 71.2 all-gather.17
  234.1 103.1 all-gather.19
  340.3 103.5 all-gather.21
  502.7 26.5 reduce-scatter.21
  549.9 230.6 reduce-scatter.23
  783.1 162.1 reduce-scatter.15
  947.7 197.9 reduce-scatter.17
  1148.0 197.9 reduce-scatter.19
  1348.9 177.5 reduce-scatter.27
  1529.3 177.8 reduce-scatter.25
  1709.9 67.1 all-reduce.4
where the time goes:
time: 1800 us; the launch traced here: 1790 us
  waiting for transfers between devices  1210 us (67%)
  blocking collectives  383 us (21%)
  matrix products  96 us (5%)
  local copies, waits for them, and re-layouts  49.2 us (3%)
  other arithmetic  36.7 us (2%)
    unnamed x17, waiting for transfers between devices  496 us
    reduce_scatter x1, waiting for transfers between devices, local(): lax.psum_scatter(grads[2].astype(jnp.bfloat16), 'shard', scatter_dimensio...  200 us
    reduce_scatter x1, waiting for transfers between devices, local(): lax.psum_scatter(grads[3].astype(jnp.bfloat16), 'shard', scatter_dimensio...  200 us
    reduce_scatter x1, waiting for transfers between devices, local(): lax.psum_scatter(grads[1].astype(jnp.bfloat16), 'shard', scatter_dimensio...  163 us
    all_gather x1, waiting for transfers between devices, local(): lax.all_gather(w_down[layer_id], 'shard', axis=0, tiled=True)  102 us
    all_gather x1, blocking collectives, local(): lax.all_gather(biases[layer_id], 'shard', axis=1, tiled=True)  86.7 us
    unnamed x1, blocking collectives  79.5 us
    all_gather x1, blocking collectives, local(): lax.all_gather(norm_gains[layer_id], 'shard', axis=1, tiled=True)  79.5 us
  transfers between devices with their start and end apart: 13, of which 10 were waited for; matrix products, arithmetic and copies ran while one was open for 5% of the time, Pallas kernels for 0%

commit v1 on v0

--- a/solution.py
+++ b/solution.py
@@ -204,71 +204,72 @@
     return (d_hidden, (d_wqkv, d_wout, d_wup, d_wdown, d_biases, d_gains, d_bup))
 
 
+def pack_rows(tensor, parts):
+    return tensor.reshape(parts, -1)
+
+
+def pack_cols(tensor, parts):
+    rows = tensor.shape[0]
+    return tensor.reshape(rows, parts, -1).transpose(1, 0, 2).reshape(parts, -1)
+
+
+def unpack_cols(flat, parts, rows):
+    return flat.reshape(parts, rows, -1).transpose(1, 0, 2).reshape(rows, -1)
+
+
 def local(inputs, segment_ids, cotangent, w_qkv, w_out, w_up, w_down, biases, norm_gains, up_bias):
     hidden = inputs
     layer_id = 0
+    parts = lax.axis_size("shard")
+    local_params = (
+        w_qkv[layer_id],
+        w_out[layer_id],
+        w_up[layer_id],
+        w_down[layer_id],
+        biases[layer_id],
+        norm_gains[layer_id],
+        up_bias[layer_id],
+    )
+    sizes = [tensor.size for tensor in local_params]
+    offsets = [sum(sizes[:i]) for i in range(len(sizes) + 1)]
+    packed = jnp.concatenate([tensor.reshape(-1) for tensor in local_params])
+    gathered = lax.all_gather(packed, "shard", axis=0, tiled=False)
+    pieces = [gathered[:, offsets[i] : offsets[i + 1]] for i in range(len(sizes))]
     weights = (
-        lax.all_gather(w_qkv[layer_id], "shard", axis=0, tiled=True),
-        lax.all_gather(w_out[layer_id], "shard", axis=0, tiled=True),
-        lax.all_gather(w_up[layer_id], "shard", axis=0, tiled=True),
-        lax.all_gather(w_down[layer_id], "shard", axis=0, tiled=True),
-        lax.all_gather(biases[layer_id], "shard", axis=1, tiled=True),
-        lax.all_gather(norm_gains[layer_id], "shard", axis=1, tiled=True),
-        lax.all_gather(up_bias[layer_id], "shard", axis=0, tiled=True),
-    )
-    kept_weights = [weights]
+        pieces[0].reshape(-1, local_params[0].shape[1]),
+        pieces[1].reshape(-1, local_params[1].shape[1]),
+        pieces[2].reshape(-1, local_params[2].shape[1]),
+        pieces[3].reshape(-1, local_params[3].shape[1]),
+        unpack_cols(pieces[4], parts, local_params[4].shape[0]),
+        unpack_cols(pieces[5], parts, local_params[5].shape[0]),
+        pieces[6].reshape(-1),
+    )
     hidden, saved = forward_layer(hidden, segment_ids, weights)
-    saved_list = [saved]
     grad_rows = cotangent.reshape(-1, cotangent.shape[-1])
-    layer_shares = [None] * LAYERS
-    for layer_id in reversed(range(LAYERS)):
-        weights = kept_weights[layer_id]
-        grad_rows, grads = backward_layer(grad_rows, segment_ids, weights, saved_list[layer_id])
-        shares = (
-            lax.psum_scatter(
-                grads[0].astype(jnp.bfloat16), "shard", scatter_dimension=0, tiled=True
-            ).astype(jnp.float32),
-            lax.psum_scatter(
-                grads[1].astype(jnp.bfloat16), "shard", scatter_dimension=0, tiled=True
-            ).astype(jnp.float32),
-            lax.psum_scatter(
-                grads[2].astype(jnp.bfloat16), "shard", scatter_dimension=0, tiled=True
-            ).astype(jnp.float32),
-            lax.psum_scatter(
-                grads[3].astype(jnp.bfloat16), "shard", scatter_dimension=0, tiled=True
-            ).astype(jnp.float32),
-            lax.psum_scatter(
-                grads[4].astype(jnp.bfloat16), "shard", scatter_dimension=1, tiled=True
-            ).astype(jnp.float32),
-            lax.psum_scatter(
-                grads[5].astype(jnp.bfloat16), "shard", scatter_dimension=1, tiled=True
-            ).astype(jnp.float32),
-            lax.psum_scatter(
-                grads[6].astype(jnp.bfloat16), "shard", scatter_dimension=0, tiled=True
-            ).astype(jnp.float32),
-        )
-        shares = (
-            lax.psum(shares[0].astype(jnp.bfloat16), "rep").astype(jnp.float32),
-            lax.psum(shares[1].astype(jnp.bfloat16), "rep").astype(jnp.float32),
-            lax.psum(shares[2].astype(jnp.bfloat16), "rep").astype(jnp.float32),
-            lax.psum(shares[3].astype(jnp.bfloat16), "rep").astype(jnp.float32),
-            lax.psum(shares[4].astype(jnp.bfloat16), "rep").astype(jnp.float32),
-            lax.psum(shares[5].astype(jnp.bfloat16), "rep").astype(jnp.float32),
-            lax.psum(shares[6].astype(jnp.bfloat16), "rep").astype(jnp.float32),
-        )
-        layer_shares[layer_id] = shares
-    totals = tuple((jnp.stack([layer_shares[0][kind_id]]) for kind_id in range(7)))
-    return (
-        hidden,
-        grad_rows.reshape(inputs.shape),
-        totals[0],
-        totals[1],
-        totals[2],
-        totals[3],
-        totals[4],
-        totals[5],
-        totals[6],
-    )
+    grad_rows, grads = backward_layer(grad_rows, segment_ids, weights, saved)
+    grads_b = [grad.astype(jnp.bfloat16) for grad in grads]
+    grad_pack = jnp.concatenate(
+        [
+            pack_rows(grads_b[0], parts),
+            pack_rows(grads_b[1], parts),
+            pack_rows(grads_b[2], parts),
+            pack_rows(grads_b[3], parts),
+            pack_cols(grads_b[4], parts),
+            pack_cols(grads_b[5], parts),
+            pack_rows(grads_b[6], parts),
+        ],
+        axis=1,
+    )
+    width = grad_pack.shape[1]
+    padded = -(-width // 1024) * 1024
+    grad_pack = jnp.pad(grad_pack, ((0, 0), (0, padded - width))).reshape(parts * 8, -1)
+    shares = lax.psum_scatter(grad_pack, "shard", scatter_dimension=0, tiled=True)
+    shares = lax.psum(shares, "rep").astype(jnp.float32).reshape(-1)
+    totals = [
+        shares[offsets[i] : offsets[i + 1]].reshape((1,) + local_params[i].shape)
+        for i in range(len(sizes))
+    ]
+    return (hidden, grad_rows.reshape(inputs.shape), *totals)
 
 
 def solution(mesh):

time: 1800 us -> 1340 us (0.74)
  blocking collectives: 383 us -> 6.26 us
  waiting for transfers between devices: 1210 us -> 952 us
  local copies, waits for them, and re-layouts: 49.2 us -> 261 us
  other arithmetic: 36.7 us -> 8.66 us
    reduce_scatter x3 -> x0, waiting for transfers between devices: 563 us -> none  [the longest x1 200 us: local(): lax.psum_scatter(grads[2].astype(jnp.bfloat16), 'shard', scatter_dimensio...]
    all_gather x4 -> x1, waiting for transfers between devices: 114 us -> 366 us  [local(): gathered = lax.all_gather(packed, 'shard', axis=0, tiled=False)]
    all_gather x3 -> x0, blocking collectives: 239 us -> none  [the longest x1 86.7 us: local(): lax.all_gather(biases[layer_id], 'shard', axis=1, tiled=True)]
    reshape x0 -> x20, local copies, waits for them, and re-layouts: none -> 98.6 us  [the longest x1 33.4 us: local(): jnp.pad(grad_pack, ((0, 0), (0, padded - width))).reshape(parts * 8, -1)]
    unnamed x1 -> x0, blocking collectives: 79.5 us -> none
    unnamed x17 -> x7, waiting for transfers between devices: 496 us -> 554 us
    unnamed x59 -> x73, local copies, waits for them, and re-layouts: 43.9 us -> 93.9 us
    psum x1 -> x0, blocking collectives: 31.4 us -> none  [local(): lax.psum(shares[4].astype(jnp.bfloat16), 'rep').astype(jnp.float32)]
  transfers between devices with their start and end apart: 13 -> 5, of which waited for: 10 -> 3; matrix products, arithmetic and copies ran while one was open for 5% -> 8% of each run, Pallas kernels for 0% -> 0%
where the time goes in v1:
time: 1340 us; the launch traced here: 1330 us
  waiting for transfers between devices  952 us (71%)
  local copies, waits for them, and re-layouts  261 us (19%)
  matrix products  85.8 us (6%)
  between operations  15.1 us (1%)
    unnamed x7, waiting for transfers between devices  554 us
    all_gather x1, waiting for transfers between devices, local(): gathered = lax.all_gather(packed, 'shard', axis=0, tiled=False)  366 us
    unnamed x73, local copies, waits for them, and re-layouts  93.9 us
    reshape x1, local copies, waits for them, and re-layouts, local(): jnp.pad(grad_pack, ((0, 0), (0, padded - width))).reshape(parts * 8, -1)  33.4 us
    psum x1, waiting for transfers between devices, local(): shares = lax.psum(shares, 'rep').astype(jnp.float32).reshape(-1)  32.5 us
    reshape x4, local copies, waits for them, and re-layouts, pack_rows(): return tensor.reshape(parts, -1)  29.4 us
  transfers between devices with their start and end apart: 5, of which 3 were waited for; matrix products, arithmetic and copies ran while one was open for 8% of the time, Pallas kernels for 0%

profile of v1, /device:TPU:1, one launch (start us, length us, event | category | flops | bytes accessed | tf_op | source)
XLA Modules:
  0.0 1329.6 jit_solution(7786354182064792578)
XLA Ops:
  13.8 9.7 reshape.459
  23.6 6.3 all_gather.17
  30.0 365.7 %all-gather.8.cloned.1.call-done = bf16[32,1,393600]{2,1,0:T(2,128)(2,1)} async-done(((bf16[1,1,393600]{2,1,0:T(2,128)(2,1)}), bf16[32,1,393600]{2,1,0:T(2,128)(2,1)}) %all-gather.8.cloned.1.call-update) | async-done | bytes 25190416 | tf_op jit(solution)/shard_map/all_gather | solution.py:236
  395.7 29.9 %copy.42 = bf16[32,1,393600]{2,0,1:T(8,128)(2,1)} copy(bf16[32,1,393600]{2,1,0:T(2,128)(2,1)} %all-gather.8.cloned.1.call-done) | data formatting | bytes 50380800
  427.1 5.9 slice.131
  433.7 7.3 reshape.417
  441.0 4.6 convolution_bitcast_fusion
  447.2 11.5 fusion.74
  458.7 3.1 slice.140
  461.9 2.9 reshape.424
  464.9 9.5 reshape.426
  474.5 8.9 reshape.427
  484.2 1.7 fusion.75
  492.2 1.3 convolution_add_fusion
  494.6 1.5 fusion.79
  497.7 3.5 fusion.82
  501.2 3.0 multiply_reduce_fusion.1
  506.2 4.1 fusion.85
  510.3 2.1 fusion.20
  512.5 18.5 %fusion.23 = bf16[16,64,512]{2,1,0:T(8,128)(2,1)} fusion(bf16[128,16,64]{0,2,1:T(8,128)(2,1)S(1)} %bitcast.154, f32[16,128,512]{2,1,0:T(8,128)} %fusion.85, f32[16,128,512]{2,1,0:T(8,128)} %copy-done.19, f32[16,128]{1,0:T(8,128)S(1)} %log.8, pred[128,512]{1,0:T(8,128)(4,1)S(1)} %broadcast_compare_fusion), kind=kOutput, calls=%fused_computation.33 | convolution fusion | flops 146278912 | bytes 9773056 | tf_op jit(solution)/shard_map/shqk,sqhe->skhe/dot_general | solution.py:171
  530.9 3.1 pad_maximum_fusion
  534.0 10.9 copy.32
  544.9 4.9 copy.43
  551.4 18.5 %fusion.77 = (bf16[16,64]{1,0:T(8,128)(2,1)S(1)}, bf16[1,128,16,64]{1,3,2,0:T(8,128)(2,1)S(1)}) fusion(bf16[512,16,64]{0,2,1:T(8,128)(2,1)} %bitcast.141, f32[16,128,512]{2,1,0:T(8,128)} %fusion.85, f32[16,128]{1,0:T(8,128)S(1)} %log.8, f32[16,128,512]{2,1,0:T(8,128)} %copy-done.19, pred[128,512]{1,0:T(8,128)(4,1)S(1)} %broadcast_compare_fusion), kind=kOutput, calls=%fused_computation.135 | convolution fusion | flops 146015744 | bytes 9775104 | tf_op jit(solution)/shard_map/shqk,skhe->sqhe/dot_general | solution.py:168
  570.2 6.9 convolution_convert_fusion.1
  577.1 9.1 reshape.436
  586.2 3.0 convolution_convert_fusion.2
  589.2 4.2 reshape.435
  593.5 4.6 convolution_convert_fusion
  598.0 8.9 reshape.437
  607.2 1.7 reshape_bitcast_fusion
  610.2 4.4 convert_bitcast_fusion
  614.6 8.7 copy.29
  623.3 7.3 reshape.434
  630.6 6.0 constant_dynamic-update-slice_fusion.10
  636.5 1.5 constant_dynamic-update-slice_fusion.9
  638.0 7.2 constant_dynamic-update-slice_fusion.8
  645.2 7.2 constant_dynamic-update-slice_fusion.7
  652.4 1.4 dynamic-update-slice.4
  653.8 1.5 dynamic-update-slice.5
  655.9 20.6 %pad.4 = bf16[32,394240]{1,0:T(8,128)(2,1)} pad(bf16[32,393600]{1,0:T(8,128)(2,1)} %constant_dynamic-update-slice_fusion.6, bf16[]{:T(256)} %constant.28.clone.1), padding=0_0x0_640 | pad | bytes 50421760 | tf_op jit(solution)/shard_map/jit(_pad)/pad | solution.py:265
  676.5 33.4 %reshape.440 = bf16[256,49280]{1,0:T(8,128)(2,1)} reshape(bf16[32,394240]{1,0:T(8,128)(2,1)} %pad.4) | data formatting | bytes 50462720 | tf_op jit(solution)/shard_map/reshape | solution.py:265
  711.7 554.1 %all-reduce.7.cloned.1.call-done = bf16[256,49280]{1,0:T(8,128)(2,1)} async-done(((bf16[256,49280]{1,0:T(8,128)(2,1)}), bf16[256,49280]{1,0:T(8,128)(2,1)}) %all-reduce.7.cloned.1.call-update) | async-done | bytes 25231376
  1265.8 2.1 constant_dynamic-slice_fusion
  1267.9 5.8 fusion.31
  1273.8 32.5 %all-reduce.5.cloned.1.call-done = bf16[8,49280]{1,0:T(8,128)(2,1)} async-done(((bf16[8,49280]{1,0:T(8,128)(2,1)}), bf16[8,49280]{1,0:T(8,128)(2,1)}) %all-reduce.5.cloned.1.call-update) | async-done | bytes 788496 | tf_op jit(solution)/shard_map/psum | solution.py:267
  1306.2 2.4 reshape.441
  1310.0 7.8 slice.128
  (143 shorter events, 34.2 us)
Async XLA Ops:
  7.2 16.5 %copy-start.17 = (s32[1,128]{1,0:T(1,128)S(1)}, s32[1,128]{1,0:T(1,128)}, u32[]{:S(2)}) copy-start(s32[1,128]{1,0:T(1,128)} %param.11) | copy-start | bytes 1540
  7.2 388.5 %all-gather.8.cloned.1.call-start = ((), (), s32[]{:S(2)}) async-start(), calls=%async_computation.3 | async-start | bytes 51955200 | tf_op jit(solution)/shard_map/all_gather | solution.py:236
  23.6 460.7 %all-gather.6.cloned.1.call-start = ((), (), s32[]{:S(2)}) async-start(), calls=%async_computation.2 | async-start | bytes 2621440 | tf_op jit(solution)/shard_map/all_gather | solution.py:75
  433.7 7.3 copy-start.3
  446.1 39.9 %copy-start.15 = (bf16[128,1024]{0,1:T(8,128)(2,1)}, bf16[128,1024]{0,1:T(8,128)(2,1)S(1)}, u32[]{:S(2)}) copy-start(bf16[128,1024]{0,1:T(8,128)(2,1)S(1)} %get-tuple-element.34) | copy-start | bytes 786436
  447.0 160.2 %reduce-scatter.4.cloned.1.call-start = ((), (), s32[]{:S(2)}) async-start(), calls=%async_computation.4 | async-start | bytes 2621440
  464.8 25.5 %copy-start = (bf16[1024,1024]{1,0:T(8,128)(2,1)}, bf16[1024,1024]{1,0:T(8,128)(2,1)S(1)}, u32[]{:S(2)}) copy-start(bf16[1024,1024]{1,0:T(8,128)(2,1)S(1)} %reshape.424) | copy-start | bytes 6291460
  485.9 1.0 copy-start.12
  485.9 3.4 copy-start.8
  486.9 4.2 slice-start
  488.1 2.1 copy-start.19
  488.1 4.1 slice-start.1
  490.2 0.7 copy-start.13
  490.9 2.6 slice-start.2
  492.2 2.4 slice-start.3
  494.6 1.7 copy-start.5
  497.7 3.5 copy-start.6
  501.2 3.1 copy-start.9
  501.2 3.3 copy-start.1
  506.2 4.1 copy-start.14
  506.2 4.1 copy-start.20
  510.3 2.1 copy-start.16
  549.8 716.0 %all-reduce.7.cloned.1.call-start = ((), (), s32[]{:S(2)}) async-start(), calls=%async_computation.5 | async-start | bytes 50462720
  586.2 7.3 copy-start.7
  606.9 3.3 copy-start.4
  630.6 6.0 copy-start.2
  709.8 0.7 copy-start.18
  709.8 596.4 %all-reduce.5.cloned.1.call-start = ((), (), s32[]{:S(2)}) async-start(), calls=%async_computation.1 | async-start | bytes 1576960 | tf_op jit(solution)/shard_map/psum | solution.py:267
  1306.2 3.7 copy-start.10
  1310.0 10.8 copy-start.11
Sparse Core Ops, SparseCore 0:
  23.7 371.9 all-gather.7
  447.1 27.5 all-gather.5
  549.9 26.5 reduce-scatter.3
  710.0 555.7 all-reduce.6
  1268.3 37.8 all-reduce.4

commit v2 on v1

v2 whole, which is shorter than its diff:
```python
import math

import jax
import jax.numpy as jnp
from jax import lax
from jax.sharding import PartitionSpec as P

D = 1024
HEADS = 16
HEAD_DIM = 64
LAYERS = 1


epsilon = 1e-06


def normalize(residual):
    center = residual - jnp.mean(residual, axis=-1, keepdims=True)
    rstd_val = lax.rsqrt(jnp.mean(center * center, axis=-1, keepdims=True) + epsilon)
    return (center * rstd_val, rstd_val)


def norm_back(grad_out, x_hat, rstd_val, gain_row):
    d_hat = grad_out * gain_row
    return rstd_val * (
        d_hat
        - jnp.mean(d_hat, axis=-1, keepdims=True)
        - x_hat * jnp.mean(d_hat * x_hat, axis=-1, keepdims=True)
    )


def gelu_pair(pre_act):
    normal_cdf = 0.5 * (1.0 + lax.erf(pre_act * (1.0 / math.sqrt(2.0))))
    density = jnp.exp(-0.5 * pre_act * pre_act) * (1.0 / math.sqrt(2.0 * math.pi))
    return (pre_act * normal_cdf, normal_cdf + pre_act * density)


def matmul(first_op, second_op):
    return jnp.dot(first_op, second_op, preferred_element_type=jnp.float32)


def matmul_lt(first_op, second_op):
    return lax.dot_general(
        first_op, second_op, (((0,), (0,)), ((), ())), preferred_element_type=jnp.float32
    )


def matmul_rt(first_op, second_op):
    return lax.dot_general(
        first_op, second_op, (((1,), (1,)), ((), ())), preferred_element_type=jnp.float32
    )


def attention_scores(queries, keys_all, seg_rows, seg_cols):
    scores = jnp.einsum(
        "sqhe,skhe->shqk", queries, keys_all, preferred_element_type=jnp.float32
    ) * (1.0 / math.sqrt(HEAD_DIM))
    allowed = seg_rows[:, None, :, None] == seg_cols[:, None, None, :]
    return (scores, allowed)


def pick(tensor, index, axis):
    return lax.dynamic_index_in_dim(tensor, index, axis=axis, keepdims=False)


def pack_cols(tensor, parts):
    rows = tensor.shape[0]
    return tensor.reshape(rows, parts, -1).transpose(1, 0, 2).reshape(parts, -1)


def unpack_cols(flat, parts, rows):
    return flat.reshape(parts, rows, -1).transpose(1, 0, 2).reshape(rows, -1)


def gather_rep(tensor):
    return lax.all_gather(tensor, "rep", axis=0, tiled=True)


def scatter_rep(tensor):
    return lax.psum_scatter(tensor, "rep", scatter_dimension=0, tiled=True)


def local(inputs, segment_ids, cotangent, w_qkv, w_out, w_up, w_down, biases, norm_gains, up_bias):
    parts = lax.axis_size("shard")
    reps = lax.axis_size("rep")
    r = lax.axis_index("rep")
    head_cols = D // reps
    heads_here = HEADS // reps
    ff_all = w_up.shape[2]
    ff_chunk = ff_all // parts
    ff_piece = ff_chunk // reps
    k_rows = D // parts

    qkv_piece = pick(w_qkv[0].reshape(k_rows, 3, reps, head_cols), r, 2).reshape(k_rows, -1)
    out_piece = w_out[0]
    up_piece = pick(w_up[0].reshape(k_rows, parts, reps, ff_piece), r, 2).reshape(k_rows, -1)
    down_piece = pick(w_down[0].reshape(reps, ff_piece, D), r, 0)
    upb_piece = pick(up_bias[0].reshape(reps, ff_piece), r, 0)
    pieces = (qkv_piece, out_piece, up_piece, down_piece, upb_piece, biases[0], norm_gains[0])
    sizes = [piece.size for piece in pieces]
    offsets = [sum(sizes[:i]) for i in range(len(sizes) + 1)]
    packed = jnp.concatenate([piece.reshape(-1) for piece in pieces])
    packed = jnp.pad(packed, (0, -(-packed.size // 1024) * 1024 - packed.size))
    gathered = lax.all_gather(packed, "shard", axis=0, tiled=False)
    got = [gathered[:, offsets[i] : offsets[i + 1]] for i in range(len(sizes))]
    w_qkv_r = got[0].reshape(D, 3 * head_cols)
    w_out_all = got[1].reshape(D, D)
    w_out_r = lax.dynamic_slice_in_dim(w_out_all, r * head_cols, head_cols, axis=0)
    w_up_r = got[2].reshape(D, -1)
    w_down_r = got[3].reshape(-1, D)
    up_bias_r = got[4].reshape(-1)
    bias_all = unpack_cols(got[5], parts, biases.shape[1])
    gain_all = unpack_cols(got[6], parts, norm_gains.shape[1])
    bias_q = lax.dynamic_slice_in_dim(bias_all[0], r * head_cols, head_cols)
    bias_v = lax.dynamic_slice_in_dim(bias_all[1], r * head_cols, head_cols)

    rows_f32 = inputs[0]
    own = rows_f32.shape[0]
    rows_bf = rows_f32.astype(jnp.bfloat16)
    seg_tag = jnp.broadcast_to(segment_ids[0].astype(jnp.bfloat16)[:, None], (own, 128))
    hb_seg = gather_rep(jnp.concatenate([rows_bf, seg_tag], axis=1))
    hb_all = hb_seg[:, :D]
    seg_all = hb_seg[:, D]
    qkv_rows = matmul(hb_all, w_qkv_r)
    queries = (qkv_rows[:, :head_cols] + bias_q).astype(jnp.bfloat16).reshape(1, -1, heads_here, HEAD_DIM)
    keys_all = qkv_rows[:, head_cols : 2 * head_cols].astype(jnp.bfloat16).reshape(1, -1, heads_here, HEAD_DIM)
    values_all = (
        (qkv_rows[:, 2 * head_cols :] + bias_v).astype(jnp.bfloat16).reshape(1, -1, heads_here, HEAD_DIM)
    )
    seg_rows = seg_all[None]
    scores, allowed = attention_scores(queries, keys_all, seg_rows, seg_rows)
    expo_all = jnp.where(allowed, jnp.exp(scores), 0.0)
    row_total = jnp.sum(expo_all, axis=-1, keepdims=True)
    log_total = jnp.log(row_total)
    attn_probs = (expo_all / row_total).astype(jnp.bfloat16)
    context = (
        jnp.einsum("shqk,skhe->sqhe", attn_probs, values_all, preferred_element_type=jnp.float32)
        .astype(jnp.bfloat16)
        .reshape(-1, head_cols)
    )
    first_sum = rows_f32 + scatter_rep(matmul(context, w_out_r)) + bias_all[2]
    norm_one, rstd_one = normalize(first_sum)
    mid_norm = norm_one * gain_all[0] + bias_all[3]
    mid_b = mid_norm.astype(jnp.bfloat16)
    mid_all = gather_rep(mid_b)
    pre_act = matmul(mid_all, w_up_r) + up_bias_r
    act_f32, gelu_slope = gelu_pair(pre_act)
    act_b = act_f32.astype(jnp.bfloat16)
    second_sum = mid_norm + scatter_rep(matmul(act_b, w_down_r)) + bias_all[4]
    norm_two, rstd_two = normalize(second_sum)
    layer_out = norm_two * gain_all[1] + bias_all[5]

    grad_rows = cotangent[0]
    d_gain_two = jnp.sum(grad_rows * norm_two, axis=0)
    d_bias_two = jnp.sum(grad_rows, axis=0)
    d_second = norm_back(grad_rows, norm_two, rstd_two, gain_all[1])
    d_bdown = jnp.sum(d_second, axis=0)
    d_second_all = gather_rep(d_second.astype(jnp.bfloat16))
    d_wdown = matmul_lt(act_b, d_second_all)
    d_pre = matmul_rt(d_second_all, w_down_r) * gelu_slope
    d_bup = jnp.sum(d_pre, axis=0)
    d_pre_b = d_pre.astype(jnp.bfloat16)
    d_wup = matmul_lt(mid_all, d_pre_b)
    d_mid = d_second + scatter_rep(matmul_rt(d_pre_b, w_up_r))
    d_gain_one = jnp.sum(d_mid * norm_one, axis=0)
    d_bias_one = jnp.sum(d_mid, axis=0)
    d_first = norm_back(d_mid, norm_one, rstd_one, gain_all[0])
    d_bout = jnp.sum(d_first, axis=0)
    d_first_all = gather_rep(d_first.astype(jnp.bfloat16))
    d_wout = matmul_lt(context, d_first_all)
    d_context = (
        matmul_rt(d_first_all, w_out_r).astype(jnp.bfloat16).reshape(1, -1, heads_here, HEAD_DIM)
    )
    probs_again = jnp.where(allowed, jnp.exp(scores - log_total), 0.0)
    d_probs = jnp.einsum(
        "sqhe,skhe->shqk", d_context, values_all, preferred_element_type=jnp.float32
    )
    d_scores = (
        probs_again
        * (d_probs - jnp.sum(probs_again * d_probs, axis=-1, keepdims=True))
        * (1.0 / math.sqrt(HEAD_DIM))
    ).astype(jnp.bfloat16)
    d_queries = jnp.einsum(
        "shqk,skhe->sqhe", d_scores, keys_all, preferred_element_type=jnp.float32
    ).reshape(-1, head_cols)
    d_keys = jnp.einsum(
        "shqk,sqhe->skhe", d_scores, queries, preferred_element_type=jnp.float32
    ).reshape(-1, head_cols)
    d_values = jnp.einsum(
        "shqk,sqhe->skhe",
        probs_again.astype(jnp.bfloat16),
        d_context,
        preferred_element_type=jnp.float32,
    ).reshape(-1, head_cols)
    d_qkv = jnp.concatenate([d_queries, d_keys, d_values], axis=-1).astype(jnp.bfloat16)
    d_wqkv = matmul_lt(hb_all, d_qkv)
    input_grad = d_first + scatter_rep(matmul_rt(d_qkv, w_qkv_r))

    zeros_cols = jnp.zeros((D,), jnp.float32)
    d_bq = lax.dynamic_update_slice_in_dim(zeros_cols, jnp.sum(d_queries, axis=0), r * head_cols, 0)
    d_bv = lax.dynamic_update_slice_in_dim(zeros_cols, jnp.sum(d_values, axis=0), r * head_cols, 0)
    d_biases = jnp.stack([d_bq, d_bv, d_bout, d_bias_one, d_bdown, d_bias_two])
    d_gains = jnp.stack([d_gain_one, d_gain_two])
    d_wout_all = lax.dynamic_update_slice_in_dim(
        jnp.zeros((D, D), jnp.bfloat16), d_wout.astype(jnp.bfloat16), r * head_cols, 0
    )
    d_bup_all = lax.dynamic_update_slice_in_dim(
        jnp.zeros((parts, reps, ff_piece), jnp.float32), d_bup.reshape(parts, 1, ff_piece), r, 1
    )
    grad_parts = (
        d_wqkv.astype(jnp.bfloat16).reshape(parts, -1),
        d_wout_all.reshape(parts, -1),
        d_wup.astype(jnp.bfloat16).reshape(parts, -1),
        d_wdown.astype(jnp.bfloat16).reshape(parts, -1),
        d_bup_all.astype(jnp.bfloat16).reshape(parts, -1),
        pack_cols(d_biases.astype(jnp.bfloat16), parts),
        pack_cols(d_gains.astype(jnp.bfloat16), parts),
    )
    g_sizes = [piece.shape[1] for piece in grad_parts]
    g_offsets = [sum(g_sizes[:i]) for i in range(len(g_sizes) + 1)]
    grad_pack = jnp.concatenate(grad_parts, axis=1)
    width = grad_pack.shape[1]
    padded = -(-width // 4096) * 4096
    grad_pack = jnp.pad(grad_pack, ((0, 0), (0, padded - width))).reshape(parts * 32, -1)
    shares = lax.psum_scatter(grad_pack, "shard", scatter_dimension=0, tiled=True)
    joined = lax.all_gather(shares.reshape(-1), "rep", axis=0, tiled=False).astype(jnp.float32)
    got = [joined[:, g_offsets[i] : g_offsets[i + 1]] for i in range(len(g_sizes))]
    grad_w_qkv = got[0].reshape(reps, k_rows, 3, head_cols).transpose(1, 2, 0, 3).reshape(k_rows, -1)
    grad_w_out = jnp.sum(got[1], axis=0).reshape(k_rows, D)
    grad_w_up = got[2].reshape(reps, k_rows, parts, ff_piece).transpose(1, 2, 0, 3).reshape(k_rows, -1)
    grad_w_down = got[3].reshape(reps * ff_piece, D)
    grad_up_bias = jnp.sum(got[4], axis=0)
    grad_biases = jnp.sum(got[5], axis=0).reshape(biases.shape[1], -1)
    grad_gains = jnp.sum(got[6], axis=0).reshape(norm_gains.shape[1], -1)
    return (
        layer_out[None],
        input_grad[None],
        grad_w_qkv[None],
        grad_w_out[None],
        grad_w_up[None],
        grad_w_down[None],
        grad_biases[None],
        grad_gains[None],
        grad_up_bias[None],
    )


def solution(mesh):
    in_specs = (
        P("shard", "rep", None),
        P("shard", "rep"),
        P("shard", "rep", None),
        P(None, "shard", None),
        P(None, "shard", None),
        P(None, "shard", None),
        P(None, "shard", None),
        P(None, None, "shard"),
        P(None, None, "shard"),
        P(None, "shard"),
    )
    out_specs = (
        P("shard", "rep", None),
        P("shard", "rep", None),
        P(None, "shard", None),
        P(None, "shard", None),
        P(None, "shard", None),
        P(None, "shard", None),
        P(None, None, "shard"),
        P(None, None, "shard"),
        P(None, "shard"),
    )
    return jax.shard_map(local, mesh=mesh, in_specs=in_specs, out_specs=out_specs, check_vma=False)
```

time: 1340 us -> 671 us (0.50)
  waiting for transfers between devices: 952 us -> 429 us
  local copies, waits for them, and re-layouts: 261 us -> 98.6 us
  blocking collectives: 6.26 us -> 39.2 us
  matrix products: 85.8 us -> 62.9 us
    unnamed x7 -> x10, waiting for transfers between devices: 554 us -> 0.16 us
    all_gather x1, waiting for transfers between devices: 366 us -> 104 us  [local(): gathered = lax.all_gather(packed, 'shard', axis=0, tiled=False)]
    reduce_scatter x0 -> x5, waiting for transfers between devices: none -> 261 us  [the longest x1 177 us: local(): lax.psum_scatter(grad_pack, 'shard', scatter_dimension=0, tiled=True)]
    unnamed x73 -> x69, local copies, waits for them, and re-layouts: 93.9 us -> 19.2 us
    reshape x16 -> x13, local copies, waits for them, and re-layouts: 98.2 us -> 32 us  [the longest x1 8.67 us: local(): jnp.pad(grad_pack, ((0, 0), (0, padded - width))).reshape(parts * 32, -1)]
    all_gather x1 -> x4, waiting for transfers between devices: 0.01 us -> 63.3 us  [gather_rep(): return lax.all_gather(tensor, 'rep', axis=0, tiled=True)]
    all_gather x1, blocking collectives: 6.26 us -> 39.2 us  [local(): lax.all_gather(shares.reshape(-1), 'rep', axis=0, tiled=False)]
    psum x1 -> x0, waiting for transfers between devices: 32.5 us -> none  [local(): shares = lax.psum(shares, 'rep').astype(jnp.float32).reshape(-1)]
  transfers between devices with their start and end apart: 5 -> 10, of which waited for: 3 -> 9; matrix products, arithmetic and copies ran while one was open for 8% -> 11% of each run, Pallas kernels for 0% -> 0%
where the time goes in v2:
time: 671 us; the launch traced here: 662 us
  waiting for transfers between devices  429 us (64%)
  local copies, waits for them, and re-layouts  98.6 us (15%)
  matrix products  62.9 us (9%)
  blocking collectives  39.2 us (6%)
  other arithmetic  16.3 us (2%)
  between operations  15.1 us (2%)
    reduce_scatter x1, waiting for transfers between devices, local(): lax.psum_scatter(grad_pack, 'shard', scatter_dimension=0, tiled=True)  177 us
    all_gather x1, waiting for transfers between devices, local(): gathered = lax.all_gather(packed, 'shard', axis=0, tiled=False)  104 us
    reduce_scatter x4, waiting for transfers between devices, scatter_rep(): return lax.psum_scatter(tensor, 'rep', scatter_dimension=0, tiled=True)  83.6 us
    all_gather x4, waiting for transfers between devices, gather_rep(): return lax.all_gather(tensor, 'rep', axis=0, tiled=True)  63.3 us
    all_gather x1, blocking collectives, local(): lax.all_gather(shares.reshape(-1), 'rep', axis=0, tiled=False)  39.2 us
    unnamed x69, local copies, waits for them, and re-layouts  19.2 us
  transfers between devices with their start and end apart: 10, of which 9 were waited for; matrix products, arithmetic and copies ran while one was open for 11% of the time, Pallas kernels for 0%

profile of v2, /device:TPU:1, one launch (start us, length us, event | category | flops | bytes accessed | tf_op | source)
XLA Modules:
  0.0 661.6 jit_solution(1091013414977626246)
XLA Ops:
  12.3 1.7 dynamic-slice_reduce_fusion
  17.1 18.4 %all-gather.8.cloned.1.call-done = bf16[512,1152]{1,0:T(8,128)(2,1)} async-done(((bf16[128,1152]{1,0:T(8,128)(2,1)}), bf16[512,1152]{1,0:T(8,128)(2,1)}) %all-gather.8.cloned.1.call-update) | async-done | bytes 1179664 | tf_op jit(solution)/shard_map/all_gather | solution.py:76
  37.5 104.4 %all-gather.16.cloned.1.call-done = bf16[3964928]{0:T(1024)(128)(2,1)} async-done(((bf16[123904]{0:T(1024)(128)(2,1)}), bf16[3964928]{0:T(1024)(128)(2,1)}) %all-gather.16.cloned.1.call-update) | async-done | bytes 7929872 | tf_op jit(solution)/shard_map/all_gather | solution.py:104
  141.9 8.3 %reshape.387 = bf16[32,123904]{1,0:T(8,128)(2,1)} reshape(bf16[3964928]{0:T(1024)(128)(2,1)} %all-gather.16.cloned.1.call-done) | data formatting | bytes 15859712 | tf_op jit(solution)/shard_map/all_gather | solution.py:104
  151.1 5.8 fusion.76
  158.9 2.2 fusion.33
  162.9 2.3 reshape.361
  168.6 2.9 fusion.45
  172.9 25.4 %reduce-scatter.6.cloned.1.call-done = f32[128,1024]{1,0:T(8,128)} async-done(((f32[512,1024]{1,0:T(8,128)}), f32[128,1024]{1,0:T(8,128)}) %reduce-scatter.6.cloned.1.call-update) | async-done | bytes 524304 | tf_op jit(solution)/shard_map/reduce_scatter | solution.py:80
  201.6 4.4 reshape.363
  206.0 2.4 reshape.364
  208.4 14.3 %all-gather.10.cloned.1.call-done = bf16[512,1024]{1,0:T(8,128)(2,1)} async-done(((bf16[128,1024]{1,0:T(8,128)(2,1)}), bf16[512,1024]{1,0:T(8,128)(2,1)}) %all-gather.10.cloned.1.call-update) | async-done | bytes 1048592 | tf_op jit(solution)/shard_map/all_gather | solution.py:76
  222.7 4.6 multiply_convert_fusion.1
  228.3 2.6 fusion.83
  231.1 29.0 %reduce-scatter.8.cloned.1.call-done = f32[128,1024]{1,0:T(8,128)} async-done(((f32[512,1024]{1,0:T(8,128)}), f32[128,1024]{1,0:T(8,128)}) %reduce-scatter.8.cloned.1.call-update) | async-done | bytes 524304 | tf_op jit(solution)/shard_map/reduce_scatter | solution.py:80
  263.8 22.0 %all-gather.12.cloned.1.call-done = bf16[512,1024]{1,0:T(8,128)(2,1)} async-done(((bf16[128,1024]{1,0:T(8,128)(2,1)}), bf16[512,1024]{1,0:T(8,128)(2,1)}) %all-gather.12.cloned.1.call-update) | async-done | bytes 1048592 | tf_op jit(solution)/shard_map/all_gather | solution.py:76
  285.8 4.6 fusion.82
  290.4 2.6 fusion.40
  293.1 29.2 %reduce-scatter.10.cloned.1.call-done = f32[128,1024]{1,0:T(8,128)} async-done(((f32[512,1024]{1,0:T(8,128)}), f32[128,1024]{1,0:T(8,128)}) %reduce-scatter.10.cloned.1.call-update) | async-done | bytes 524304 | tf_op jit(solution)/shard_map/reduce_scatter | solution.py:80
  322.3 1.3 multiply_reduce_fusion.1
  325.0 2.8 convolution_convert_fusion.1
  327.8 2.4 reshape.371
  330.2 4.1 convolution_convert_fusion
  334.3 2.9 reshape.372
  338.1 8.6 %all-gather.14.cloned.1.call-done = bf16[512,1024]{1,0:T(8,128)(2,1)} async-done(((bf16[128,1024]{1,0:T(8,128)(2,1)}), bf16[512,1024]{1,0:T(8,128)(2,1)}) %all-gather.14.cloned.1.call-update) | async-done | bytes 1048592 | tf_op jit(solution)/shard_map/all_gather | solution.py:76
  346.7 1.8 convolution_convert_fusion.4
  348.5 2.7 fusion.84
  351.9 1.7 fusion.78
  353.6 9.5 %fusion.29 = bf16[4,64,512]{2,1,0:T(8,128)(2,1)} fusion(bf16[512,4,64]{0,2,1:T(8,128)(2,1)} %bitcast.114, f32[4,512,512]{1,2,0:T(8,128)} %fusion.84, f32[4,512,512]{1,2,0:T(8,128)} %copy-done.22, f32[4,512]{1,0:T(4,128)S(1)} %log.8, pred[512,512]{0,1:T(8,128)(4,1)S(1)} %copy-done.12), kind=kOutput, calls=%fused_computation.32 | convolution fusion | flops 145885696 | bytes 9183232 | tf_op jit(solution)/shard_map/shqk,sqhe->skhe/dot_general | solution.py:186
  363.1 9.4 %fusion.79 = (bf16[4,64]{1,0:T(4,128)(2,1)S(1)}, bf16[1,512,4,64]{1,3,2,0:T(8,128)(2,1)}) fusion(bf16[512,4,64]{0,2,1:T(8,128)(2,1)S(1)} %bitcast.112, f32[4,512,512]{1,2,0:T(8,128)} %fusion.84, f32[4,512]{1,0:T(4,128)S(1)} %log.8, f32[4,512,512]{1,2,0:T(8,128)} %copy-done.22, pred[512,512]{0,1:T(8,128)(4,1)S(1)} %copy-done.12), kind=kOutput, calls=%fused_computation.145 | convolution fusion | flops 146016512 | bytes 9183744 | tf_op jit(solution)/shard_map/shqk,skhe->sqhe/dot_general | solution.py:183
  372.5 4.0 fusion.47
  377.5 3.5 convolution_convert_fusion.2
  381.0 2.8 reshape.369
  383.8 2.7 constant_dynamic-update-slice_fusion.10
  386.5 1.6 broadcast_in_dim.35
  389.4 4.2 reshape.370
  394.0 3.3 constant_dynamic-update-slice_fusion.9
  397.3 1.4 constant_dynamic-update-slice_fusion.8
  398.9 1.5 constant_dynamic-update-slice_fusion.7
  401.0 1.3 dynamic-update-slice.5
  402.3 1.4 dynamic-update-slice.6
  403.7 7.0 %pad.9 = bf16[32,126976]{1,0:T(8,128)(2,1)} pad(bf16[32,123264]{1,0:T(8,128)(2,1)} %dynamic-update-slice.6, bf16[]{:T(256)} %constant.31.clone.1), padding=0_0x0_3712 | pad | bytes 16015362 | tf_op jit(solution)/shard_map/jit(_pad)/pad | solution.py:224
  410.8 8.7 %reshape.377 = bf16[1024,3968]{1,0:T(8,128)(2,1)} reshape(bf16[32,126976]{1,0:T(8,128)(2,1)} %pad.9) | data formatting | bytes 16252928 | tf_op jit(solution)/shard_map/reshape | solution.py:224
  419.5 1.9 add_bitcast_fusion
  421.4 177.4 %reduce-scatter.14.cloned.1.call-done = bf16[32,3968]{1,0:T(8,128)(2,1)} async-done(((bf16[1024,3968]{1,0:T(8,128)(2,1)}), bf16[32,3968]{1,0:T(8,128)(2,1)}) %reduce-scatter.14.cloned.1.call-update) | async-done | bytes 253968 | tf_op jit(solution)/shard_map/reduce_scatter | solution.py:225
  599.9 39.2 %all-gather.1 = bf16[4,1,126976]{2,1,0:T(2,128)(2,1)S(1)} all-gather(bf16[1,1,126976]{2,1,0:T(2,128)(2,1)S(1)} %reshape.388), channel_id=1, replica_groups=mesh['rep'=4,'shard'=32] {'rep'}, dimensions={0}, use_global_device_ids=true | all-gather | bytes 1269760 | tf_op jit(solution)/shard_map/all_gather | solution.py:226
  644.3 3.1 copy.67
  647.5 4.4 broadcast_in_dim_reshape.20
  (190 shorter events, 42.5 us)
Async XLA Ops:
  7.2 7.0 %copy-start = (bf16[1,128,1024]{2,1,0:T(8,128)(2,1)S(1)}, bf16[1,128,1024]{2,1,0:T(8,128)(2,1)}, u32[]{:S(2)}) copy-start(bf16[1,128,1024]{2,1,0:T(8,128)(2,1)} %param.16) | copy-start | bytes 786436
  7.2 4.2 copy-start.16
  7.2 4.3 copy-start.11
  7.2 28.4 %all-gather.8.cloned.1.call-start = ((), (), s32[]{:S(2)}) async-start(), calls=%async_computation.5 | async-start | bytes 1474560 | tf_op jit(solution)/shard_map/all_gather | solution.py:76
  9.1 5.6 copy-start.18
  9.1 6.4 copy-start.17
  9.2 6.4 copy-start.19
  9.9 132.0 %all-gather.16.cloned.1.call-start = ((), (), s32[]{:S(2)}) async-start(), calls=%async_computation.14 | async-start | bytes 8177664 | tf_op jit(solution)/shard_map/all_gather | solution.py:104
  17.1 181.2 %reduce-scatter.6.cloned.1.call-start = ((), (), s32[]{:S(2)}) async-start(), calls=%async_computation.6 | async-start | bytes 2621440 | tf_op jit(solution)/shard_map/reduce_scatter | solution.py:80
  151.1 5.9 slice-start
  157.8 1.2 copy-start.9
  161.2 1.7 copy-start.4
  161.7 3.5 copy-start.15
  161.8 3.4 copy-start.13
  162.9 2.3 copy-start.12
  166.5 2.0 copy-start.22
  168.6 29.8 %copy-start.8 = (f32[1,128,1024]{2,1,0:T(8,128)S(1)}, f32[1,128,1024]{2,1,0:T(8,128)}, u32[]{:S(2)}) copy-start(f32[1,128,1024]{2,1,0:T(8,128)} %param.10) | copy-start | bytes 1572868
  171.5 51.2 %all-gather.10.cloned.1.call-start = ((), (), s32[]{:S(2)}) async-start(), calls=%async_computation.7 | async-start | bytes 1310720 | tf_op jit(solution)/shard_map/all_gather | solution.py:76
  200.6 59.5 %reduce-scatter.8.cloned.1.call-start = ((), (), s32[]{:S(2)}) async-start(), calls=%async_computation.8 | async-start | bytes 2621440 | tf_op jit(solution)/shard_map/reduce_scatter | solution.py:80
  201.6 4.4 copy-start.3
  208.4 19.9 %copy-start.7 = (bf16[1024,1024]{1,0:T(8,128)(2,1)S(1)}, bf16[1024,1024]{1,0:T(8,128)(2,1)}, u32[]{:S(2)}) copy-start(bf16[1024,1024]{1,0:T(8,128)(2,1)} %reshape.364) | copy-start | bytes 6291460
  227.3 1.0 copy-start.24
  230.9 30.8 %copy-start.5 = (f32[1,128,1024]{2,1,0:T(8,128)S(1)}, f32[1,128,1024]{2,1,0:T(8,128)}, u32[]{:S(2)}) copy-start(f32[1,128,1024]{2,1,0:T(8,128)} %param.12) | copy-start | bytes 1572868
  230.9 54.9 %all-gather.12.cloned.1.call-start = ((), (), s32[]{:S(2)}) async-start(), calls=%async_computation.9 | async-start | bytes 1310720 | tf_op jit(solution)/shard_map/all_gather | solution.py:76
  263.8 58.6 %reduce-scatter.10.cloned.1.call-start = ((), (), s32[]{:S(2)}) async-start(), calls=%async_computation.10 | async-start | bytes 2621440 | tf_op jit(solution)/shard_map/reduce_scatter | solution.py:80
  285.8 4.6 copy-start.6
  290.4 2.7 copy-start.25
  293.1 53.6 %all-gather.14.cloned.1.call-start = ((), (), s32[]{:S(2)}) async-start(), calls=%async_computation.11 | async-start | bytes 1310720 | tf_op jit(solution)/shard_map/all_gather | solution.py:76
  324.6 94.8 %reduce-scatter.12.cloned.1.call-start = ((), (), s32[]{:S(2)}) async-start(), calls=%async_computation.12 | async-start | bytes 2621440 | tf_op jit(solution)/shard_map/reduce_scatter | solution.py:80
  348.5 3.4 copy-start.23
  353.6 9.5 %copy-start.14 = (bf16[512,256]{0,1:T(8,128)(2,1)S(1)}, bf16[512,256]{0,1:T(8,128)(2,1)}, u32[]{:S(2)}) copy-start(bf16[512,256]{0,1:T(8,128)(2,1)} %copy-done.13) | copy-start | bytes 786436
  376.5 0.9 copy-start.20
  376.5 1.0 copy-start.21
  376.5 222.3 %reduce-scatter.14.cloned.1.call-start = ((), (), s32[]{:S(2)}) async-start(), calls=%async_computation.13 | async-start | bytes 8380416 | tf_op jit(solution)/shard_map/reduce_scatter | solution.py:225
  383.8 4.3 copy-start.10
  394.0 3.3 copy-start.2
  644.3 10.0 %copy-start.1 = (bf16[1,128,1024]{2,1,0:T(8,128)(2,1)S(1)}, bf16[1,128,1024]{2,1,0:T(8,128)(2,1)}, u32[]{:S(2)}) copy-start(bf16[1,128,1024]{2,1,0:T(8,128)(2,1)} %param.16) | copy-start | bytes 786436
Sparse Core Ops, SparseCore 0:
  10.3 25.2 all-gather.7
  39.3 102.5 all-gather.15
  171.6 26.7 reduce-scatter.5
  200.8 21.8 all-gather.9
  231.0 29.0 reduce-scatter.7
  263.9 21.8 all-gather.11
  293.2 29.0 reduce-scatter.9
  324.8 21.8 all-gather.13
  376.6 29.0 reduce-scatter.11
  419.6 179.1 reduce-scatter.13

commit v3 on v2

--- a/solution.py
+++ b/solution.py
@@ -220,9 +220,10 @@
     g_offsets = [sum(g_sizes[:i]) for i in range(len(g_sizes) + 1)]
     grad_pack = jnp.concatenate(grad_parts, axis=1)
     width = grad_pack.shape[1]
-    padded = -(-width // 4096) * 4096
-    grad_pack = jnp.pad(grad_pack, ((0, 0), (0, padded - width))).reshape(parts * 32, -1)
-    shares = lax.psum_scatter(grad_pack, "shard", scatter_dimension=0, tiled=True)
+    padded = -(-width // 1024) * 1024
+    grad_pack = jnp.pad(grad_pack, ((0, 0), (0, padded - width)))
+    received = lax.all_to_all(grad_pack, "shard", 0, 0, tiled=True)
+    shares = jnp.sum(received.astype(jnp.float32), axis=0).astype(jnp.bfloat16)
     joined = lax.all_gather(shares.reshape(-1), "rep", axis=0, tiled=False).astype(jnp.float32)
     got = [joined[:, g_offsets[i] : g_offsets[i + 1]] for i in range(len(g_sizes))]
     grad_w_qkv = got[0].reshape(reps, k_rows, 3, head_cols).transpose(1, 2, 0, 3).reshape(k_rows, -1)

time: 671 us -> 639 us (0.952)
  the two profiles are of different devices: /device:TPU:1 before, /device:TPU:5 now
where the time goes in v3:
time: 639 us; the launch traced here: 629 us
  waiting for transfers between devices  361 us (56%)
  local copies, waits for them, and re-layouts  125 us (20%)
  matrix products  62.7 us (10%)
  other arithmetic  44.6 us (7%)
  between operations  14.8 us (2%)
  starting transfers between devices  10.1 us (2%)
  blocking collectives  10.1 us (2%)
    reduce_scatter x4, waiting for transfers between devices, scatter_rep(): return lax.psum_scatter(tensor, 'rep', scatter_dimension=0, tiled=True)  180 us
    all_gather x1, waiting for transfers between devices, local(): gathered = lax.all_gather(packed, 'shard', axis=0, tiled=False)  104 us
    all_gather x4, waiting for transfers between devices, gather_rep(): return lax.all_gather(tensor, 'rep', axis=0, tiled=True)  57.1 us
    unnamed x69, local copies, waits for them, and re-layouts  49.5 us
    all_to_all x1, waiting for transfers between devices, local(): received = lax.all_to_all(grad_pack, 'shard', 0, 0, tiled=True)  19 us
    reduce_sum x1, other arithmetic, local(): shares = jnp.sum(received.astype(jnp.float32), axis=0).astype(jnp.bfloat16)  16.6 us
    dot_general x4, matrix products, matmul_lt(): lax.dot_general(first_op, second_op, (((0,), (0,)), ((), ())), preferred_...  13.1 us
  transfers between devices with their start and end apart: 10, of which 10 were waited for; matrix products, arithmetic and copies ran while one was open for 6% of the time, Pallas kernels for 0%

profile of v3, /device:TPU:5, one launch (start us, length us, event | category | flops | bytes accessed | tf_op | source)
XLA Modules:
  0.0 628.5 jit_solution(9531023695125590099)
XLA Ops:
  15.6 1.7 dynamic-slice_reduce_fusion
  19.0 15.7 %all-gather.8.cloned.1.call-done = bf16[512,1152]{1,0:T(8,128)(2,1)} async-done(((bf16[128,1152]{1,0:T(8,128)(2,1)}), bf16[512,1152]{1,0:T(8,128)(2,1)}) %all-gather.8.cloned.1.call-update) | async-done | bytes 1179664 | tf_op jit(solution)/shard_map/all_gather | solution.py:76
  36.6 104.4 %all-gather.16.cloned.1.call-done = bf16[3964928]{0:T(1024)(128)(2,1)} async-done(((bf16[123904]{0:T(1024)(128)(2,1)}), bf16[3964928]{0:T(1024)(128)(2,1)}) %all-gather.16.cloned.1.call-update) | async-done | bytes 7929872 | tf_op jit(solution)/shard_map/all_gather | solution.py:104
  141.1 8.3 %reshape.385 = bf16[32,123904]{1,0:T(8,128)(2,1)} reshape(bf16[3964928]{0:T(1024)(128)(2,1)} %all-gather.16.cloned.1.call-done) | data formatting | bytes 15859712 | tf_op jit(solution)/shard_map/all_gather | solution.py:104
  150.2 5.8 fusion.76
  158.3 2.2 fusion.33
  162.3 2.3 reshape.360
  168.0 2.9 fusion.45
  172.3 25.4 %reduce-scatter.5.cloned.1.call-done = f32[128,1024]{1,0:T(8,128)} async-done(((f32[512,1024]{1,0:T(8,128)}), f32[128,1024]{1,0:T(8,128)}) %reduce-scatter.5.cloned.1.call-update) | async-done | bytes 524304 | tf_op jit(solution)/shard_map/reduce_scatter | solution.py:80
  201.4 4.4 reshape.363
  205.7 2.4 reshape.362
  208.1 14.0 %all-gather.10.cloned.1.call-done = bf16[512,1024]{1,0:T(8,128)(2,1)} async-done(((bf16[128,1024]{1,0:T(8,128)(2,1)}), bf16[512,1024]{1,0:T(8,128)(2,1)}) %all-gather.10.cloned.1.call-update) | async-done | bytes 1048592 | tf_op jit(solution)/shard_map/all_gather | solution.py:76
  222.1 4.6 multiply_convert_fusion.1
  227.7 2.6 fusion.83
  230.6 29.0 %reduce-scatter.7.cloned.1.call-done = f32[128,1024]{1,0:T(8,128)} async-done(((f32[512,1024]{1,0:T(8,128)}), f32[128,1024]{1,0:T(8,128)}) %reduce-scatter.7.cloned.1.call-update) | async-done | bytes 524304 | tf_op jit(solution)/shard_map/reduce_scatter | solution.py:80
  263.3 22.0 %all-gather.12.cloned.1.call-done = bf16[512,1024]{1,0:T(8,128)(2,1)} async-done(((bf16[128,1024]{1,0:T(8,128)(2,1)}), bf16[512,1024]{1,0:T(8,128)(2,1)}) %all-gather.12.cloned.1.call-update) | async-done | bytes 1048592 | tf_op jit(solution)/shard_map/all_gather | solution.py:76
  285.3 4.6 fusion.82
  289.9 2.6 fusion.40
  292.6 29.2 %reduce-scatter.9.cloned.1.call-done = f32[128,1024]{1,0:T(8,128)} async-done(((f32[512,1024]{1,0:T(8,128)}), f32[128,1024]{1,0:T(8,128)}) %reduce-scatter.9.cloned.1.call-update) | async-done | bytes 524304 | tf_op jit(solution)/shard_map/reduce_scatter | solution.py:80
  324.4 4.2 convolution_convert_fusion.1
  328.6 2.9 reshape.370
  331.5 4.2 convolution_convert_fusion
  335.7 4.2 reshape.371
  340.7 5.4 all-gather.14.cloned.1.call-done
  346.1 1.8 convolution_convert_fusion.4
  347.9 2.7 fusion.84
  351.3 1.7 fusion.78
  353.1 9.5 %fusion.29 = bf16[4,64,512]{2,1,0:T(8,128)(2,1)} fusion(bf16[512,4,64]{0,2,1:T(8,128)(2,1)} %bitcast.110, f32[4,512,512]{1,2,0:T(8,128)} %fusion.84, f32[4,512,512]{1,2,0:T(8,128)} %copy-done.22, f32[4,512]{1,0:T(4,128)S(1)} %log.8, pred[512,512]{0,1:T(8,128)(4,1)S(1)} %copy-done.14), kind=kOutput, calls=%fused_computation.33 | convolution fusion | flops 145885696 | bytes 9183232 | tf_op jit(solution)/shard_map/shqk,sqhe->skhe/dot_general | solution.py:186
  362.6 9.4 %fusion.79 = (bf16[4,64]{1,0:T(4,128)(2,1)S(1)}, bf16[1,512,4,64]{1,3,2,0:T(8,128)(2,1)}) fusion(bf16[512,4,64]{0,2,1:T(8,128)(2,1)S(1)} %bitcast.108, f32[4,512,512]{1,2,0:T(8,128)} %fusion.84, f32[4,512]{1,0:T(4,128)S(1)} %log.8, f32[4,512,512]{1,2,0:T(8,128)} %copy-done.22, pred[512,512]{0,1:T(8,128)(4,1)S(1)} %copy-done.14), kind=kOutput, calls=%fused_computation.146 | convolution fusion | flops 146016512 | bytes 9183744 | tf_op jit(solution)/shard_map/shqk,skhe->sqhe/dot_general | solution.py:183
  371.9 1.6 broadcast_in_dim.35
  374.8 4.4 reshape.369
  379.8 3.5 convolution_convert_fusion.2
  383.2 2.7 reshape.368
  386.0 2.8 constant_dynamic-update-slice_fusion.10
  390.2 1.5 constant_dynamic-update-slice_fusion.8
  397.4 6.8 %pad_bitcast_fusion = bf16[32,1,123904]{2,0,1:T(8,128)(2,1)} fusion(bf16[32,123264]{1,0:T(8,128)(2,1)} %dynamic-update-slice.6), kind=kLoop, calls=%fused_computation.1 | loop fusion | bytes 15818752 | tf_op jit(solution)/shard_map/all_to_all | solution.py:225
  404.7 11.1 %reduce.51 = bf16[32,123904]{1,0:T(8,128)(2,1)} reduce(bf16[32,1,123904]{2,0,1:T(8,128)(2,1)} %pad_bitcast_fusion, bf16[]{:T(256)} %broadcast.197), dimensions={1}, to_apply=%copy.79.reduce_sub_computation | reduce | bytes 15859714 | tf_op jit(solution)/shard_map/all_to_all | solution.py:225
  415.8 10.5 %reshape.436 = bf16[32,2,61952]{2,1,0:T(2,128)(2,1)} reshape(bf16[32,123904]{1,0:T(8,128)(2,1)} %reduce.51) | data formatting | bytes 15859712
  426.3 9.3 %all-to-all-start = ((bf16[32,2,61952]{2,1,0:T(2,128)(2,1)}), bf16[32,2,61952]{2,1,0:T(2,128)(2,1)}, u32[]{:S(2)}, u32[]{:S(2)}) async-start(bf16[32,2,61952]{2,1,0:T(2,128)(2,1)} %reshape.436), calls=%async_computation.4 | async-start | bytes 15859712 | tf_op jit(solution)/shard_map/all_to_all | solution.py:225
  435.7 2.4 fusion.47
  438.2 96.5 %reduce-scatter.11.cloned.1.call-done = f32[128,1024]{1,0:T(8,128)} async-done(((f32[512,1024]{1,0:T(8,128)}), f32[128,1024]{1,0:T(8,128)}) %reduce-scatter.11.cloned.1.call-update) | async-done | bytes 524304 | tf_op jit(solution)/shard_map/reduce_scatter | solution.py:80
  534.6 1.9 add_bitcast_fusion
  536.5 19.0 %all-to-all-done = bf16[32,2,61952]{2,1,0:T(2,128)(2,1)} async-done(((bf16[32,2,61952]{2,1,0:T(2,128)(2,1)}), bf16[32,2,61952]{2,1,0:T(2,128)(2,1)}, u32[]{:S(2)}, u32[]{:S(2)}) %all-to-all-start) | async-done | bytes 7929888 | tf_op jit(solution)/shard_map/all_to_all | solution.py:225
  555.6 22.8 %reshape.437 = bf16[32,1,123904]{2,1,0:T(2,128)(2,1)} reshape(bf16[32,2,61952]{2,1,0:T(2,128)(2,1)} %all-to-all-done) | data formatting | bytes 15859712
  578.3 16.6 %reduce_sum.238 = bf16[123904]{0:T(1024)(128)(2,1)S(1)} reduce(bf16[32,1,123904]{2,1,0:T(2,128)(2,1)} %reshape.437, bf16[]{:T(256)} %constant.52.clone.1), dimensions={0,1}, to_apply=%region_23.24 | reduce | flops 3841024 | bytes 8177666 | tf_op jit(solution)/shard_map/reduce_sum | solution.py:226
  594.9 10.1 %all-gather.1 = bf16[495616]{0:T(1024)(128)(2,1)S(1)} all-gather(bf16[123904]{0:T(1024)(128)(2,1)S(1)} %reduce_sum.238), channel_id=3, replica_groups=mesh['rep'=4,'shard'=32] {'rep'}, dimensions={0}, use_global_device_ids=true | all-gather | bytes 1239040 | tf_op jit(solution)/shard_map/all_gather | solution.py:227
  614.0 3.1 copy.91
  617.2 4.4 broadcast_in_dim_reshape.20
  (192 shorter events, 52.6 us)
Async XLA Ops:
  7.2 7.1 %copy-start = (bf16[1,128,1024]{2,1,0:T(8,128)(2,1)S(1)}, bf16[1,128,1024]{2,1,0:T(8,128)(2,1)}, u32[]{:S(2)}) copy-start(bf16[1,128,1024]{2,1,0:T(8,128)(2,1)} %param.16) | copy-start | bytes 786436
  7.2 7.1 %copy-start.18 = (bf16[1,32,3072]{2,1,0:T(8,128)(2,1)S(1)}, bf16[1,32,3072]{2,1,0:T(8,128)(2,1)}, u32[]{:S(2)}) copy-start(bf16[1,32,3072]{2,1,0:T(8,128)(2,1)} %param.13) | copy-start | bytes 589828
  7.2 7.6 %copy-start.13 = (bf16[1,32,4096]{2,1,0:T(8,128)(2,1)S(1)}, bf16[1,32,4096]{2,1,0:T(8,128)(2,1)}, u32[]{:S(2)}) copy-start(bf16[1,32,4096]{2,1,0:T(8,128)(2,1)} %param.15) | copy-start | bytes 786436
  7.2 27.5 %all-gather.8.cloned.1.call-start = ((), (), s32[]{:S(2)}) async-start(), calls=%async_computation.5 | async-start | bytes 1474560 | tf_op jit(solution)/shard_map/all_gather | solution.py:76
  9.9 131.2 %all-gather.16.cloned.1.call-start = ((), (), s32[]{:S(2)}) async-start(), calls=%async_computation.13 | async-start | bytes 8177664 | tf_op jit(solution)/shard_map/all_gather | solution.py:104
  19.0 178.8 %reduce-scatter.5.cloned.1.call-start = ((), (), s32[]{:S(2)}) async-start(), calls=%async_computation.6 | async-start | bytes 2621440 | tf_op jit(solution)/shard_map/reduce_scatter | solution.py:80
  150.2 6.2 slice-start
  157.2 1.2 copy-start.10
  160.5 1.8 copy-start.5
  160.9 3.7 copy-start.17
  161.1 3.6 copy-start.15
  162.3 2.3 copy-start.14
  166.0 2.0 copy-start.22
  168.0 29.8 %copy-start.9 = (f32[1,128,1024]{2,1,0:T(8,128)S(1)}, f32[1,128,1024]{2,1,0:T(8,128)}, u32[]{:S(2)}) copy-start(f32[1,128,1024]{2,1,0:T(8,128)} %param.10) | copy-start | bytes 1572868
  170.9 51.2 %all-gather.10.cloned.1.call-start = ((), (), s32[]{:S(2)}) async-start(), calls=%async_computation.7 | async-start | bytes 1310720 | tf_op jit(solution)/shard_map/all_gather | solution.py:76
  200.1 59.5 %reduce-scatter.7.cloned.1.call-start = ((), (), s32[]{:S(2)}) async-start(), calls=%async_computation.8 | async-start | bytes 2621440 | tf_op jit(solution)/shard_map/reduce_scatter | solution.py:80
  201.4 4.4 copy-start.4
  208.1 19.6 %copy-start.7 = (bf16[1024,1024]{1,0:T(8,128)(2,1)S(1)}, bf16[1024,1024]{1,0:T(8,128)(2,1)}, u32[]{:S(2)}) copy-start(bf16[1024,1024]{1,0:T(8,128)(2,1)} %reshape.363) | copy-start | bytes 6291460
  226.7 1.0 copy-start.24
  230.3 30.8 %copy-start.6 = (f32[1,128,1024]{2,1,0:T(8,128)S(1)}, f32[1,128,1024]{2,1,0:T(8,128)}, u32[]{:S(2)}) copy-start(f32[1,128,1024]{2,1,0:T(8,128)} %param.12) | copy-start | bytes 1572868
  230.3 54.9 %all-gather.12.cloned.1.call-start = ((), (), s32[]{:S(2)}) async-start(), calls=%async_computation.9 | async-start | bytes 1310720 | tf_op jit(solution)/shard_map/all_gather | solution.py:76
  263.2 58.6 %reduce-scatter.9.cloned.1.call-start = ((), (), s32[]{:S(2)}) async-start(), calls=%async_computation.10 | async-start | bytes 2621440 | tf_op jit(solution)/shard_map/reduce_scatter | solution.py:80
  285.2 4.6 copy-start.8
  289.8 2.7 copy-start.25
  292.5 53.6 %all-gather.14.cloned.1.call-start = ((), (), s32[]{:S(2)}) async-start(), calls=%async_computation.11 | async-start | bytes 1310720 | tf_op jit(solution)/shard_map/all_gather | solution.py:76
  347.9 3.4 copy-start.23
  353.1 9.5 %copy-start.16 = (bf16[512,256]{0,1:T(8,128)(2,1)S(1)}, bf16[512,256]{0,1:T(8,128)(2,1)}, u32[]{:S(2)}) copy-start(bf16[512,256]{0,1:T(8,128)(2,1)} %copy-done.15) | copy-start | bytes 786436
  371.9 1.6 copy-start.12
  374.8 5.0 copy-start.19
  374.8 5.0 copy-start.20
  386.0 2.8 copy-start.3
  390.2 2.3 copy-start.2
  426.3 9.4 %copy-start.11 = (bf16[1024,768]{1,0:T(8,128)(2,1)S(1)}, bf16[1024,768]{1,0:T(8,128)(2,1)}, u32[]{:S(2)}) copy-start(bf16[1024,768]{1,0:T(8,128)(2,1)} %copy-done.10) | copy-start | bytes 4718596
  426.3 9.4 %copy-start.21 = (bf16[1,512,4,64]{1,3,2,0:T(8,128)(2,1)S(1)}, bf16[1,512,4,64]{1,3,2,0:T(8,128)(2,1)}, u32[]{:S(2)}) copy-start(bf16[1,512,4,64]{1,3,2,0:T(8,128)(2,1)} %get-tuple-element.45) | copy-start | bytes 786436
  426.3 129.3 %all-to-all-start = ((bf16[32,2,61952]{2,1,0:T(2,128)(2,1)}), bf16[32,2,61952]{2,1,0:T(2,128)(2,1)}, u32[]{:S(2)}, u32[]{:S(2)}) async-start(bf16[32,2,61952]{2,1,0:T(2,128)(2,1)} %reshape.436), calls=%async_computation.4 | async-start | bytes 15859712 | tf_op jit(solution)/shard_map/all_to_all | solution.py:225
  435.6 99.0 %reduce-scatter.11.cloned.1.call-start = ((), (), s32[]{:S(2)}) async-start(), calls=%async_computation.12 | async-start | bytes 2621440 | tf_op jit(solution)/shard_map/reduce_scatter | solution.py:80
  614.0 7.6 %copy-start.1 = (bf16[1,128,1024]{2,1,0:T(8,128)(2,1)S(1)}, bf16[1,128,1024]{2,1,0:T(8,128)(2,1)}, u32[]{:S(2)}) copy-start(bf16[1,128,1024]{2,1,0:T(8,128)(2,1)} %param.16) | copy-start | bytes 786436
Sparse Core Ops, SparseCore 0:
  10.3 24.3 all-gather.7
  38.5 102.5 all-gather.15
  171.0 26.7 reduce-scatter.4
  200.2 21.8 all-gather.9
  230.5 29.0 reduce-scatter.6
  263.3 21.8 all-gather.11
  292.6 29.0 reduce-scatter.8
  324.2 21.8 all-gather.13
  439.0 95.6 reduce-scatter.10

commit v4 on v3

--- a/solution.py
+++ b/solution.py
@@ -96,7 +96,7 @@
     up_piece = pick(w_up[0].reshape(k_rows, parts, reps, ff_piece), r, 2).reshape(k_rows, -1)
     down_piece = pick(w_down[0].reshape(reps, ff_piece, D), r, 0)
     upb_piece = pick(up_bias[0].reshape(reps, ff_piece), r, 0)
-    pieces = (qkv_piece, out_piece, up_piece, down_piece, upb_piece, biases[0], norm_gains[0])
+    pieces = (qkv_piece, upb_piece, biases[0], norm_gains[0])
     sizes = [piece.size for piece in pieces]
     offsets = [sum(sizes[:i]) for i in range(len(sizes) + 1)]
     packed = jnp.concatenate([piece.reshape(-1) for piece in pieces])
@@ -104,13 +104,17 @@
     gathered = lax.all_gather(packed, "shard", axis=0, tiled=False)
     got = [gathered[:, offsets[i] : offsets[i + 1]] for i in range(len(sizes))]
     w_qkv_r = got[0].reshape(D, 3 * head_cols)
-    w_out_all = got[1].reshape(D, D)
+    up_bias_r = got[1].reshape(-1)
+    bias_all = unpack_cols(got[2], parts, biases.shape[1])
+    gain_all = unpack_cols(got[3], parts, norm_gains.shape[1])
+    big = jnp.concatenate([out_piece, up_piece, down_piece], axis=1).reshape(8, -1)
+    big_all = lax.all_to_all(
+        jnp.broadcast_to(big[None], (parts,) + big.shape), "shard", 0, 0, tiled=True
+    ).reshape(parts, k_rows, -1)
+    w_out_all = big_all[:, :, :D].reshape(D, D)
     w_out_r = lax.dynamic_slice_in_dim(w_out_all, r * head_cols, head_cols, axis=0)
-    w_up_r = got[2].reshape(D, -1)
-    w_down_r = got[3].reshape(-1, D)
-    up_bias_r = got[4].reshape(-1)
-    bias_all = unpack_cols(got[5], parts, biases.shape[1])
-    gain_all = unpack_cols(got[6], parts, norm_gains.shape[1])
+    w_up_r = big_all[:, :, D : D + up_piece.shape[1]].reshape(D, -1)
+    w_down_r = big_all[:, :, D + up_piece.shape[1] :].reshape(-1, D)
     bias_q = lax.dynamic_slice_in_dim(bias_all[0], r * head_cols, head_cols)
     bias_v = lax.dynamic_slice_in_dim(bias_all[1], r * head_cols, head_cols)
 
@@ -161,6 +165,12 @@
     d_bup = jnp.sum(d_pre, axis=0)
     d_pre_b = d_pre.astype(jnp.bfloat16)
     d_wup = matmul_lt(mid_all, d_pre_b)
+    ffn_pack = jnp.concatenate(
+        [d_wup.astype(jnp.bfloat16).reshape(parts, -1), d_wdown.astype(jnp.bfloat16).reshape(parts, -1)],
+        axis=1,
+    ).reshape(parts, 8, -1)
+    ffn_recv = lax.all_to_all(ffn_pack, "shard", 0, 0, tiled=True)
+    ffn_share = jnp.sum(ffn_recv.astype(jnp.float32), axis=0).astype(jnp.bfloat16)
     d_mid = d_second + scatter_rep(matmul_rt(d_pre_b, w_up_r))
     d_gain_one = jnp.sum(d_mid * norm_one, axis=0)
     d_bias_one = jnp.sum(d_mid, axis=0)
@@ -210,29 +220,30 @@
     grad_parts = (
         d_wqkv.astype(jnp.bfloat16).reshape(parts, -1),
         d_wout_all.reshape(parts, -1),
-        d_wup.astype(jnp.bfloat16).reshape(parts, -1),
-        d_wdown.astype(jnp.bfloat16).reshape(parts, -1),
         d_bup_all.astype(jnp.bfloat16).reshape(parts, -1),
         pack_cols(d_biases.astype(jnp.bfloat16), parts),
         pack_cols(d_gains.astype(jnp.bfloat16), parts),
     )
     g_sizes = [piece.shape[1] for piece in grad_parts]
-    g_offsets = [sum(g_sizes[:i]) for i in range(len(g_sizes) + 1)]
     grad_pack = jnp.concatenate(grad_parts, axis=1)
     width = grad_pack.shape[1]
     padded = -(-width // 1024) * 1024
-    grad_pack = jnp.pad(grad_pack, ((0, 0), (0, padded - width)))
+    grad_pack = jnp.pad(grad_pack, ((0, 0), (0, padded - width))).reshape(parts, 8, -1)
     received = lax.all_to_all(grad_pack, "shard", 0, 0, tiled=True)
     shares = jnp.sum(received.astype(jnp.float32), axis=0).astype(jnp.bfloat16)
-    joined = lax.all_gather(shares.reshape(-1), "rep", axis=0, tiled=False).astype(jnp.float32)
-    got = [joined[:, g_offsets[i] : g_offsets[i + 1]] for i in range(len(g_sizes))]
-    grad_w_qkv = got[0].reshape(reps, k_rows, 3, head_cols).transpose(1, 2, 0, 3).reshape(k_rows, -1)
-    grad_w_out = jnp.sum(got[1], axis=0).reshape(k_rows, D)
-    grad_w_up = got[2].reshape(reps, k_rows, parts, ff_piece).transpose(1, 2, 0, 3).reshape(k_rows, -1)
-    grad_w_down = got[3].reshape(reps * ff_piece, D)
-    grad_up_bias = jnp.sum(got[4], axis=0)
-    grad_biases = jnp.sum(got[5], axis=0).reshape(biases.shape[1], -1)
-    grad_gains = jnp.sum(got[6], axis=0).reshape(norm_gains.shape[1], -1)
+    all_shares = jnp.concatenate([shares.reshape(-1), ffn_share.reshape(-1)])
+    joined = lax.all_gather(all_shares, "rep", axis=0, tiled=False).astype(jnp.float32)
+    g_sizes = g_sizes + [padded - width, ffn_share.size // 2, ffn_share.size // 2]
+    names = ["qkv", "out", "bup", "bias", "gain", "pad", "up", "down"]
+    g_offsets = [sum(g_sizes[:i]) for i in range(len(g_sizes) + 1)]
+    got = {names[i]: joined[:, g_offsets[i] : g_offsets[i + 1]] for i in range(len(g_sizes))}
+    grad_w_qkv = got["qkv"].reshape(reps, k_rows, 3, head_cols).transpose(1, 2, 0, 3).reshape(k_rows, -1)
+    grad_w_out = jnp.sum(got["out"], axis=0).reshape(k_rows, D)
+    grad_w_up = got["up"].reshape(reps, k_rows, parts, ff_piece).transpose(1, 2, 0, 3).reshape(k_rows, -1)
+    grad_w_down = got["down"].reshape(reps * ff_piece, D)
+    grad_up_bias = jnp.sum(got["bup"], axis=0)
+    grad_biases = jnp.sum(got["bias"], axis=0).reshape(biases.shape[1], -1)
+    grad_gains = jnp.sum(got["gain"], axis=0).reshape(norm_gains.shape[1], -1)
     return (
         layer_out[None],
         input_grad[None],

time: 639 us -> 552 us (0.86)
  the two profiles are of different devices: /device:TPU:5 before, /device:TPU:1 now
where the time goes in v4:
time: 552 us; the launch traced here: 546 us
  waiting for transfers between devices  314 us (57%)
  local copies, waits for them, and re-layouts  85.8 us (16%)
  matrix products  57.7 us (10%)
  starting transfers between devices  28.6 us (5%)
  other arithmetic  28.2 us (5%)
  blocking collectives  17.5 us (3%)
  between operations  14.7 us (3%)
    all_gather x1, waiting for transfers between devices, local(): gathered = lax.all_gather(packed, 'shard', axis=0, tiled=False)  99.3 us
    reduce_scatter x4, waiting for transfers between devices, scatter_rep(): return lax.psum_scatter(tensor, 'rep', scatter_dimension=0, tiled=True)  82.6 us
    all_gather x4, waiting for transfers between devices, gather_rep(): return lax.all_gather(tensor, 'rep', axis=0, tiled=True)  82.2 us
    all_to_all x1, waiting for transfers between devices, local(): received = lax.all_to_all(grad_pack, 'shard', 0, 0, tiled=True)  39.7 us
    all_gather x1, blocking collectives, local(): lax.all_gather(all_shares, 'rep', axis=0, tiled=False).astype(jnp.float32)  17.5 us
    unnamed x82, local copies, waits for them, and re-layouts  12.7 us
    dot_general x4, matrix products, matmul_lt(): lax.dot_general(first_op, second_op, (((0,), (0,)), ((), ())), preferred_...  11.8 us
    dot_general x4, matrix products, matmul(): return jnp.dot(first_op, second_op, preferred_element_type=jnp.float32)  11.8 us
  transfers between devices with their start and end apart: 12, of which 9 were waited for; matrix products, arithmetic and copies ran while one was open for 22% of the time, Pallas kernels for 0%

profile of v4, /device:TPU:1, one launch (start us, length us, event | category | flops | bytes accessed | tf_op | source)
XLA Modules:
  0.0 546.0 jit_solution(15871919214679311929)
XLA Ops:
  11.6 1.7 dynamic-slice_reduce_fusion
  13.9 3.4 broadcast_in_dim.38
  17.2 11.4 %all-to-all-start = ((bf16[32,8,12288]{2,1,0:T(8,128)(2,1)}), bf16[32,8,12288]{2,1,0:T(8,128)(2,1)}, u32[]{:S(2)}, u32[]{:S(2)}) async-start(bf16[32,8,12288]{2,1,0:T(8,128)(2,1)} %broadcast_in_dim.38), calls=%async_computation | async-start | bytes 12582912 | tf_op jit(solution)/shard_map/all_to_all | solution.py:111
  31.7 38.6 %all-gather.8.cloned.1.call-done = bf16[512,1152]{1,0:T(8,128)(2,1)} async-done(((bf16[128,1152]{1,0:T(8,128)(2,1)}), bf16[512,1152]{1,0:T(8,128)(2,1)}) %all-gather.8.cloned.1.call-update) | async-done | bytes 1179664 | tf_op jit(solution)/shard_map/all_gather | solution.py:76
  71.5 99.3 %all-gather.16.cloned.1.call-done = bf16[819200]{0:T(1024)(128)(2,1)} async-done(((bf16[25600]{0:T(1024)(128)(2,1)}), bf16[819200]{0:T(1024)(128)(2,1)}) %all-gather.16.cloned.1.call-update) | async-done | bytes 1638416 | tf_op jit(solution)/shard_map/all_gather | solution.py:104
  170.9 1.9 reshape.398
  174.2 2.8 reshape.364
  177.2 2.7 fusion.33
  182.0 1.9 copy-done.31
  185.2 11.1 %reshape.371 = bf16[32,32,3072]{2,1,0:T(8,128)(2,1)} reshape(bf16[32,8,12288]{2,1,0:T(8,128)(2,1)} %all-to-all-done) | data formatting | bytes 12582912 | tf_op jit(solution)/shard_map/reshape | solution.py:113
  196.3 6.2 %fusion.76 = (bf16[32,32,1024]{2,1,0:T(8,128)(2,1)}, bf16[32,32,1024]{2,1,0:T(8,128)(2,1)}, bf16[32,32,1024]{2,1,0:T(8,128)(2,1)S(1)}) fusion(bf16[32,32,3072]{2,1,0:T(8,128)(2,1)} %reshape.371), kind=kLoop, calls=%fused_computation.143 | loop fusion | bytes 12582912 | tf_op jit(solution)/shard_map/slice | solution.py:117
  203.9 1.8 fusion.45
  207.0 25.8 %reduce-scatter.5.cloned.1.call-done = f32[128,1024]{1,0:T(8,128)} async-done(((f32[512,1024]{1,0:T(8,128)}), f32[128,1024]{1,0:T(8,128)}) %reduce-scatter.5.cloned.1.call-update) | async-done | bytes 524304 | tf_op jit(solution)/shard_map/reduce_scatter | solution.py:80
  235.2 21.9 %all-gather.10.cloned.1.call-done = bf16[512,1024]{1,0:T(8,128)(2,1)} async-done(((bf16[128,1024]{1,0:T(8,128)(2,1)}), bf16[512,1024]{1,0:T(8,128)(2,1)}) %all-gather.10.cloned.1.call-update) | async-done | bytes 1048592 | tf_op jit(solution)/shard_map/all_gather | solution.py:76
  257.1 4.7 multiply_convert_fusion.1
  261.8 2.6 fusion.83
  265.4 28.4 %reduce-scatter.7.cloned.1.call-done = f32[128,1024]{1,0:T(8,128)} async-done(((f32[512,1024]{1,0:T(8,128)}), f32[128,1024]{1,0:T(8,128)}) %reduce-scatter.7.cloned.1.call-update) | async-done | bytes 524304 | tf_op jit(solution)/shard_map/reduce_scatter | solution.py:80
  297.7 21.8 %all-gather.12.cloned.1.call-done = bf16[512,1024]{1,0:T(8,128)(2,1)} async-done(((bf16[128,1024]{1,0:T(8,128)(2,1)}), bf16[512,1024]{1,0:T(8,128)(2,1)}) %all-gather.12.cloned.1.call-update) | async-done | bytes 1048592 | tf_op jit(solution)/shard_map/all_gather | solution.py:76
  319.4 4.6 fusion.82
  324.0 2.6 fusion.40
  327.5 28.4 %reduce-scatter.9.cloned.1.call-done = f32[128,1024]{1,0:T(8,128)} async-done(((f32[512,1024]{1,0:T(8,128)}), f32[128,1024]{1,0:T(8,128)}) %reduce-scatter.9.cloned.1.call-update) | async-done | bytes 524304 | tf_op jit(solution)/shard_map/reduce_scatter | solution.py:80
  358.2 4.1 convolution_convert_fusion
  362.4 3.3 concatenate.37
  365.7 4.1 convolution_convert_fusion.1
  369.8 4.5 concatenate.36
  374.3 4.6 pad_maximum_fusion
  378.9 9.2 %all-to-all-start.2 = ((bf16[32,8,8192]{2,1,0:T(8,128)(2,1)}), bf16[32,8,8192]{2,1,0:T(8,128)(2,1)}, u32[]{:S(2)}, u32[]{:S(2)}) async-start(bf16[32,8,8192]{2,1,0:T(8,128)(2,1)} %pad_maximum_fusion), calls=%async_computation.6 | async-start | bytes 8388608 | tf_op jit(solution)/shard_map/all_to_all | solution.py:172
  389.2 1.8 convolution_convert_fusion.4
  391.1 2.7 fusion.84
  395.6 7.4 %fusion.29 = bf16[4,64,512]{2,1,0:T(8,128)(2,1)S(1)} fusion(bf16[512,4,64]{0,2,1:T(8,128)(2,1)S(1)} %bitcast.121, f32[4,512,512]{1,2,0:T(8,128)} %fusion.84, f32[4,512,512]{1,2,0:T(8,128)} %copy-done.31, f32[4,512]{1,0:T(4,128)S(1)} %log.8, pred[512,512]{0,1:T(8,128)(4,1)S(1)} %broadcast_compare_fusion), kind=kOutput, calls=%fused_computation.33 | convolution fusion | flops 145885696 | bytes 9183232 | tf_op jit(solution)/shard_map/shqk,sqhe->skhe/dot_general | solution.py:196
  403.1 8.8 %fusion.79 = (bf16[4,64]{1,0:T(4,128)(2,1)S(1)}, bf16[1,512,4,64]{1,3,2,0:T(8,128)(2,1)S(1)}) fusion(bf16[512,4,64]{0,2,1:T(8,128)(2,1)S(1)} %bitcast.119, f32[4,512,512]{1,2,0:T(8,128)} %fusion.84, f32[4,512]{1,0:T(4,128)S(1)} %log.8, f32[4,512,512]{1,2,0:T(8,128)} %copy-done.31, pred[512,512]{0,1:T(8,128)(4,1)S(1)} %broadcast_compare_fusion), kind=kOutput, calls=%fused_computation.146 | convolution fusion | flops 146016512 | bytes 9183744 | tf_op jit(solution)/shard_map/shqk,skhe->sqhe/dot_general | solution.py:193
  411.9 2.3 convolution_convert_fusion.2
  414.2 1.9 reshape.380
  420.3 2.9 reshape.381
  428.6 2.3 pad.9
  430.8 2.2 copy.74
  433.1 9.6 %all-to-all-done.2 = bf16[32,8,8192]{2,1,0:T(8,128)(2,1)} async-done(((bf16[32,8,8192]{2,1,0:T(8,128)(2,1)}), bf16[32,8,8192]{2,1,0:T(8,128)(2,1)}, u32[]{:S(2)}, u32[]{:S(2)}) %all-to-all-start.2) | async-done | bytes 4194336 | tf_op jit(solution)/shard_map/all_to_all | solution.py:172
  442.6 7.0 %all-to-all-start.1 = ((bf16[32,8,7296]{2,1,0:T(8,128)(2,1)}), bf16[32,8,7296]{2,1,0:T(8,128)(2,1)}, u32[]{:S(2)}, u32[]{:S(2)}) async-start(bf16[32,8,7296]{2,1,0:T(8,128)(2,1)} %bitcast.98), calls=%async_computation.5 | async-start | bytes 7471104 | tf_op jit(solution)/shard_map/all_to_all | solution.py:232
  449.9 2.4 fusion.47
  452.4 2.8 reduce_sum.251
  455.2 39.7 %all-to-all-done.1 = bf16[32,8,7296]{2,1,0:T(8,128)(2,1)} async-done(((bf16[32,8,7296]{2,1,0:T(8,128)(2,1)}), bf16[32,8,7296]{2,1,0:T(8,128)(2,1)}, u32[]{:S(2)}, u32[]{:S(2)}) %all-to-all-start.1) | async-done | bytes 3735584 | tf_op jit(solution)/shard_map/all_to_all | solution.py:232
  494.9 2.6 reduce_sum.250
  497.7 17.5 %all-gather.1 = bf16[495616]{0:T(1024)(128)(2,1)} all-gather(bf16[123904]{0:T(1024)(128)(2,1)S(1)} %pad_maximum_fusion.5), channel_id=3, replica_groups=mesh['rep'=4,'shard'=32] {'rep'}, dimensions={0}, use_global_device_ids=true | all-gather | bytes 1239040 | tf_op jit(solution)/shard_map/all_gather | solution.py:235
  515.2 2.1 reshape.400
  520.4 1.9 broadcast_in_dim_reshape.19
  524.7 3.1 copy.77
  527.9 4.5 broadcast_in_dim_reshape.21
  537.4 1.9 add_bitcast_fusion
  (212 shorter events, 50.5 us)
Async XLA Ops:
  7.2 6.5 %copy-start = (bf16[1,128,1024]{2,1,0:T(8,128)(2,1)S(1)}, bf16[1,128,1024]{2,1,0:T(8,128)(2,1)}, u32[]{:S(2)}) copy-start(bf16[1,128,1024]{2,1,0:T(8,128)(2,1)} %param.16) | copy-start | bytes 786436
  7.2 63.1 %all-gather.8.cloned.1.call-start = ((), (), s32[]{:S(2)}) async-start(), calls=%async_computation.7 | async-start | bytes 1474560 | tf_op jit(solution)/shard_map/all_gather | solution.py:76
  7.9 5.7 %copy-start.18 = (bf16[1,32,1024]{2,1,0:T(8,128)(2,1)S(1)}, bf16[1,32,1024]{2,1,0:T(8,128)(2,1)}, u32[]{:S(2)}) copy-start(bf16[1,32,1024]{2,1,0:T(8,128)(2,1)} %param.14) | copy-start | bytes 196612
  17.2 11.5 %copy-start.15 = (bf16[1,32,3072]{2,1,0:T(8,128)(2,1)S(1)}, bf16[1,32,3072]{2,1,0:T(8,128)(2,1)}, u32[]{:S(2)}) copy-start(bf16[1,32,3072]{2,1,0:T(8,128)(2,1)} %param.13) | copy-start | bytes 589828
  17.2 12.5 %copy-start.23 = (bf16[1,128]{1,0:T(2,128)(2,1)S(1)}, bf16[1,128]{1,0:T(2,128)(2,1)}, u32[]{:S(2)}) copy-start(bf16[1,128]{1,0:T(2,128)(2,1)} %param.19) | copy-start | bytes 772
  17.2 13.3 %copy-start.22 = (bf16[1,6,32]{2,1,0:T(8,128)(2,1)S(1)}, bf16[1,6,32]{2,1,0:T(8,128)(2,1)}, u32[]{:S(2)}) copy-start(bf16[1,6,32]{2,1,0:T(8,128)(2,1)} %param.17) | copy-start | bytes 1156
  17.2 13.4 %copy-start.24 = (bf16[1,2,32]{2,1,0:T(2,128)(2,1)S(1)}, bf16[1,2,32]{2,1,0:T(2,128)(2,1)}, u32[]{:S(2)}) copy-start(bf16[1,2,32]{2,1,0:T(2,128)(2,1)} %param.18) | copy-start | bytes 388
  17.2 168.0 %all-to-all-start = ((bf16[32,8,12288]{2,1,0:T(8,128)(2,1)}), bf16[32,8,12288]{2,1,0:T(8,128)(2,1)}, u32[]{:S(2)}, u32[]{:S(2)}) async-start(bf16[32,8,12288]{2,1,0:T(8,128)(2,1)} %broadcast_in_dim.38), calls=%async_computation | async-start | bytes 12582912 | tf_op jit(solution)/shard_map/all_to_all | solution.py:111
  28.7 142.2 %all-gather.16.cloned.1.call-start = ((), (), s32[]{:S(2)}) async-start(), calls=%async_computation.15 | async-start | bytes 1689600 | tf_op jit(solution)/shard_map/all_gather | solution.py:104
  31.5 201.3 %reduce-scatter.5.cloned.1.call-start = ((), (), s32[]{:S(2)}) async-start(), calls=%async_computation.8 | async-start | bytes 2621440 | tf_op jit(solution)/shard_map/reduce_scatter | solution.py:80
  180.5 1.5 copy-start.13
  180.6 1.3 copy-start.11
  182.0 2.0 copy-start.31
  182.0 3.2 copy-start.20
  202.5 1.4 copy-start.4
  203.9 28.9 %copy-start.5 = (f32[1,128,1024]{2,1,0:T(8,128)S(1)}, f32[1,128,1024]{2,1,0:T(8,128)}, u32[]{:S(2)}) copy-start(f32[1,128,1024]{2,1,0:T(8,128)} %param.10) | copy-start | bytes 1572868
  205.7 51.4 %all-gather.10.cloned.1.call-start = ((), (), s32[]{:S(2)}) async-start(), calls=%async_computation.9 | async-start | bytes 1310720 | tf_op jit(solution)/shard_map/all_gather | solution.py:76
  235.1 58.7 %reduce-scatter.7.cloned.1.call-start = ((), (), s32[]{:S(2)}) async-start(), calls=%async_computation.10 | async-start | bytes 2621440 | tf_op jit(solution)/shard_map/reduce_scatter | solution.py:80
  257.1 4.7 copy-start.8
  261.8 2.6 copy-start.33
  264.4 0.7 copy-start.17
  264.4 0.8 copy-start.16
  264.4 30.9 %copy-start.3 = (f32[1,128,1024]{2,1,0:T(8,128)S(1)}, f32[1,128,1024]{2,1,0:T(8,128)}, u32[]{:S(2)}) copy-start(f32[1,128,1024]{2,1,0:T(8,128)} %param.12) | copy-start | bytes 1572868
  264.5 54.9 %all-gather.12.cloned.1.call-start = ((), (), s32[]{:S(2)}) async-start(), calls=%async_computation.11 | async-start | bytes 1310720 | tf_op jit(solution)/shard_map/all_gather | solution.py:76
  297.4 58.5 %reduce-scatter.9.cloned.1.call-start = ((), (), s32[]{:S(2)}) async-start(), calls=%async_computation.12 | async-start | bytes 2621440 | tf_op jit(solution)/shard_map/reduce_scatter | solution.py:80
  319.4 4.6 copy-start.7
  324.0 2.6 copy-start.34
  326.6 0.7 copy-start.21
  326.7 62.6 %all-gather.14.cloned.1.call-start = ((), (), s32[]{:S(2)}) async-start(), calls=%async_computation.13 | async-start | bytes 1310720 | tf_op jit(solution)/shard_map/all_gather | solution.py:76
  378.9 63.7 %all-to-all-start.2 = ((bf16[32,8,8192]{2,1,0:T(8,128)(2,1)}), bf16[32,8,8192]{2,1,0:T(8,128)(2,1)}, u32[]{:S(2)}, u32[]{:S(2)}) async-start(bf16[32,8,8192]{2,1,0:T(8,128)(2,1)} %pad_maximum_fusion), calls=%async_computation.6 | async-start | bytes 8388608 | tf_op jit(solution)/shard_map/all_to_all | solution.py:172
  391.1 3.4 copy-start.32
  394.5 1.1 copy-start.14
  395.6 16.3 %copy-start.25 = (bf16[1,512,4,64]{1,3,2,0:T(8,128)(2,1)}, bf16[1,512,4,64]{1,3,2,0:T(8,128)(2,1)S(1)}, u32[]{:S(2)}) copy-start(bf16[1,512,4,64]{1,3,2,0:T(8,128)(2,1)S(1)} %get-tuple-element.43) | copy-start | bytes 786436
  395.6 7.5 %copy-start.12 = (bf16[512,256]{0,1:T(8,128)(2,1)S(1)}, bf16[512,256]{0,1:T(8,128)(2,1)}, u32[]{:S(2)}) copy-start(bf16[512,256]{0,1:T(8,128)(2,1)} %copy-done.11) | copy-start | bytes 786436
  403.1 8.8 %copy-start.27 = (bf16[4,64,512]{2,1,0:T(8,128)(2,1)}, bf16[4,64,512]{2,1,0:T(8,128)(2,1)S(1)}, u32[]{:S(2)}) copy-start(bf16[4,64,512]{2,1,0:T(8,128)(2,1)S(1)} %fusion.29) | copy-start | bytes 786436
  403.1 8.8 %copy-start.19 = (bf16[512,1152]{1,0:T(8,128)(2,1)S(1)}, bf16[512,1152]{1,0:T(8,128)(2,1)}, u32[]{:S(2)}) copy-start(bf16[512,1152]{1,0:T(8,128)(2,1)} %all-gather.8.cloned.1.call-done) | copy-start | bytes 3538948
  411.9 2.3 copy-start.29
  416.1 2.9 copy-start.10
  442.6 7.2 %copy-start.9 = (bf16[1024,768]{1,0:T(8,128)(2,1)S(1)}, bf16[1024,768]{1,0:T(8,128)(2,1)}, u32[]{:S(2)}) copy-start(bf16[1024,768]{1,0:T(8,128)(2,1)} %reshape.364) | copy-start | bytes 4718596
  442.6 7.2 %copy-start.26 = (bf16[1,512,4,64]{1,3,2,0:T(8,128)(2,1)S(1)}, bf16[1,512,4,64]{1,3,2,0:T(8,128)(2,1)}, u32[]{:S(2)}) copy-start(bf16[1,512,4,64]{1,3,2,0:T(8,128)(2,1)} %copy-done.25) | copy-start | bytes 786436
  442.6 7.2 %copy-start.28 = (bf16[4,64,512]{2,1,0:T(8,128)(2,1)S(1)}, bf16[4,64,512]{2,1,0:T(8,128)(2,1)}, u32[]{:S(2)}) copy-start(bf16[4,64,512]{2,1,0:T(8,128)(2,1)} %copy-done.27) | copy-start | bytes 786436
  442.6 7.2 %copy-start.30 = (bf16[1,512,4,64]{1,3,2,0:T(8,128)(2,1)S(1)}, bf16[1,512,4,64]{1,3,2,0:T(8,128)(2,1)}, u32[]{:S(2)}) copy-start(bf16[1,512,4,64]{1,3,2,0:T(8,128)(2,1)} %copy-done.29) | copy-start | bytes 786436
  442.6 52.2 %all-to-all-start.1 = ((bf16[32,8,7296]{2,1,0:T(8,128)(2,1)}), bf16[32,8,7296]{2,1,0:T(8,128)(2,1)}, u32[]{:S(2)}, u32[]{:S(2)}) async-start(bf16[32,8,7296]{2,1,0:T(8,128)(2,1)} %bitcast.98), calls=%async_computation.5 | async-start | bytes 7471104 | tf_op jit(solution)/shard_map/all_to_all | solution.py:232
  449.6 87.8 %reduce-scatter.11.cloned.1.call-start = ((), (), s32[]{:S(2)}) async-start(), calls=%async_computation.14 | async-start | bytes 2621440 | tf_op jit(solution)/shard_map/reduce_scatter | solution.py:80
  517.2 6.1 %copy-start.2 = (f32[4,123904]{1,0:T(4,128)}, f32[4,123904]{1,0:T(4,128)S(1)}, u32[]{:S(2)}) copy-start(f32[4,123904]{1,0:T(4,128)S(1)} %reshape.400) | copy-start | bytes 5947396
  527.9 4.5 copy-start.6
  527.9 11.5 %copy-start.1 = (bf16[1,128,1024]{2,1,0:T(8,128)(2,1)S(1)}, bf16[1,128,1024]{2,1,0:T(8,128)(2,1)}, u32[]{:S(2)}) copy-start(bf16[1,128,1024]{2,1,0:T(8,128)(2,1)} %param.16) | copy-start | bytes 786436
Sparse Core Ops, SparseCore 0:
  10.3 59.9 all-gather.7
  73.9 96.8 all-gather.15
  205.8 26.9 reduce-scatter.4
  235.2 21.8 all-gather.9
  264.6 29.1 reduce-scatter.6
  297.5 21.8 all-gather.11
  326.8 29.0 reduce-scatter.8
  358.4 21.8 all-gather.13
  453.0 60.7 reduce-scatter.10

commit v5 on v4

--- a/solution.py
+++ b/solution.py
@@ -96,7 +96,7 @@
     up_piece = pick(w_up[0].reshape(k_rows, parts, reps, ff_piece), r, 2).reshape(k_rows, -1)
     down_piece = pick(w_down[0].reshape(reps, ff_piece, D), r, 0)
     upb_piece = pick(up_bias[0].reshape(reps, ff_piece), r, 0)
-    pieces = (qkv_piece, upb_piece, biases[0], norm_gains[0])
+    pieces = (qkv_piece, out_piece, up_piece, down_piece, upb_piece, biases[0], norm_gains[0])
     sizes = [piece.size for piece in pieces]
     offsets = [sum(sizes[:i]) for i in range(len(sizes) + 1)]
     packed = jnp.concatenate([piece.reshape(-1) for piece in pieces])
@@ -104,17 +104,13 @@
     gathered = lax.all_gather(packed, "shard", axis=0, tiled=False)
     got = [gathered[:, offsets[i] : offsets[i + 1]] for i in range(len(sizes))]
     w_qkv_r = got[0].reshape(D, 3 * head_cols)
-    up_bias_r = got[1].reshape(-1)
-    bias_all = unpack_cols(got[2], parts, biases.shape[1])
-    gain_all = unpack_cols(got[3], parts, norm_gains.shape[1])
-    big = jnp.concatenate([out_piece, up_piece, down_piece], axis=1).reshape(8, -1)
-    big_all = lax.all_to_all(
-        jnp.broadcast_to(big[None], (parts,) + big.shape), "shard", 0, 0, tiled=True
-    ).reshape(parts, k_rows, -1)
-    w_out_all = big_all[:, :, :D].reshape(D, D)
+    w_out_all = got[1].reshape(D, D)
     w_out_r = lax.dynamic_slice_in_dim(w_out_all, r * head_cols, head_cols, axis=0)
-    w_up_r = big_all[:, :, D : D + up_piece.shape[1]].reshape(D, -1)
-    w_down_r = big_all[:, :, D + up_piece.shape[1] :].reshape(-1, D)
+    w_up_r = got[2].reshape(D, -1)
+    w_down_r = got[3].reshape(-1, D)
+    up_bias_r = got[4].reshape(-1)
+    bias_all = unpack_cols(got[5], parts, biases.shape[1])
+    gain_all = unpack_cols(got[6], parts, norm_gains.shape[1])
     bias_q = lax.dynamic_slice_in_dim(bias_all[0], r * head_cols, head_cols)
     bias_v = lax.dynamic_slice_in_dim(bias_all[1], r * head_cols, head_cols)
 

time: 552 us -> 522 us (0.946)
  waiting for transfers between devices: 314 us -> 292 us
  starting transfers between devices: 28.6 us -> 16.9 us
    all_gather x4, waiting for transfers between devices: 82.2 us -> 54.7 us  [gather_rep(): return lax.all_gather(tensor, 'rep', axis=0, tiled=True)]
    all_to_all x1 -> x0, starting transfers between devices: 11.4 us -> none  [local(): lax.all_to_all(jnp.broadcast_to(big[None], (parts,) + big.shape), 'shard'...]
    all_gather x1, local copies, waits for them, and re-layouts: 1.86 us -> 8.33 us  [local(): gathered = lax.all_gather(packed, 'shard', axis=0, tiled=False)]
    slice x1 -> x0, local copies, waits for them, and re-layouts: 6.18 us -> none  [local(): w_down_r = big_all[:, :, D + up_piece.shape[1]:].reshape(-1, D)]
    slice x3 -> x5, local copies, waits for them, and re-layouts: 1.45 us -> 7.3 us  [local(): got = [gathered[:, offsets[i]:offsets[i + 1]] for i in range(len(sizes))]]
    reshape x2 -> x3, local copies, waits for them, and re-layouts: 11.4 us -> 9.04 us  [the longest x1 4.32 us: local(): w_up_r = got[2].reshape(D, -1)]
    unnamed x82 -> x83, local copies, waits for them, and re-layouts: 12.7 us -> 11.9 us
  transfers between devices with their start and end apart: 12 -> 11, of which waited for: 9 -> 9; matrix products, arithmetic and copies ran while one was open for 22% -> 22% of each run, Pallas kernels for 0% -> 0%
where the time goes in v5:
time: 522 us; the launch traced here: 513 us
  waiting for transfers between devices  292 us (56%)
  local copies, waits for them, and re-layouts  84 us (16%)
  matrix products  58.5 us (11%)
  other arithmetic  28.9 us (6%)
  blocking collectives  17.7 us (3%)
  starting transfers between devices  16.9 us (3%)
  between operations  15 us (3%)
    all_gather x1, waiting for transfers between devices, local(): gathered = lax.all_gather(packed, 'shard', axis=0, tiled=False)  104 us
    reduce_scatter x4, waiting for transfers between devices, scatter_rep(): return lax.psum_scatter(tensor, 'rep', scatter_dimension=0, tiled=True)  83.3 us
    all_gather x4, waiting for transfers between devices, gather_rep(): return lax.all_gather(tensor, 'rep', axis=0, tiled=True)  54.7 us
    all_to_all x1, waiting for transfers between devices, local(): received = lax.all_to_all(grad_pack, 'shard', 0, 0, tiled=True)  39.6 us
    all_gather x1, blocking collectives, local(): lax.all_gather(all_shares, 'rep', axis=0, tiled=False).astype(jnp.float32)  17.7 us
    dot_general x4, matrix products, matmul(): return jnp.dot(first_op, second_op, preferred_element_type=jnp.float32)  12.3 us
    dot_general x4, matrix products, matmul_lt(): lax.dot_general(first_op, second_op, (((0,), (0,)), ((), ())), preferred_...  12 us
    unnamed x83, local copies, waits for them, and re-layouts  11.9 us
  transfers between devices with their start and end apart: 11, of which 9 were waited for; matrix products, arithmetic and copies ran while one was open for 22% of the time, Pallas kernels for 0%

profile of v5, /device:TPU:1, one launch (start us, length us, event | category | flops | bytes accessed | tf_op | source)
XLA Modules:
  0.0 513.0 jit_solution(16374503692966600030)
XLA Ops:
  12.3 1.7 dynamic-slice_reduce_fusion
  17.1 18.4 %all-gather.8.cloned.1.call-done = bf16[512,1152]{1,0:T(8,128)(2,1)} async-done(((bf16[128,1152]{1,0:T(8,128)(2,1)}), bf16[512,1152]{1,0:T(8,128)(2,1)}) %all-gather.8.cloned.1.call-update) | async-done | bytes 1179664 | tf_op jit(solution)/shard_map/all_gather | solution.py:76
  37.5 104.4 %all-gather.16.cloned.1.call-done = bf16[3964928]{0:T(1024)(128)(2,1)} async-done(((bf16[123904]{0:T(1024)(128)(2,1)}), bf16[3964928]{0:T(1024)(128)(2,1)}) %all-gather.16.cloned.1.call-update) | async-done | bytes 7929872 | tf_op jit(solution)/shard_map/all_gather | solution.py:104
  141.9 8.3 %reshape.394 = bf16[32,123904]{1,0:T(8,128)(2,1)} reshape(bf16[3964928]{0:T(1024)(128)(2,1)} %all-gather.16.cloned.1.call-done) | data formatting | bytes 15859712 | tf_op jit(solution)/shard_map/all_gather | solution.py:104
  151.1 5.7 %fusion.76 = (bf16[32,32768]{1,0:T(8,128)(2,1)}, bf16[32,32768]{1,0:T(8,128)(2,1)}, bf16[32,32768]{1,0:T(8,128)(2,1)}) fusion(bf16[32,123904]{1,0:T(8,128)(2,1)} %reshape.394), kind=kLoop, calls=%fused_computation.142 | loop fusion | bytes 12582912 | tf_op jit(solution)/shard_map/slice | solution.py:105
  158.8 2.2 fusion.33
  162.8 2.4 reshape.368
  168.5 3.0 fusion.45
  172.9 25.4 %reduce-scatter.5.cloned.1.call-done = f32[128,1024]{1,0:T(8,128)} async-done(((f32[512,1024]{1,0:T(8,128)}), f32[128,1024]{1,0:T(8,128)}) %reduce-scatter.5.cloned.1.call-update) | async-done | bytes 524304 | tf_op jit(solution)/shard_map/reduce_scatter | solution.py:80
  201.6 4.3 reshape.370
  206.0 2.4 reshape.371
  208.3 14.3 %all-gather.10.cloned.1.call-done = bf16[512,1024]{1,0:T(8,128)(2,1)} async-done(((bf16[128,1024]{1,0:T(8,128)(2,1)}), bf16[512,1024]{1,0:T(8,128)(2,1)}) %all-gather.10.cloned.1.call-update) | async-done | bytes 1048592 | tf_op jit(solution)/shard_map/all_gather | solution.py:76
  222.7 4.6 multiply_convert_fusion.1
  228.2 2.6 fusion.83
  231.1 29.0 %reduce-scatter.7.cloned.1.call-done = f32[128,1024]{1,0:T(8,128)} async-done(((f32[512,1024]{1,0:T(8,128)}), f32[128,1024]{1,0:T(8,128)}) %reduce-scatter.7.cloned.1.call-update) | async-done | bytes 524304 | tf_op jit(solution)/shard_map/reduce_scatter | solution.py:80
  263.7 22.0 %all-gather.12.cloned.1.call-done = bf16[512,1024]{1,0:T(8,128)(2,1)} async-done(((bf16[128,1024]{1,0:T(8,128)(2,1)}), bf16[512,1024]{1,0:T(8,128)(2,1)}) %all-gather.12.cloned.1.call-update) | async-done | bytes 1048592 | tf_op jit(solution)/shard_map/all_gather | solution.py:76
  285.7 4.6 fusion.82
  290.3 2.7 fusion.40
  293.4 28.9 %reduce-scatter.9.cloned.1.call-done = f32[128,1024]{1,0:T(8,128)} async-done(((f32[512,1024]{1,0:T(8,128)}), f32[128,1024]{1,0:T(8,128)}) %reduce-scatter.9.cloned.1.call-update) | async-done | bytes 524304 | tf_op jit(solution)/shard_map/reduce_scatter | solution.py:80
  324.6 4.2 convolution_convert_fusion
  328.9 3.3 concatenate.33
  332.2 4.2 convolution_convert_fusion.1
  336.4 4.5 concatenate.32
  340.9 4.6 pad_maximum_fusion
  345.5 9.2 %all-to-all-start.1 = ((bf16[32,8,8192]{2,1,0:T(8,128)(2,1)}), bf16[32,8,8192]{2,1,0:T(8,128)(2,1)}, u32[]{:S(2)}, u32[]{:S(2)}) async-start(bf16[32,8,8192]{2,1,0:T(8,128)(2,1)} %pad_maximum_fusion), calls=%async_computation.5 | async-start | bytes 8388608 | tf_op jit(solution)/shard_map/all_to_all | solution.py:168
  355.6 1.8 convolution_convert_fusion.4
  357.5 2.7 fusion.84
  362.0 7.5 %fusion.29 = bf16[4,64,512]{2,1,0:T(8,128)(2,1)S(1)} fusion(bf16[512,4,64]{0,2,1:T(8,128)(2,1)S(1)} %bitcast.116, f32[4,512,512]{1,2,0:T(8,128)} %fusion.84, f32[4,512,512]{1,2,0:T(8,128)} %copy-done.30, f32[4,512]{1,0:T(4,128)S(1)} %log.8, pred[512,512]{0,1:T(8,128)(4,1)S(1)} %copy-done.14), kind=kOutput, calls=%fused_computation.33 | convolution fusion | flops 145885696 | bytes 9183232 | tf_op jit(solution)/shard_map/shqk,sqhe->skhe/dot_general | solution.py:192
  369.5 8.8 %fusion.79 = (bf16[4,64]{1,0:T(4,128)(2,1)S(1)}, bf16[1,512,4,64]{1,3,2,0:T(8,128)(2,1)S(1)}) fusion(bf16[512,4,64]{0,2,1:T(8,128)(2,1)S(1)} %bitcast.114, f32[4,512,512]{1,2,0:T(8,128)} %fusion.84, f32[4,512]{1,0:T(4,128)S(1)} %log.8, f32[4,512,512]{1,2,0:T(8,128)} %copy-done.30, pred[512,512]{0,1:T(8,128)(4,1)S(1)} %copy-done.14), kind=kOutput, calls=%fused_computation.145 | convolution fusion | flops 146016512 | bytes 9183744 | tf_op jit(solution)/shard_map/shqk,skhe->sqhe/dot_general | solution.py:189
  378.4 2.2 convolution_convert_fusion.2
  380.5 1.9 reshape.376
  383.7 1.7 broadcast_in_dim.35
  386.6 2.9 reshape.377
  390.1 1.5 constant_dynamic-update-slice_fusion.7
  395.0 2.3 pad.9
  397.2 2.2 copy.76
  399.5 9.8 %all-to-all-done.1 = bf16[32,8,8192]{2,1,0:T(8,128)(2,1)} async-done(((bf16[32,8,8192]{2,1,0:T(8,128)(2,1)}), bf16[32,8,8192]{2,1,0:T(8,128)(2,1)}, u32[]{:S(2)}, u32[]{:S(2)}) %all-to-all-start.1) | async-done | bytes 4194336 | tf_op jit(solution)/shard_map/all_to_all | solution.py:168
  409.2 6.9 %all-to-all-start = ((bf16[32,8,7296]{2,1,0:T(8,128)(2,1)}), bf16[32,8,7296]{2,1,0:T(8,128)(2,1)}, u32[]{:S(2)}, u32[]{:S(2)}) async-start(bf16[32,8,7296]{2,1,0:T(8,128)(2,1)} %bitcast.97), calls=%async_computation.4 | async-start | bytes 7471104 | tf_op jit(solution)/shard_map/all_to_all | solution.py:228
  416.5 2.5 fusion.47
  419.0 2.8 reduce_sum.251
  421.8 39.6 %all-to-all-done = bf16[32,8,7296]{2,1,0:T(8,128)(2,1)} async-done(((bf16[32,8,7296]{2,1,0:T(8,128)(2,1)}), bf16[32,8,7296]{2,1,0:T(8,128)(2,1)}, u32[]{:S(2)}, u32[]{:S(2)}) %all-to-all-start) | async-done | bytes 3735584 | tf_op jit(solution)/shard_map/all_to_all | solution.py:228
  461.4 2.6 reduce_sum.250
  464.2 17.7 %all-gather.1 = bf16[495616]{0:T(1024)(128)(2,1)} all-gather(bf16[123904]{0:T(1024)(128)(2,1)S(1)} %pad_maximum_fusion.5), channel_id=3, replica_groups=mesh['rep'=4,'shard'=32] {'rep'}, dimensions={0}, use_global_device_ids=true | all-gather | bytes 1239040 | tf_op jit(solution)/shard_map/all_gather | solution.py:231
  481.9 2.1 reshape.396
  487.2 1.9 broadcast_in_dim_reshape.18
  491.5 3.1 copy.79
  494.6 4.5 broadcast_in_dim_reshape.20
  504.2 1.9 add_bitcast_fusion
  (210 shorter events, 50.3 us)
Async XLA Ops:
  7.2 7.0 %copy-start = (bf16[1,128,1024]{2,1,0:T(8,128)(2,1)S(1)}, bf16[1,128,1024]{2,1,0:T(8,128)(2,1)}, u32[]{:S(2)}) copy-start(bf16[1,128,1024]{2,1,0:T(8,128)(2,1)} %param.16) | copy-start | bytes 786436
  7.2 4.2 copy-start.19
  7.2 4.3 copy-start.13
  7.2 28.4 %all-gather.8.cloned.1.call-start = ((), (), s32[]{:S(2)}) async-start(), calls=%async_computation.6 | async-start | bytes 1474560 | tf_op jit(solution)/shard_map/all_gather | solution.py:76
  9.1 5.6 %copy-start.22 = (bf16[1,128]{1,0:T(2,128)(2,1)S(1)}, bf16[1,128]{1,0:T(2,128)(2,1)}, u32[]{:S(2)}) copy-start(bf16[1,128]{1,0:T(2,128)(2,1)} %param.19) | copy-start | bytes 772
  9.1 6.4 %copy-start.21 = (bf16[1,6,32]{2,1,0:T(8,128)(2,1)S(1)}, bf16[1,6,32]{2,1,0:T(8,128)(2,1)}, u32[]{:S(2)}) copy-start(bf16[1,6,32]{2,1,0:T(8,128)(2,1)} %param.17) | copy-start | bytes 1156
  9.2 6.4 %copy-start.23 = (bf16[1,2,32]{2,1,0:T(2,128)(2,1)S(1)}, bf16[1,2,32]{2,1,0:T(2,128)(2,1)}, u32[]{:S(2)}) copy-start(bf16[1,2,32]{2,1,0:T(2,128)(2,1)} %param.18) | copy-start | bytes 388
  9.9 132.0 %all-gather.16.cloned.1.call-start = ((), (), s32[]{:S(2)}) async-start(), calls=%async_computation.14 | async-start | bytes 8177664 | tf_op jit(solution)/shard_map/all_gather | solution.py:104
  17.1 181.2 %reduce-scatter.5.cloned.1.call-start = ((), (), s32[]{:S(2)}) async-start(), calls=%async_computation.7 | async-start | bytes 2621440 | tf_op jit(solution)/shard_map/reduce_scatter | solution.py:80
  151.1 5.8 %slice-start = ((bf16[32,123904]{1,0:T(8,128)(2,1)}), bf16[32,24576]{1,0:T(8,128)(2,1)S(1)}, s32[]{:S(2)}) async-start(bf16[32,123904]{1,0:T(8,128)(2,1)} %reshape.394), calls=%async_computation.15 | async-start | bytes 3145728 | tf_op jit(solution)/shard_map/slice | solution.py:105
  157.7 1.2 copy-start.10
  161.0 1.7 copy-start.3
  161.6 3.6 copy-start.17
  161.7 3.4 copy-start.15
  162.8 2.4 copy-start.14
  166.5 2.0 copy-start.30
  168.5 29.9 %copy-start.8 = (f32[1,128,1024]{2,1,0:T(8,128)S(1)}, f32[1,128,1024]{2,1,0:T(8,128)}, u32[]{:S(2)}) copy-start(f32[1,128,1024]{2,1,0:T(8,128)} %param.10) | copy-start | bytes 1572868
  171.5 51.2 %all-gather.10.cloned.1.call-start = ((), (), s32[]{:S(2)}) async-start(), calls=%async_computation.8 | async-start | bytes 1310720 | tf_op jit(solution)/shard_map/all_gather | solution.py:76
  200.6 59.4 %reduce-scatter.7.cloned.1.call-start = ((), (), s32[]{:S(2)}) async-start(), calls=%async_computation.9 | async-start | bytes 2621440 | tf_op jit(solution)/shard_map/reduce_scatter | solution.py:80
  201.6 4.3 copy-start.2
  208.3 19.9 %copy-start.7 = (bf16[1024,1024]{1,0:T(8,128)(2,1)S(1)}, bf16[1024,1024]{1,0:T(8,128)(2,1)}, u32[]{:S(2)}) copy-start(bf16[1024,1024]{1,0:T(8,128)(2,1)} %reshape.371) | copy-start | bytes 6291460
  227.3 1.0 copy-start.32
  230.8 30.8 %copy-start.5 = (f32[1,128,1024]{2,1,0:T(8,128)S(1)}, f32[1,128,1024]{2,1,0:T(8,128)}, u32[]{:S(2)}) copy-start(f32[1,128,1024]{2,1,0:T(8,128)} %param.12) | copy-start | bytes 1572868
  230.8 54.9 %all-gather.12.cloned.1.call-start = ((), (), s32[]{:S(2)}) async-start(), calls=%async_computation.10 | async-start | bytes 1310720 | tf_op jit(solution)/shard_map/all_gather | solution.py:76
  263.7 58.6 %reduce-scatter.9.cloned.1.call-start = ((), (), s32[]{:S(2)}) async-start(), calls=%async_computation.11 | async-start | bytes 2621440 | tf_op jit(solution)/shard_map/reduce_scatter | solution.py:80
  285.7 4.6 copy-start.6
  290.3 2.7 copy-start.33
  293.0 62.6 %all-gather.14.cloned.1.call-start = ((), (), s32[]{:S(2)}) async-start(), calls=%async_computation.12 | async-start | bytes 1310720 | tf_op jit(solution)/shard_map/all_gather | solution.py:76
  345.5 63.7 %all-to-all-start.1 = ((bf16[32,8,8192]{2,1,0:T(8,128)(2,1)}), bf16[32,8,8192]{2,1,0:T(8,128)(2,1)}, u32[]{:S(2)}, u32[]{:S(2)}) async-start(bf16[32,8,8192]{2,1,0:T(8,128)(2,1)} %pad_maximum_fusion), calls=%async_computation.5 | async-start | bytes 8388608 | tf_op jit(solution)/shard_map/all_to_all | solution.py:168
  357.5 3.4 copy-start.31
  360.9 1.1 copy-start.18
  362.0 16.3 %copy-start.24 = (bf16[1,512,4,64]{1,3,2,0:T(8,128)(2,1)}, bf16[1,512,4,64]{1,3,2,0:T(8,128)(2,1)S(1)}, u32[]{:S(2)}) copy-start(bf16[1,512,4,64]{1,3,2,0:T(8,128)(2,1)S(1)} %get-tuple-element.43) | copy-start | bytes 786436
  362.0 7.5 %copy-start.16 = (bf16[512,256]{0,1:T(8,128)(2,1)S(1)}, bf16[512,256]{0,1:T(8,128)(2,1)}, u32[]{:S(2)}) copy-start(bf16[512,256]{0,1:T(8,128)(2,1)} %copy-done.15) | copy-start | bytes 786436
  369.5 8.9 %copy-start.26 = (bf16[4,64,512]{2,1,0:T(8,128)(2,1)}, bf16[4,64,512]{2,1,0:T(8,128)(2,1)S(1)}, u32[]{:S(2)}) copy-start(bf16[4,64,512]{2,1,0:T(8,128)(2,1)S(1)} %fusion.29) | copy-start | bytes 786436
  369.5 8.9 %copy-start.20 = (bf16[512,1152]{1,0:T(8,128)(2,1)S(1)}, bf16[512,1152]{1,0:T(8,128)(2,1)}, u32[]{:S(2)}) copy-start(bf16[512,1152]{1,0:T(8,128)(2,1)} %all-gather.8.cloned.1.call-done) | copy-start | bytes 3538948
  378.3 2.2 copy-start.28
  382.4 2.9 copy-start.12
  409.2 7.2 %copy-start.11 = (bf16[1024,768]{1,0:T(8,128)(2,1)S(1)}, bf16[1024,768]{1,0:T(8,128)(2,1)}, u32[]{:S(2)}) copy-start(bf16[1024,768]{1,0:T(8,128)(2,1)} %copy-done.10) | copy-start | bytes 4718596
  409.2 7.2 %copy-start.25 = (bf16[1,512,4,64]{1,3,2,0:T(8,128)(2,1)S(1)}, bf16[1,512,4,64]{1,3,2,0:T(8,128)(2,1)}, u32[]{:S(2)}) copy-start(bf16[1,512,4,64]{1,3,2,0:T(8,128)(2,1)} %copy-done.24) | copy-start | bytes 786436
  409.2 7.2 %copy-start.27 = (bf16[4,64,512]{2,1,0:T(8,128)(2,1)S(1)}, bf16[4,64,512]{2,1,0:T(8,128)(2,1)}, u32[]{:S(2)}) copy-start(bf16[4,64,512]{2,1,0:T(8,128)(2,1)} %copy-done.26) | copy-start | bytes 786436
  409.2 7.3 %copy-start.29 = (bf16[1,512,4,64]{1,3,2,0:T(8,128)(2,1)S(1)}, bf16[1,512,4,64]{1,3,2,0:T(8,128)(2,1)}, u32[]{:S(2)}) copy-start(bf16[1,512,4,64]{1,3,2,0:T(8,128)(2,1)} %copy-done.28) | copy-start | bytes 786436
  409.2 52.1 %all-to-all-start = ((bf16[32,8,7296]{2,1,0:T(8,128)(2,1)}), bf16[32,8,7296]{2,1,0:T(8,128)(2,1)}, u32[]{:S(2)}, u32[]{:S(2)}) async-start(bf16[32,8,7296]{2,1,0:T(8,128)(2,1)} %bitcast.97), calls=%async_computation.4 | async-start | bytes 7471104 | tf_op jit(solution)/shard_map/all_to_all | solution.py:228
  416.1 88.0 %reduce-scatter.11.cloned.1.call-start = ((), (), s32[]{:S(2)}) async-start(), calls=%async_computation.13 | async-start | bytes 2621440 | tf_op jit(solution)/shard_map/reduce_scatter | solution.py:80
  484.0 6.1 %copy-start.4 = (f32[4,123904]{1,0:T(4,128)}, f32[4,123904]{1,0:T(4,128)S(1)}, u32[]{:S(2)}) copy-start(f32[4,123904]{1,0:T(4,128)S(1)} %reshape.396) | copy-start | bytes 5947396
  494.6 4.5 copy-start.9
  494.6 11.5 %copy-start.1 = (bf16[1,128,1024]{2,1,0:T(8,128)(2,1)S(1)}, bf16[1,128,1024]{2,1,0:T(8,128)(2,1)}, u32[]{:S(2)}) copy-start(bf16[1,128,1024]{2,1,0:T(8,128)(2,1)} %param.16) | copy-start | bytes 786436
Sparse Core Ops, SparseCore 0:
  10.3 25.2 all-gather.7
  39.3 102.5 all-gather.15
  171.6 26.7 reduce-scatter.4
  200.8 21.8 all-gather.9
  230.9 29.0 reduce-scatter.6
  263.8 21.8 all-gather.11
  293.2 29.0 reduce-scatter.8
  324.7 21.8 all-gather.13
  419.5 60.8 reduce-scatter.10

commit v6 on v5

--- a/solution.py
+++ b/solution.py
@@ -3,6 +3,8 @@
 import jax
 import jax.numpy as jnp
 from jax import lax
+from jax.experimental import pallas as pl
+from jax.experimental.pallas import tpu as pltpu
 from jax.sharding import PartitionSpec as P
 
 D = 1024
@@ -72,8 +74,44 @@
     return flat.reshape(parts, rows, -1).transpose(1, 0, 2).reshape(rows, -1)
 
 
-def gather_rep(tensor):
-    return lax.all_gather(tensor, "rep", axis=0, tiled=True)
+def rep_gather_kernel(x_ref, o_ref, send_sem, recv_sem):
+    n = lax.axis_size("rep")
+    me = lax.axis_index("rep")
+    rows = x_ref.shape[0]
+    o_ref[pl.ds(me * rows, rows), :] = x_ref[...]
+    barrier = pltpu.get_barrier_semaphore()
+    for k in range(1, n):
+        pl.semaphore_signal(
+            barrier, inc=1, device_id={"rep": lax.rem(me + k, n)}, device_id_type=pl.DeviceIdType.MESH
+        )
+    pl.semaphore_wait(barrier, n - 1)
+    copies = []
+    for k in range(1, n):
+        copy = pltpu.make_async_remote_copy(
+            src_ref=x_ref,
+            dst_ref=o_ref.at[pl.ds(me * rows, rows)],
+            send_sem=send_sem.at[k - 1],
+            recv_sem=recv_sem.at[k - 1],
+            device_id={"rep": lax.rem(me + k, n)},
+            device_id_type=pl.DeviceIdType.MESH,
+        )
+        copy.start()
+        copies.append(copy)
+    for copy in copies:
+        copy.wait()
+
+
+def gather_rep(tensor, cid=1):
+    n = lax.axis_size("rep")
+    rows, cols = tensor.shape
+    return pl.pallas_call(
+        rep_gather_kernel,
+        out_shape=jax.ShapeDtypeStruct((n * rows, cols), tensor.dtype),
+        in_specs=[pl.BlockSpec(memory_space=pltpu.VMEM)],
+        out_specs=pl.BlockSpec(memory_space=pltpu.VMEM),
+        scratch_shapes=[pltpu.SemaphoreType.DMA((n - 1,)), pltpu.SemaphoreType.DMA((n - 1,))],
+        compiler_params=pltpu.CompilerParams(collective_id=cid, has_side_effects=True),
+    )(tensor)
 
 
 def scatter_rep(tensor):
@@ -118,7 +156,7 @@
     own = rows_f32.shape[0]
     rows_bf = rows_f32.astype(jnp.bfloat16)
     seg_tag = jnp.broadcast_to(segment_ids[0].astype(jnp.bfloat16)[:, None], (own, 128))
-    hb_seg = gather_rep(jnp.concatenate([rows_bf, seg_tag], axis=1))
+    hb_seg = gather_rep(jnp.concatenate([rows_bf, seg_tag], axis=1), cid=0)
     hb_all = hb_seg[:, :D]
     seg_all = hb_seg[:, D]
     qkv_rows = matmul(hb_all, w_qkv_r)

time: 522 us -> 523 us (level)
  waiting for transfers between devices: 292 us -> 179 us
  Pallas kernels: 0 us -> 106 us
  blocking collectives: 17.7 us -> 10.3 us
  local copies, waits for them, and re-layouts: 84 us -> 91.2 us
  starting transfers between devices: 16.9 us -> 22.3 us
    pallas_call x0 -> x4, Pallas kernels: none -> 106 us  [gather_rep(): pl.pallas_call(rep_gather_kernel, out_shape=jax.ShapeDtypeStruct((n * row...]
    all_gather x4 -> x0, waiting for transfers between devices: 54.7 us -> none  [gather_rep(): return lax.all_gather(tensor, 'rep', axis=0, tiled=True)]
    reduce_scatter x4, waiting for transfers between devices: 83.3 us -> 46.6 us  [scatter_rep(): return lax.psum_scatter(tensor, 'rep', scatter_dimension=0, tiled=True)]
    all_gather x1, waiting for transfers between devices: 104 us -> 82.7 us  [local(): gathered = lax.all_gather(packed, 'shard', axis=0, tiled=False)]
    all_to_all x1, waiting for transfers between devices: 9.76 us -> 0.01 us  [local(): ffn_recv = lax.all_to_all(ffn_pack, 'shard', 0, 0, tiled=True)]
    all_to_all x1, waiting for transfers between devices: 39.6 us -> 49.2 us  [local(): received = lax.all_to_all(grad_pack, 'shard', 0, 0, tiled=True)]
    all_gather x1, blocking collectives: 17.7 us -> 10.3 us  [local(): lax.all_gather(all_shares, 'rep', axis=0, tiled=False).astype(jnp.float32)]
    all_to_all x1, starting transfers between devices: 6.91 us -> 12.7 us  [local(): received = lax.all_to_all(grad_pack, 'shard', 0, 0, tiled=True)]
  transfers between devices with their start and end apart: 11 -> 7, of which waited for: 9 -> 4; matrix products, arithmetic and copies ran while one was open for 22% -> 21% of each run, Pallas kernels for 0% -> 14%
where the time goes in v6:
time: 523 us; the launch traced here: 514 us
  waiting for transfers between devices  179 us (34%)
  Pallas kernels  106 us (20%)
  local copies, waits for them, and re-layouts  91.2 us (17%)
  matrix products  61.3 us (12%)
  other arithmetic  29.2 us (6%)
  starting transfers between devices  22.3 us (4%)
  between operations  14.9 us (3%)
  blocking collectives  10.3 us (2%)
    pallas_call x4, Pallas kernels, gather_rep(): pl.pallas_call(rep_gather_kernel, out_shape=jax.ShapeDtypeStruct((n * row...  106 us
    all_gather x1, waiting for transfers between devices, local(): gathered = lax.all_gather(packed, 'shard', axis=0, tiled=False)  82.7 us
    all_to_all x1, waiting for transfers between devices, local(): received = lax.all_to_all(grad_pack, 'shard', 0, 0, tiled=True)  49.2 us
    reduce_scatter x4, waiting for transfers between devices, scatter_rep(): return lax.psum_scatter(tensor, 'rep', scatter_dimension=0, tiled=True)  46.6 us
    unnamed x83, local copies, waits for them, and re-layouts  14.7 us
    dot_general x4, matrix products, matmul(): return jnp.dot(first_op, second_op, preferred_element_type=jnp.float32)  13.4 us
    all_to_all x1, starting transfers between devices, local(): received = lax.all_to_all(grad_pack, 'shard', 0, 0, tiled=True)  12.7 us
    dot_general x4, matrix products, matmul_lt(): lax.dot_general(first_op, second_op, (((0,), (0,)), ((), ())), preferred_...  11.7 us
  transfers between devices with their start and end apart: 7, of which 4 were waited for; matrix products, arithmetic and copies ran while one was open for 21% of the time, Pallas kernels for 14%

profile of v6, /device:TPU:1, one launch (start us, length us, event | category | flops | bytes accessed | tf_op | source)
XLA Modules:
  0.0 513.6 jit_solution(8179076707825323648)
XLA Ops:
  9.7 1.7 reshape_squeeze.23
  11.4 1.7 dynamic-slice_reduce_fusion
  17.1 20.9 %shard_map.169 = bf16[512,1152]{1,0:T(8,128)(2,1)} custom-call(bf16[128,1152]{1,0:T(8,128)(2,1)} %pad_maximum_fusion.4.x_ref), custom_call_target="tpu_custom_call" | custom-call | tf_op jit(solution)/shard_map/pallas_call | solution.py:107
  40.1 82.7 %all-gather.4.cloned.1.call-done = bf16[3964928]{0:T(1024)(128)(2,1)} async-done(((bf16[123904]{0:T(1024)(128)(2,1)}), bf16[3964928]{0:T(1024)(128)(2,1)}) %all-gather.4.cloned.1.call-update) | async-done | bytes 7929872 | tf_op jit(solution)/shard_map/all_gather | solution.py:142
  122.7 8.3 %reshape.394 = bf16[32,123904]{1,0:T(8,128)(2,1)} reshape(bf16[3964928]{0:T(1024)(128)(2,1)} %all-gather.4.cloned.1.call-done) | data formatting | bytes 15859712 | tf_op jit(solution)/shard_map/all_gather | solution.py:142
  131.9 5.7 %fusion.76 = (bf16[32,32768]{1,0:T(8,128)(2,1)}, bf16[32,32768]{1,0:T(8,128)(2,1)}, bf16[32,32768]{1,0:T(8,128)(2,1)}) fusion(bf16[32,123904]{1,0:T(8,128)(2,1)} %reshape.394), kind=kLoop, calls=%fused_computation.142 | loop fusion | bytes 12582912 | tf_op jit(solution)/shard_map/slice | solution.py:143
  139.4 3.9 fusion.33
  144.8 2.0 fusion.35
  148.9 2.4 reshape.368
  151.3 2.3 fusion.2
  156.4 2.9 fusion.45
  161.7 4.4 reshape.370
  166.0 2.3 reshape.371
  168.4 17.7 %reduce-scatter.5.cloned.1.call-done = f32[128,1024]{1,0:T(8,128)} async-done(((f32[512,1024]{1,0:T(8,128)}), f32[128,1024]{1,0:T(8,128)}) %reduce-scatter.5.cloned.1.call-update) | async-done | bytes 524304 | tf_op jit(solution)/shard_map/reduce_scatter | solution.py:118
  188.4 16.0 %shard_map.170 = bf16[512,1024]{1,0:T(8,128)(2,1)} custom-call(bf16[128,1024]{1,0:T(8,128)(2,1)} %fusion.42.x_ref), custom_call_target="tpu_custom_call" | custom-call | tf_op jit(solution)/shard_map/pallas_call | solution.py:107
  204.4 4.1 multiply_convert_fusion.1
  209.5 2.6 fusion.83
  212.3 28.9 %reduce-scatter.7.cloned.1.call-done = f32[128,1024]{1,0:T(8,128)} async-done(((f32[512,1024]{1,0:T(8,128)}), f32[128,1024]{1,0:T(8,128)}) %reduce-scatter.7.cloned.1.call-update) | async-done | bytes 524304 | tf_op jit(solution)/shard_map/reduce_scatter | solution.py:118
  244.8 15.9 %shard_map.171 = bf16[512,1024]{1,0:T(8,128)(2,1)} custom-call(bf16[128,1024]{1,0:T(8,128)(2,1)} %convert_element_type.195.x_ref), custom_call_target="tpu_custom_call" | custom-call | tf_op jit(solution)/shard_map/pallas_call | solution.py:107
  260.8 4.6 fusion.82
  266.4 2.6 fusion.40
  270.2 3.8 convolution_convert_fusion
  274.1 3.3 concatenate.33
  277.4 4.4 convolution_convert_fusion.1
  281.8 4.5 concatenate.32
  286.3 4.6 pad_maximum_fusion
  290.8 9.0 %all-to-all-start.1 = ((bf16[32,8,8192]{2,1,0:T(8,128)(2,1)}), bf16[32,8,8192]{2,1,0:T(8,128)(2,1)}, u32[]{:S(2)}, u32[]{:S(2)}) async-start(bf16[32,8,8192]{2,1,0:T(8,128)(2,1)} %pad_maximum_fusion), calls=%async_computation.5 | async-start | bytes 8388608 | tf_op jit(solution)/shard_map/all_to_all | solution.py:206
  302.6 53.1 %shard_map.172 = bf16[512,1024]{1,0:T(8,128)(2,1)} custom-call(bf16[128,1024]{1,0:T(8,128)(2,1)} %convert_element_type.197.x_ref), custom_call_target="tpu_custom_call" | custom-call | tf_op jit(solution)/shard_map/pallas_call | solution.py:107
  355.6 1.8 convolution_convert_fusion.4
  357.5 2.8 fusion.84
  362.3 8.1 %fusion.29 = bf16[4,64,512]{2,1,0:T(8,128)(2,1)S(1)} fusion(bf16[512,4,64]{0,2,1:T(8,128)(2,1)S(1)} %bitcast.116, f32[4,512,512]{1,2,0:T(8,128)} %fusion.84, f32[4,512,512]{1,2,0:T(8,128)} %copy-done.30, f32[4,512]{1,0:T(4,128)S(1)} %log.8, pred[512,512]{0,1:T(8,128)(4,1)S(1)} %copy-done.18), kind=kOutput, calls=%fused_computation.33 | convolution fusion | flops 145885696 | bytes 9183232 | tf_op jit(solution)/shard_map/shqk,sqhe->skhe/dot_general | solution.py:230
  370.4 9.3 %fusion.79 = (bf16[4,64]{1,0:T(4,128)(2,1)S(1)}, bf16[1,512,4,64]{1,3,2,0:T(8,128)(2,1)S(1)}) fusion(bf16[512,4,64]{0,2,1:T(8,128)(2,1)S(1)} %bitcast.114, f32[4,512,512]{1,2,0:T(8,128)} %fusion.84, f32[4,512]{1,0:T(4,128)S(1)} %log.8, f32[4,512,512]{1,2,0:T(8,128)} %copy-done.30, pred[512,512]{0,1:T(8,128)(4,1)S(1)} %copy-done.18), kind=kOutput, calls=%fused_computation.145 | convolution fusion | flops 146016512 | bytes 9183744 | tf_op jit(solution)/shard_map/shqk,skhe->sqhe/dot_general | solution.py:227
  380.4 2.2 convolution_convert_fusion.2
  382.6 1.9 reshape.376
  388.7 2.9 reshape.377
  397.3 2.3 pad.9
  399.6 2.2 copy.76
  401.9 12.7 %all-to-all-start = ((bf16[32,8,7296]{2,1,0:T(8,128)(2,1)}), bf16[32,8,7296]{2,1,0:T(8,128)(2,1)}, u32[]{:S(2)}, u32[]{:S(2)}) async-start(bf16[32,8,7296]{2,1,0:T(8,128)(2,1)} %bitcast.97), calls=%async_computation.4 | async-start | bytes 7471104 | tf_op jit(solution)/shard_map/all_to_all | solution.py:266
  414.9 2.4 fusion.47
  417.4 2.8 reduce_sum.251
  420.2 49.2 %all-to-all-done = bf16[32,8,7296]{2,1,0:T(8,128)(2,1)} async-done(((bf16[32,8,7296]{2,1,0:T(8,128)(2,1)}), bf16[32,8,7296]{2,1,0:T(8,128)(2,1)}, u32[]{:S(2)}, u32[]{:S(2)}) %all-to-all-start) | async-done | bytes 3735584 | tf_op jit(solution)/shard_map/all_to_all | solution.py:266
  469.3 2.6 reduce_sum.250
  472.2 10.3 %all-gather.1 = bf16[495616]{0:T(1024)(128)(2,1)} all-gather(bf16[123904]{0:T(1024)(128)(2,1)S(1)} %pad_maximum_fusion.5), channel_id=3, replica_groups=mesh['rep'=4,'shard'=32] {'rep'}, dimensions={0}, use_global_device_ids=true | all-gather | bytes 1239040 | tf_op jit(solution)/shard_map/all_gather | solution.py:269
  482.5 2.1 reshape.396
  487.7 1.9 broadcast_in_dim_reshape.18
  492.0 3.1 copy.79
  495.1 4.5 broadcast_in_dim_reshape.20
  504.8 1.9 add_bitcast_fusion
  (202 shorter events, 55.5 us)
Async XLA Ops:
  7.2 6.1 %copy-start = (bf16[1,128,1024]{2,1,0:T(8,128)(2,1)S(1)}, bf16[1,128,1024]{2,1,0:T(8,128)(2,1)}, u32[]{:S(2)}) copy-start(bf16[1,128,1024]{2,1,0:T(8,128)(2,1)} %param.16) | copy-start | bytes 786436
  7.2 6.7 %copy-start.23 = (bf16[1,128]{1,0:T(2,128)(2,1)S(1)}, bf16[1,128]{1,0:T(2,128)(2,1)}, u32[]{:S(2)}) copy-start(bf16[1,128]{1,0:T(2,128)(2,1)} %param.19) | copy-start | bytes 772
  7.2 7.4 %copy-start.22 = (bf16[1,6,32]{2,1,0:T(8,128)(2,1)S(1)}, bf16[1,6,32]{2,1,0:T(8,128)(2,1)}, u32[]{:S(2)}) copy-start(bf16[1,6,32]{2,1,0:T(8,128)(2,1)} %param.17) | copy-start | bytes 1156
  7.2 7.5 %copy-start.24 = (bf16[1,2,32]{2,1,0:T(2,128)(2,1)S(1)}, bf16[1,2,32]{2,1,0:T(2,128)(2,1)}, u32[]{:S(2)}) copy-start(bf16[1,2,32]{2,1,0:T(2,128)(2,1)} %param.18) | copy-start | bytes 388
  7.2 115.5 %all-gather.4.cloned.1.call-start = ((), (), s32[]{:S(2)}) async-start(), calls=%async_computation.10 | async-start | bytes 8177664 | tf_op jit(solution)/shard_map/all_gather | solution.py:142
  8.7 7.5 %copy-start.25 = (s32[1,128]{1,0:T(1,128)S(1)}, s32[1,128]{1,0:T(1,128)}, u32[]{:S(2)}) copy-start(s32[1,128]{1,0:T(1,128)} %param.11) | copy-start | bytes 1540
  8.7 7.6 %copy-start.10 = (f32[1,128,1024]{2,1,0:T(8,128)S(1)}, f32[1,128,1024]{2,1,0:T(8,128)}, u32[]{:S(2)}) copy-start(f32[1,128,1024]{2,1,0:T(8,128)} %param.10) | copy-start | bytes 1572868
  16.2 169.9 %reduce-scatter.5.cloned.1.call-start = ((), (), s32[]{:S(2)}) async-start(), calls=%async_computation.6 | async-start | bytes 2621440 | tf_op jit(solution)/shard_map/reduce_scatter | solution.py:118
  131.9 5.9 %slice-start = ((bf16[32,123904]{1,0:T(8,128)(2,1)}), bf16[32,24576]{1,0:T(8,128)(2,1)S(1)}, s32[]{:S(2)}) async-start(bf16[32,123904]{1,0:T(8,128)(2,1)} %reshape.394), calls=%async_computation.11 | async-start | bytes 3145728 | tf_op jit(solution)/shard_map/slice | solution.py:143
  143.3 5.7 %copy-start.3 = (bf16[32,32768]{1,0:T(8,128)(2,1)S(1)}, bf16[32,32768]{1,0:T(8,128)(2,1)}, u32[]{:S(2)}) copy-start(bf16[32,32768]{1,0:T(8,128)(2,1)} %get-tuple-element.35) | copy-start | bytes 6291460
  148.9 2.4 copy-start.19
  148.9 2.4 copy-start.17
  153.6 2.0 copy-start.30
  155.7 0.7 copy-start.15
  159.3 82.0 %reduce-scatter.7.cloned.1.call-start = ((), (), s32[]{:S(2)}) async-start(), calls=%async_computation.7 | async-start | bytes 2621440 | tf_op jit(solution)/shard_map/reduce_scatter | solution.py:118
  161.6 4.4 copy-start.2
  168.4 36.0 %copy-start.7 = (bf16[1024,1024]{1,0:T(8,128)(2,1)S(1)}, bf16[1024,1024]{1,0:T(8,128)(2,1)}, u32[]{:S(2)}) copy-start(bf16[1024,1024]{1,0:T(8,128)(2,1)} %reshape.370) | copy-start | bytes 6291460
  204.3 5.1 copy-start.9
  208.4 1.0 copy-start.32
  212.1 30.7 %copy-start.5 = (f32[1,128,1024]{2,1,0:T(8,128)S(1)}, f32[1,128,1024]{2,1,0:T(8,128)}, u32[]{:S(2)}) copy-start(f32[1,128,1024]{2,1,0:T(8,128)} %param.12) | copy-start | bytes 1572868
  212.1 88.2 %reduce-scatter.9.cloned.1.call-start = ((), (), s32[]{:S(2)}) async-start(), calls=%async_computation.8 | async-start | bytes 2621440 | tf_op jit(solution)/shard_map/reduce_scatter | solution.py:118
  260.8 5.6 %copy-start.8 = (bf16[1024,1024]{1,0:T(8,128)(2,1)S(1)}, bf16[1024,1024]{1,0:T(8,128)(2,1)}, u32[]{:S(2)}) copy-start(bf16[1024,1024]{1,0:T(8,128)(2,1)} %reshape.370) | copy-start | bytes 6291460
  265.4 1.0 copy-start.33
  269.0 1.2 copy-start.14
  290.8 111.0 %all-to-all-start.1 = ((bf16[32,8,8192]{2,1,0:T(8,128)(2,1)}), bf16[32,8,8192]{2,1,0:T(8,128)(2,1)}, u32[]{:S(2)}, u32[]{:S(2)}) async-start(bf16[32,8,8192]{2,1,0:T(8,128)(2,1)} %pad_maximum_fusion), calls=%async_computation.5 | async-start | bytes 8388608 | tf_op jit(solution)/shard_map/all_to_all | solution.py:206
  357.5 2.9 copy-start.18
  357.5 3.6 copy-start.31
  361.2 1.1 copy-start.21
  362.3 8.1 %copy-start.20 = (bf16[512,256]{0,1:T(8,128)(2,1)S(1)}, bf16[512,256]{0,1:T(8,128)(2,1)}, u32[]{:S(2)}) copy-start(bf16[512,256]{0,1:T(8,128)(2,1)} %copy-done.19) | copy-start | bytes 786436
  370.4 9.3 %copy-start.26 = (bf16[4,64,512]{2,1,0:T(8,128)(2,1)}, bf16[4,64,512]{2,1,0:T(8,128)(2,1)S(1)}, u32[]{:S(2)}) copy-start(bf16[4,64,512]{2,1,0:T(8,128)(2,1)S(1)} %fusion.29) | copy-start | bytes 786436
  370.4 10.0 %copy-start.13 = (bf16[512,1152]{1,0:T(8,128)(2,1)S(1)}, bf16[512,1152]{1,0:T(8,128)(2,1)}, u32[]{:S(2)}) copy-start(bf16[512,1152]{1,0:T(8,128)(2,1)} %shard_map.169) | copy-start | bytes 3538948
  379.7 0.7 copy-start.28
  384.5 3.0 copy-start.6
  384.5 3.0 copy-start.16
  401.9 13.0 %copy-start.12 = (bf16[1024,768]{1,0:T(8,128)(2,1)S(1)}, bf16[1024,768]{1,0:T(8,128)(2,1)}, u32[]{:S(2)}) copy-start(bf16[1024,768]{1,0:T(8,128)(2,1)} %reshape.362) | copy-start | bytes 4718596
  401.9 13.0 %copy-start.27 = (bf16[4,64,512]{2,1,0:T(8,128)(2,1)S(1)}, bf16[4,64,512]{2,1,0:T(8,128)(2,1)}, u32[]{:S(2)}) copy-start(bf16[4,64,512]{2,1,0:T(8,128)(2,1)} %copy-done.26) | copy-start | bytes 786436
  401.9 13.0 %copy-start.29 = (bf16[1,512,4,64]{1,3,2,0:T(8,128)(2,1)S(1)}, bf16[1,512,4,64]{1,3,2,0:T(8,128)(2,1)}, u32[]{:S(2)}) copy-start(bf16[1,512,4,64]{1,3,2,0:T(8,128)(2,1)} %copy-done.28) | copy-start | bytes 786436
  401.9 67.4 %all-to-all-start = ((bf16[32,8,7296]{2,1,0:T(8,128)(2,1)}), bf16[32,8,7296]{2,1,0:T(8,128)(2,1)}, u32[]{:S(2)}, u32[]{:S(2)}) async-start(bf16[32,8,7296]{2,1,0:T(8,128)(2,1)} %bitcast.97), calls=%async_computation.4 | async-start | bytes 7471104 | tf_op jit(solution)/shard_map/all_to_all | solution.py:266
  414.6 90.1 %reduce-scatter.11.cloned.1.call-start = ((), (), s32[]{:S(2)}) async-start(), calls=%async_computation.9 | async-start | bytes 2621440 | tf_op jit(solution)/shard_map/reduce_scatter | solution.py:118
  484.6 6.1 %copy-start.4 = (f32[4,123904]{1,0:T(4,128)}, f32[4,123904]{1,0:T(4,128)S(1)}, u32[]{:S(2)}) copy-start(f32[4,123904]{1,0:T(4,128)S(1)} %reshape.396) | copy-start | bytes 5947396
  495.1 4.5 copy-start.11
  495.1 11.5 %copy-start.1 = (bf16[1,128,1024]{2,1,0:T(8,128)(2,1)S(1)}, bf16[1,128,1024]{2,1,0:T(8,128)(2,1)}, u32[]{:S(2)}) copy-start(bf16[1,128,1024]{2,1,0:T(8,128)(2,1)} %param.16) | copy-start | bytes 786436
Sparse Core Ops, SparseCore 0:
  16.3 106.3 all-gather.3
  159.4 26.6 reduce-scatter.4
  212.2 28.9 reduce-scatter.6
  269.2 29.0 reduce-scatter.8
  417.7 55.7 reduce-scatter.10

commit v7 on v6

--- a/solution.py
+++ b/solution.py
@@ -266,7 +266,7 @@
     received = lax.all_to_all(grad_pack, "shard", 0, 0, tiled=True)
     shares = jnp.sum(received.astype(jnp.float32), axis=0).astype(jnp.bfloat16)
     all_shares = jnp.concatenate([shares.reshape(-1), ffn_share.reshape(-1)])
-    joined = lax.all_gather(all_shares, "rep", axis=0, tiled=False).astype(jnp.float32)
+    joined = gather_rep(all_shares.reshape(-1, 128), cid=2).reshape(reps, -1).astype(jnp.float32)
     g_sizes = g_sizes + [padded - width, ffn_share.size // 2, ffn_share.size // 2]
     names = ["qkv", "out", "bup", "bias", "gain", "pad", "up", "down"]
     g_offsets = [sum(g_sizes[:i]) for i in range(len(g_sizes) + 1)]

time: 523 us -> 529 us (1.011)
  Pallas kernels: 106 us -> 121 us
  blocking collectives: 10.3 us -> 0 us
    pallas_call x4 -> x5, Pallas kernels: 106 us -> 121 us  [gather_rep(): pl.pallas_call(rep_gather_kernel, out_shape=jax.ShapeDtypeStruct((n * row...]
    all_gather x1 -> x0, blocking collectives: 10.3 us -> none  [local(): lax.all_gather(all_shares, 'rep', axis=0, tiled=False).astype(jnp.float32)]
  transfers between devices with their start and end apart: 7 -> 7, of which waited for: 4 -> 4; matrix products, arithmetic and copies ran while one was open for 21% -> 21% of each run, Pallas kernels for 14% -> 17%
where the time goes in v7:
time: 529 us; the launch traced here: 519 us
  waiting for transfers between devices  179 us (34%)
  Pallas kernels  121 us (23%)
  local copies, waits for them, and re-layouts  91.2 us (17%)
  matrix products  61.3 us (12%)
  other arithmetic  29.9 us (6%)
  starting transfers between devices  22.3 us (4%)
  between operations  14.9 us (3%)
    pallas_call x5, Pallas kernels, gather_rep(): pl.pallas_call(rep_gather_kernel, out_shape=jax.ShapeDtypeStruct((n * row...  121 us
    all_gather x1, waiting for transfers between devices, local(): gathered = lax.all_gather(packed, 'shard', axis=0, tiled=False)  82.7 us
    all_to_all x1, waiting for transfers between devices, local(): received = lax.all_to_all(grad_pack, 'shard', 0, 0, tiled=True)  49.2 us
    reduce_scatter x4, waiting for transfers between devices, scatter_rep(): return lax.psum_scatter(tensor, 'rep', scatter_dimension=0, tiled=True)  46.6 us
    unnamed x83, local copies, waits for them, and re-layouts  14.7 us
    dot_general x4, matrix products, matmul(): return jnp.dot(first_op, second_op, preferred_element_type=jnp.float32)  13.4 us
    all_to_all x1, starting transfers between devices, local(): received = lax.all_to_all(grad_pack, 'shard', 0, 0, tiled=True)  12.7 us
    dot_general x4, matrix products, matmul_lt(): lax.dot_general(first_op, second_op, (((0,), (0,)), ((), ())), preferred_...  11.7 us
  transfers between devices with their start and end apart: 7, of which 4 were waited for; matrix products, arithmetic and copies ran while one was open for 21% of the time, Pallas kernels for 17%

profile of v7, /device:TPU:1, one launch (start us, length us, event | category | flops | bytes accessed | tf_op | source)
XLA Modules:
  0.0 519.3 jit_solution(17704082814276824314)
XLA Ops:
  9.7 1.7 reshape_squeeze.23
  11.4 1.7 dynamic-slice_reduce_fusion
  17.1 20.9 %shard_map.169 = bf16[512,1152]{1,0:T(8,128)(2,1)} custom-call(bf16[128,1152]{1,0:T(8,128)(2,1)} %pad_maximum_fusion.4.x_ref), custom_call_target="tpu_custom_call" | custom-call | tf_op jit(solution)/shard_map/pallas_call | solution.py:107
  40.1 82.7 %all-gather.3.cloned.1.call-done = bf16[3964928]{0:T(1024)(128)(2,1)} async-done(((bf16[123904]{0:T(1024)(128)(2,1)}), bf16[3964928]{0:T(1024)(128)(2,1)}) %all-gather.3.cloned.1.call-update) | async-done | bytes 7929872 | tf_op jit(solution)/shard_map/all_gather | solution.py:142
  122.7 8.3 %reshape.402 = bf16[32,123904]{1,0:T(8,128)(2,1)} reshape(bf16[3964928]{0:T(1024)(128)(2,1)} %all-gather.3.cloned.1.call-done) | data formatting | bytes 15859712 | tf_op jit(solution)/shard_map/all_gather | solution.py:142
  131.9 5.7 %fusion.76 = (bf16[32,32768]{1,0:T(8,128)(2,1)}, bf16[32,32768]{1,0:T(8,128)(2,1)}, bf16[32,32768]{1,0:T(8,128)(2,1)}) fusion(bf16[32,123904]{1,0:T(8,128)(2,1)} %reshape.402), kind=kLoop, calls=%fused_computation.142 | loop fusion | bytes 12582912 | tf_op jit(solution)/shard_map/slice | solution.py:143
  139.4 3.9 fusion.33
  144.8 2.0 fusion.35
  148.9 2.4 reshape.374
  151.3 2.3 fusion.2
  156.4 2.9 fusion.45
  161.7 4.4 reshape.376
  166.0 2.3 reshape.377
  168.4 17.7 %reduce-scatter.5.cloned.1.call-done = f32[128,1024]{1,0:T(8,128)} async-done(((f32[512,1024]{1,0:T(8,128)}), f32[128,1024]{1,0:T(8,128)}) %reduce-scatter.5.cloned.1.call-update) | async-done | bytes 524304 | tf_op jit(solution)/shard_map/reduce_scatter | solution.py:118
  188.4 16.0 %shard_map.170 = bf16[512,1024]{1,0:T(8,128)(2,1)} custom-call(bf16[128,1024]{1,0:T(8,128)(2,1)} %fusion.42.x_ref), custom_call_target="tpu_custom_call" | custom-call | tf_op jit(solution)/shard_map/pallas_call | solution.py:107
  204.4 4.1 multiply_convert_fusion.1
  209.5 2.6 fusion.83
  212.3 28.9 %reduce-scatter.7.cloned.1.call-done = f32[128,1024]{1,0:T(8,128)} async-done(((f32[512,1024]{1,0:T(8,128)}), f32[128,1024]{1,0:T(8,128)}) %reduce-scatter.7.cloned.1.call-update) | async-done | bytes 524304 | tf_op jit(solution)/shard_map/reduce_scatter | solution.py:118
  244.8 15.9 %shard_map.171 = bf16[512,1024]{1,0:T(8,128)(2,1)} custom-call(bf16[128,1024]{1,0:T(8,128)(2,1)} %convert_element_type.198.x_ref), custom_call_target="tpu_custom_call" | custom-call | tf_op jit(solution)/shard_map/pallas_call | solution.py:107
  260.8 4.6 fusion.82
  266.4 2.6 fusion.40
  270.2 3.8 convolution_convert_fusion
  274.1 3.3 concatenate.33
  277.4 4.4 convolution_convert_fusion.1
  281.8 4.5 concatenate.32
  286.3 4.6 pad_maximum_fusion
  290.8 9.0 %all-to-all-start.1 = ((bf16[32,8,8192]{2,1,0:T(8,128)(2,1)}), bf16[32,8,8192]{2,1,0:T(8,128)(2,1)}, u32[]{:S(2)}, u32[]{:S(2)}) async-start(bf16[32,8,8192]{2,1,0:T(8,128)(2,1)} %pad_maximum_fusion), calls=%async_computation.5 | async-start | bytes 8388608 | tf_op jit(solution)/shard_map/all_to_all | solution.py:206
  302.6 53.1 %shard_map.172 = bf16[512,1024]{1,0:T(8,128)(2,1)} custom-call(bf16[128,1024]{1,0:T(8,128)(2,1)} %convert_element_type.200.x_ref), custom_call_target="tpu_custom_call" | custom-call | tf_op jit(solution)/shard_map/pallas_call | solution.py:107
  355.6 1.8 convolution_convert_fusion.4
  357.5 2.8 fusion.84
  362.3 8.1 %fusion.29 = bf16[4,64,512]{2,1,0:T(8,128)(2,1)S(1)} fusion(bf16[512,4,64]{0,2,1:T(8,128)(2,1)S(1)} %bitcast.118, f32[4,512,512]{1,2,0:T(8,128)} %fusion.84, f32[4,512,512]{1,2,0:T(8,128)} %copy-done.30, f32[4,512]{1,0:T(4,128)S(1)} %log.8, pred[512,512]{0,1:T(8,128)(4,1)S(1)} %copy-done.18), kind=kOutput, calls=%fused_computation.33 | convolution fusion | flops 145885696 | bytes 9183232 | tf_op jit(solution)/shard_map/shqk,sqhe->skhe/dot_general | solution.py:230
  370.4 9.3 %fusion.79 = (bf16[4,64]{1,0:T(4,128)(2,1)S(1)}, bf16[1,512,4,64]{1,3,2,0:T(8,128)(2,1)S(1)}) fusion(bf16[512,4,64]{0,2,1:T(8,128)(2,1)S(1)} %bitcast.116, f32[4,512,512]{1,2,0:T(8,128)} %fusion.84, f32[4,512]{1,0:T(4,128)S(1)} %log.8, f32[4,512,512]{1,2,0:T(8,128)} %copy-done.30, pred[512,512]{0,1:T(8,128)(4,1)S(1)} %copy-done.18), kind=kOutput, calls=%fused_computation.145 | convolution fusion | flops 146016512 | bytes 9183744 | tf_op jit(solution)/shard_map/shqk,skhe->sqhe/dot_general | solution.py:227
  380.4 2.2 convolution_convert_fusion.2
  382.6 1.9 reshape.382
  388.7 2.9 reshape.383
  397.3 2.3 pad.9
  399.6 2.2 copy.76
  401.9 12.7 %all-to-all-start = ((bf16[32,8,7296]{2,1,0:T(8,128)(2,1)}), bf16[32,8,7296]{2,1,0:T(8,128)(2,1)}, u32[]{:S(2)}, u32[]{:S(2)}) async-start(bf16[32,8,7296]{2,1,0:T(8,128)(2,1)} %bitcast.99), calls=%async_computation.4 | async-start | bytes 7471104 | tf_op jit(solution)/shard_map/all_to_all | solution.py:266
  414.9 2.4 fusion.47
  417.4 2.8 reduce_sum.251
  420.2 49.2 %all-to-all-done = bf16[32,8,7296]{2,1,0:T(8,128)(2,1)} async-done(((bf16[32,8,7296]{2,1,0:T(8,128)(2,1)}), bf16[32,8,7296]{2,1,0:T(8,128)(2,1)}, u32[]{:S(2)}, u32[]{:S(2)}) %all-to-all-start) | async-done | bytes 3735584 | tf_op jit(solution)/shard_map/all_to_all | solution.py:266
  469.3 2.6 reduce_sum.250
  472.9 15.2 %shard_map.173 = bf16[3872,128]{1,0:T(8,128)(2,1)} custom-call(bf16[968,128]{1,0:T(8,128)(2,1)} %maximum_bitcast_fusion.x_ref), custom_call_target="tpu_custom_call" | custom-call | tf_op jit(solution)/shard_map/pallas_call | solution.py:107
  488.1 2.1 reshape.401
  493.4 1.9 broadcast_in_dim_reshape.18
  497.7 3.1 copy.79
  500.8 4.5 broadcast_in_dim_reshape.20
  510.4 1.9 add_bitcast_fusion
  (202 shorter events, 56.2 us)
Async XLA Ops:
  7.2 6.1 %copy-start = (bf16[1,128,1024]{2,1,0:T(8,128)(2,1)S(1)}, bf16[1,128,1024]{2,1,0:T(8,128)(2,1)}, u32[]{:S(2)}) copy-start(bf16[1,128,1024]{2,1,0:T(8,128)(2,1)} %param.16) | copy-start | bytes 786436
  7.2 6.7 %copy-start.23 = (bf16[1,128]{1,0:T(2,128)(2,1)S(1)}, bf16[1,128]{1,0:T(2,128)(2,1)}, u32[]{:S(2)}) copy-start(bf16[1,128]{1,0:T(2,128)(2,1)} %param.19) | copy-start | bytes 772
  7.2 7.4 %copy-start.22 = (bf16[1,6,32]{2,1,0:T(8,128)(2,1)S(1)}, bf16[1,6,32]{2,1,0:T(8,128)(2,1)}, u32[]{:S(2)}) copy-start(bf16[1,6,32]{2,1,0:T(8,128)(2,1)} %param.17) | copy-start | bytes 1156
  7.2 7.5 %copy-start.24 = (bf16[1,2,32]{2,1,0:T(2,128)(2,1)S(1)}, bf16[1,2,32]{2,1,0:T(2,128)(2,1)}, u32[]{:S(2)}) copy-start(bf16[1,2,32]{2,1,0:T(2,128)(2,1)} %param.18) | copy-start | bytes 388
  7.2 115.5 %all-gather.3.cloned.1.call-start = ((), (), s32[]{:S(2)}) async-start(), calls=%async_computation.10 | async-start | bytes 8177664 | tf_op jit(solution)/shard_map/all_gather | solution.py:142
  8.7 7.5 %copy-start.25 = (s32[1,128]{1,0:T(1,128)S(1)}, s32[1,128]{1,0:T(1,128)}, u32[]{:S(2)}) copy-start(s32[1,128]{1,0:T(1,128)} %param.11) | copy-start | bytes 1540
  8.7 7.6 %copy-start.10 = (f32[1,128,1024]{2,1,0:T(8,128)S(1)}, f32[1,128,1024]{2,1,0:T(8,128)}, u32[]{:S(2)}) copy-start(f32[1,128,1024]{2,1,0:T(8,128)} %param.10) | copy-start | bytes 1572868
  16.2 169.9 %reduce-scatter.5.cloned.1.call-start = ((), (), s32[]{:S(2)}) async-start(), calls=%async_computation.6 | async-start | bytes 2621440 | tf_op jit(solution)/shard_map/reduce_scatter | solution.py:118
  131.9 5.9 %slice-start = ((bf16[32,123904]{1,0:T(8,128)(2,1)}), bf16[32,24576]{1,0:T(8,128)(2,1)S(1)}, s32[]{:S(2)}) async-start(bf16[32,123904]{1,0:T(8,128)(2,1)} %reshape.402), calls=%async_computation.11 | async-start | bytes 3145728 | tf_op jit(solution)/shard_map/slice | solution.py:143
  143.3 5.7 %copy-start.3 = (bf16[32,32768]{1,0:T(8,128)(2,1)S(1)}, bf16[32,32768]{1,0:T(8,128)(2,1)}, u32[]{:S(2)}) copy-start(bf16[32,32768]{1,0:T(8,128)(2,1)} %get-tuple-element.35) | copy-start | bytes 6291460
  148.9 2.4 copy-start.19
  148.9 2.4 copy-start.17
  153.6 2.0 copy-start.30
  155.7 0.7 copy-start.15
  159.3 82.0 %reduce-scatter.7.cloned.1.call-start = ((), (), s32[]{:S(2)}) async-start(), calls=%async_computation.7 | async-start | bytes 2621440 | tf_op jit(solution)/shard_map/reduce_scatter | solution.py:118
  161.6 4.4 copy-start.2
  168.4 36.0 %copy-start.7 = (bf16[1024,1024]{1,0:T(8,128)(2,1)S(1)}, bf16[1024,1024]{1,0:T(8,128)(2,1)}, u32[]{:S(2)}) copy-start(bf16[1024,1024]{1,0:T(8,128)(2,1)} %reshape.376) | copy-start | bytes 6291460
  204.3 5.1 copy-start.9
  208.4 1.0 copy-start.32
  212.1 30.7 %copy-start.5 = (f32[1,128,1024]{2,1,0:T(8,128)S(1)}, f32[1,128,1024]{2,1,0:T(8,128)}, u32[]{:S(2)}) copy-start(f32[1,128,1024]{2,1,0:T(8,128)} %param.12) | copy-start | bytes 1572868
  212.1 88.2 %reduce-scatter.9.cloned.1.call-start = ((), (), s32[]{:S(2)}) async-start(), calls=%async_computation.8 | async-start | bytes 2621440 | tf_op jit(solution)/shard_map/reduce_scatter | solution.py:118
  260.8 5.6 %copy-start.8 = (bf16[1024,1024]{1,0:T(8,128)(2,1)S(1)}, bf16[1024,1024]{1,0:T(8,128)(2,1)}, u32[]{:S(2)}) copy-start(bf16[1024,1024]{1,0:T(8,128)(2,1)} %reshape.376) | copy-start | bytes 6291460
  265.4 1.0 copy-start.33
  269.0 1.2 copy-start.14
  290.8 111.0 %all-to-all-start.1 = ((bf16[32,8,8192]{2,1,0:T(8,128)(2,1)}), bf16[32,8,8192]{2,1,0:T(8,128)(2,1)}, u32[]{:S(2)}, u32[]{:S(2)}) async-start(bf16[32,8,8192]{2,1,0:T(8,128)(2,1)} %pad_maximum_fusion), calls=%async_computation.5 | async-start | bytes 8388608 | tf_op jit(solution)/shard_map/all_to_all | solution.py:206
  357.5 2.9 copy-start.18
  357.5 3.6 copy-start.31
  361.2 1.1 copy-start.21
  362.3 8.1 %copy-start.20 = (bf16[512,256]{0,1:T(8,128)(2,1)S(1)}, bf16[512,256]{0,1:T(8,128)(2,1)}, u32[]{:S(2)}) copy-start(bf16[512,256]{0,1:T(8,128)(2,1)} %copy-done.19) | copy-start | bytes 786436
  370.4 9.3 %copy-start.26 = (bf16[4,64,512]{2,1,0:T(8,128)(2,1)}, bf16[4,64,512]{2,1,0:T(8,128)(2,1)S(1)}, u32[]{:S(2)}) copy-start(bf16[4,64,512]{2,1,0:T(8,128)(2,1)S(1)} %fusion.29) | copy-start | bytes 786436
  370.4 10.0 %copy-start.13 = (bf16[512,1152]{1,0:T(8,128)(2,1)S(1)}, bf16[512,1152]{1,0:T(8,128)(2,1)}, u32[]{:S(2)}) copy-start(bf16[512,1152]{1,0:T(8,128)(2,1)} %shard_map.169) | copy-start | bytes 3538948
  379.7 0.7 copy-start.28
  384.5 3.0 copy-start.6
  384.5 3.0 copy-start.16
  401.9 13.0 %copy-start.12 = (bf16[1024,768]{1,0:T(8,128)(2,1)S(1)}, bf16[1024,768]{1,0:T(8,128)(2,1)}, u32[]{:S(2)}) copy-start(bf16[1024,768]{1,0:T(8,128)(2,1)} %reshape.368) | copy-start | bytes 4718596
  401.9 13.0 %copy-start.27 = (bf16[4,64,512]{2,1,0:T(8,128)(2,1)S(1)}, bf16[4,64,512]{2,1,0:T(8,128)(2,1)}, u32[]{:S(2)}) copy-start(bf16[4,64,512]{2,1,0:T(8,128)(2,1)} %copy-done.26) | copy-start | bytes 786436
  401.9 13.0 %copy-start.29 = (bf16[1,512,4,64]{1,3,2,0:T(8,128)(2,1)S(1)}, bf16[1,512,4,64]{1,3,2,0:T(8,128)(2,1)}, u32[]{:S(2)}) copy-start(bf16[1,512,4,64]{1,3,2,0:T(8,128)(2,1)} %copy-done.28) | copy-start | bytes 786436
  401.9 67.4 %all-to-all-start = ((bf16[32,8,7296]{2,1,0:T(8,128)(2,1)}), bf16[32,8,7296]{2,1,0:T(8,128)(2,1)}, u32[]{:S(2)}, u32[]{:S(2)}) async-start(bf16[32,8,7296]{2,1,0:T(8,128)(2,1)} %bitcast.99), calls=%async_computation.4 | async-start | bytes 7471104 | tf_op jit(solution)/shard_map/all_to_all | solution.py:266
  414.6 95.8 %reduce-scatter.11.cloned.1.call-start = ((), (), s32[]{:S(2)}) async-start(), calls=%async_computation.9 | async-start | bytes 2621440 | tf_op jit(solution)/shard_map/reduce_scatter | solution.py:118
  490.2 6.1 %copy-start.4 = (f32[4,123904]{1,0:T(4,128)}, f32[4,123904]{1,0:T(4,128)S(1)}, u32[]{:S(2)}) copy-start(f32[4,123904]{1,0:T(4,128)S(1)} %reshape.401) | copy-start | bytes 5947396
  500.8 4.5 copy-start.11
  500.8 11.5 %copy-start.1 = (bf16[1,128,1024]{2,1,0:T(8,128)(2,1)S(1)}, bf16[1,128,1024]{2,1,0:T(8,128)(2,1)}, u32[]{:S(2)}) copy-start(bf16[1,128,1024]{2,1,0:T(8,128)(2,1)} %param.16) | copy-start | bytes 786436
Sparse Core Ops, SparseCore 0:
  16.3 106.3 all-gather.2
  159.4 26.6 reduce-scatter.4
  212.2 28.9 reduce-scatter.6
  269.2 29.0 reduce-scatter.8
  417.7 55.7 reduce-scatter.10

commit v8 on v6

--- a/solution.py
+++ b/solution.py
@@ -177,6 +177,7 @@
         .reshape(-1, head_cols)
     )
     first_sum = rows_f32 + scatter_rep(matmul(context, w_out_r)) + bias_all[2]
+    context_stack = gather_rep(context, cid=2).reshape(reps, -1, head_cols)
     norm_one, rstd_one = normalize(first_sum)
     mid_norm = norm_one * gain_all[0] + bias_all[3]
     mid_b = mid_norm.astype(jnp.bfloat16)
@@ -211,7 +212,10 @@
     d_first = norm_back(d_mid, norm_one, rstd_one, gain_all[0])
     d_bout = jnp.sum(d_first, axis=0)
     d_first_all = gather_rep(d_first.astype(jnp.bfloat16))
-    d_wout = matmul_lt(context, d_first_all)
+    d_first_cols = lax.dynamic_slice_in_dim(d_first_all, r * head_cols, head_cols, axis=1)
+    d_wout_cols = jnp.einsum(
+        "utc,tk->uck", context_stack, d_first_cols, preferred_element_type=jnp.float32
+    ).reshape(D, head_cols)
     d_context = (
         matmul_rt(d_first_all, w_out_r).astype(jnp.bfloat16).reshape(1, -1, heads_here, HEAD_DIM)
     )
@@ -245,15 +249,12 @@
     d_bv = lax.dynamic_update_slice_in_dim(zeros_cols, jnp.sum(d_values, axis=0), r * head_cols, 0)
     d_biases = jnp.stack([d_bq, d_bv, d_bout, d_bias_one, d_bdown, d_bias_two])
     d_gains = jnp.stack([d_gain_one, d_gain_two])
-    d_wout_all = lax.dynamic_update_slice_in_dim(
-        jnp.zeros((D, D), jnp.bfloat16), d_wout.astype(jnp.bfloat16), r * head_cols, 0
-    )
     d_bup_all = lax.dynamic_update_slice_in_dim(
         jnp.zeros((parts, reps, ff_piece), jnp.float32), d_bup.reshape(parts, 1, ff_piece), r, 1
     )
     grad_parts = (
         d_wqkv.astype(jnp.bfloat16).reshape(parts, -1),
-        d_wout_all.reshape(parts, -1),
+        d_wout_cols.astype(jnp.bfloat16).reshape(parts, -1),
         d_bup_all.astype(jnp.bfloat16).reshape(parts, -1),
         pack_cols(d_biases.astype(jnp.bfloat16), parts),
         pack_cols(d_gains.astype(jnp.bfloat16), parts),
@@ -272,7 +273,7 @@
     g_offsets = [sum(g_sizes[:i]) for i in range(len(g_sizes) + 1)]
     got = {names[i]: joined[:, g_offsets[i] : g_offsets[i + 1]] for i in range(len(g_sizes))}
     grad_w_qkv = got["qkv"].reshape(reps, k_rows, 3, head_cols).transpose(1, 2, 0, 3).reshape(k_rows, -1)
-    grad_w_out = jnp.sum(got["out"], axis=0).reshape(k_rows, D)
+    grad_w_out = got["out"].reshape(reps, k_rows, head_cols).transpose(1, 0, 2).reshape(k_rows, D)
     grad_w_up = got["up"].reshape(reps, k_rows, parts, ff_piece).transpose(1, 2, 0, 3).reshape(k_rows, -1)
     grad_w_down = got["down"].reshape(reps * ff_piece, D)
     grad_up_bias = jnp.sum(got["bup"], axis=0)

time: 523 us -> 509 us (0.973)
  waiting for transfers between devices: 179 us -> 153 us
  Pallas kernels: 106 us -> 127 us
  local copies, waits for them, and re-layouts: 91.2 us -> 80.4 us
    all_to_all x1, waiting for transfers between devices: 49.2 us -> 23.4 us  [local(): received = lax.all_to_all(grad_pack, 'shard', 0, 0, tiled=True)]
    pallas_call x4 -> x5, Pallas kernels: 106 us -> 127 us  [gather_rep(): pl.pallas_call(rep_gather_kernel, out_shape=jax.ShapeDtypeStruct((n * row...]
    unnamed x83 -> x81, local copies, waits for them, and re-layouts: 14.7 us -> 9.99 us
    dot_general x4 -> x3, matrix products: 11.7 us -> 10 us  [matmul_lt(): lax.dot_general(first_op, second_op, (((0,), (0,)), ((), ())), preferred_...]
  transfers between devices with their start and end apart: 7 -> 7, of which waited for: 4 -> 4; matrix products, arithmetic and copies ran while one was open for 21% -> 20% of each run, Pallas kernels for 14% -> 19%
where the time goes in v8:
time: 509 us; the launch traced here: 500 us
  waiting for transfers between devices  153 us (30%)
  Pallas kernels  127 us (25%)
  local copies, waits for them, and re-layouts  80.4 us (16%)
  matrix products  62.4 us (12%)
  other arithmetic  25.9 us (5%)
  starting transfers between devices  22.2 us (4%)
  between operations  14.9 us (3%)
  blocking collectives  14.2 us (3%)
    pallas_call x5, Pallas kernels, gather_rep(): pl.pallas_call(rep_gather_kernel, out_shape=jax.ShapeDtypeStruct((n * row...  127 us
    all_gather x1, waiting for transfers between devices, local(): gathered = lax.all_gather(packed, 'shard', axis=0, tiled=False)  82.7 us
    reduce_scatter x4, waiting for transfers between devices, scatter_rep(): return lax.psum_scatter(tensor, 'rep', scatter_dimension=0, tiled=True)  46.6 us
    all_to_all x1, waiting for transfers between devices, local(): received = lax.all_to_all(grad_pack, 'shard', 0, 0, tiled=True)  23.4 us
    all_gather x1, blocking collectives, local(): lax.all_gather(all_shares, 'rep', axis=0, tiled=False).astype(jnp.float32)  14.2 us
    dot_general x4, matrix products, matmul(): return jnp.dot(first_op, second_op, preferred_element_type=jnp.float32)  13.4 us
    dot_general x4, matrix products, matmul_rt(): lax.dot_general(first_op, second_op, (((1,), (1,)), ((), ())), preferred_...  12.9 us
    all_to_all x1, starting transfers between devices, local(): received = lax.all_to_all(grad_pack, 'shard', 0, 0, tiled=True)  12.3 us
  transfers between devices with their start and end apart: 7, of which 4 were waited for; matrix products, arithmetic and copies ran while one was open for 20% of the time, Pallas kernels for 19%

profile of v8, /device:TPU:1, one launch (start us, length us, event | category | flops | bytes accessed | tf_op | source)
XLA Modules:
  0.0 500.1 jit_solution(6985211828779181236)
XLA Ops:
  9.7 1.7 reshape_squeeze.23
  11.4 1.7 dynamic-slice_reduce_fusion
  17.1 20.9 %shard_map.169 = bf16[512,1152]{1,0:T(8,128)(2,1)} custom-call(bf16[128,1152]{1,0:T(8,128)(2,1)} %pad_maximum_fusion.4.x_ref), custom_call_target="tpu_custom_call" | custom-call | tf_op jit(solution)/shard_map/pallas_call | solution.py:107
  40.1 82.7 %all-gather.4.cloned.1.call-done = bf16[3964928]{0:T(1024)(128)(2,1)} async-done(((bf16[123904]{0:T(1024)(128)(2,1)}), bf16[3964928]{0:T(1024)(128)(2,1)}) %all-gather.4.cloned.1.call-update) | async-done | bytes 7929872 | tf_op jit(solution)/shard_map/all_gather | solution.py:142
  122.7 8.3 %reshape.404 = bf16[32,123904]{1,0:T(8,128)(2,1)} reshape(bf16[3964928]{0:T(1024)(128)(2,1)} %all-gather.4.cloned.1.call-done) | data formatting | bytes 15859712 | tf_op jit(solution)/shard_map/all_gather | solution.py:142
  131.9 5.7 %fusion.77 = (bf16[32,32768]{1,0:T(8,128)(2,1)}, bf16[32,32768]{1,0:T(8,128)(2,1)}, bf16[32,32768]{1,0:T(8,128)(2,1)}) fusion(bf16[32,123904]{1,0:T(8,128)(2,1)} %reshape.404), kind=kLoop, calls=%fused_computation.142 | loop fusion | bytes 12582912 | tf_op jit(solution)/shard_map/slice | solution.py:143
  137.7 1.7 reshape.370
  139.4 3.9 fusion.32
  144.8 2.0 fusion.34
  148.9 2.4 reshape.376
  151.3 2.3 fusion.2
  156.3 2.9 fusion.44
  161.6 4.4 reshape.378
  166.0 2.3 reshape.379
  168.3 17.7 %reduce-scatter.5.cloned.1.call-done = f32[128,1024]{1,0:T(8,128)} async-done(((f32[512,1024]{1,0:T(8,128)}), f32[128,1024]{1,0:T(8,128)}) %reduce-scatter.5.cloned.1.call-update) | async-done | bytes 524304 | tf_op jit(solution)/shard_map/reduce_scatter | solution.py:118
  188.3 16.0 %shard_map.170 = bf16[512,1024]{1,0:T(8,128)(2,1)} custom-call(bf16[128,1024]{1,0:T(8,128)(2,1)} %fusion.41.x_ref), custom_call_target="tpu_custom_call" | custom-call | tf_op jit(solution)/shard_map/pallas_call | solution.py:107
  204.4 4.0 multiply_convert_fusion.1
  209.4 2.6 fusion.84
  212.2 28.9 %reduce-scatter.7.cloned.1.call-done = f32[128,1024]{1,0:T(8,128)} async-done(((f32[512,1024]{1,0:T(8,128)}), f32[128,1024]{1,0:T(8,128)}) %reduce-scatter.7.cloned.1.call-update) | async-done | bytes 524304 | tf_op jit(solution)/shard_map/reduce_scatter | solution.py:118
  244.7 16.0 %shard_map.171 = bf16[512,1024]{1,0:T(8,128)(2,1)} custom-call(bf16[128,1024]{1,0:T(8,128)(2,1)} %convert_element_type.195.x_ref), custom_call_target="tpu_custom_call" | custom-call | tf_op jit(solution)/shard_map/pallas_call | solution.py:107
  260.8 4.6 fusion.83
  266.3 2.6 fusion.39
  270.7 21.9 %shard_map.173 = bf16[2048,256]{1,0:T(8,128)(2,1)} custom-call(bf16[512,256]{1,0:T(8,128)(2,1)} %copy.72.x_ref), custom_call_target="tpu_custom_call" | custom-call | tf_op jit(solution)/shard_map/pallas_call | solution.py:107
  292.6 2.3 copy.73
  294.9 2.7 convolution_convert_fusion
  297.6 3.3 concatenate.33
  300.9 4.2 convolution_convert_fusion.1
  305.1 4.5 concatenate.32
  309.6 4.6 pad_maximum_fusion
  314.2 9.2 %all-to-all-start.1 = ((bf16[32,8,8192]{2,1,0:T(8,128)(2,1)}), bf16[32,8,8192]{2,1,0:T(8,128)(2,1)}, u32[]{:S(2)}, u32[]{:S(2)}) async-start(bf16[32,8,8192]{2,1,0:T(8,128)(2,1)} %pad_maximum_fusion), calls=%async_computation.5 | async-start | bytes 8388608 | tf_op jit(solution)/shard_map/all_to_all | solution.py:207
  326.4 52.4 %shard_map.172 = bf16[512,1024]{1,0:T(8,128)(2,1)} custom-call(bf16[128,1024]{1,0:T(8,128)(2,1)} %convert_element_type.197.x_ref), custom_call_target="tpu_custom_call" | custom-call | tf_op jit(solution)/shard_map/pallas_call | solution.py:107
  378.9 1.8 convolution_convert_fusion.4
  380.7 2.8 fusion.85
  385.5 7.7 %fusion.28 = bf16[4,64,512]{2,1,0:T(8,128)(2,1)S(1)} fusion(bf16[512,4,64]{0,2,1:T(8,128)(2,1)S(1)} %bitcast.124, f32[4,512,512]{1,2,0:T(8,128)} %fusion.85, f32[4,512,512]{1,2,0:T(8,128)} %copy-done.28, f32[4,512]{1,0:T(4,128)S(1)} %log.8, pred[512,512]{0,1:T(8,128)(4,1)S(1)} %copy-done.17), kind=kOutput, calls=%fused_computation.32 | convolution fusion | flops 145885696 | bytes 9183232 | tf_op jit(solution)/shard_map/shqk,sqhe->skhe/dot_general | solution.py:234
  393.2 9.5 %fusion.80 = (bf16[4,64]{1,0:T(4,128)(2,1)S(1)}, bf16[1,512,4,64]{1,3,2,0:T(8,128)(2,1)}) fusion(bf16[512,4,64]{0,2,1:T(8,128)(2,1)S(1)} %bitcast.122, f32[4,512,512]{1,2,0:T(8,128)} %fusion.85, f32[4,512]{1,0:T(4,128)S(1)} %log.8, f32[4,512,512]{1,2,0:T(8,128)} %copy-done.28, pred[512,512]{0,1:T(8,128)(4,1)S(1)} %copy-done.17), kind=kOutput, calls=%fused_computation.145 | convolution fusion | flops 146016512 | bytes 9183744 | tf_op jit(solution)/shard_map/shqk,skhe->sqhe/dot_general | solution.py:231
  402.8 3.1 convolution_convert_fusion.2
  405.9 2.8 reshape.384
  411.4 1.5 constant_dynamic-update-slice_fusion.8
  413.6 1.6 copy.87
  415.2 12.3 %all-to-all-start = ((bf16[32,8,4224]{2,1,0:T(8,128)(2,1)}), bf16[32,8,4224]{2,1,0:T(8,128)(2,1)S(1)}, u32[]{:S(2)}, u32[]{:S(2)}) async-start(bf16[32,8,4224]{2,1,0:T(8,128)(2,1)} %bitcast.48), calls=%async_computation.4 | async-start | bytes 4325376 | tf_op jit(solution)/shard_map/all_to_all | solution.py:267
  427.8 2.8 reduce_sum.242
  430.7 3.9 fusion.46
  434.6 23.4 %all-to-all-done = bf16[32,8,4224]{2,1,0:T(8,128)(2,1)S(1)} async-done(((bf16[32,8,4224]{2,1,0:T(8,128)(2,1)}), bf16[32,8,4224]{2,1,0:T(8,128)(2,1)S(1)}, u32[]{:S(2)}, u32[]{:S(2)}) %all-to-all-start) | async-done | bytes 2162720 | tf_op jit(solution)/shard_map/all_to_all | solution.py:267
  458.5 14.2 %all-gather.1 = bf16[397312]{0:T(1024)(128)(2,1)} all-gather(bf16[99328]{0:T(1024)(128)(2,1)S(1)} %pad_maximum_fusion.5), channel_id=3, replica_groups=mesh['rep'=4,'shard'=32] {'rep'}, dimensions={0}, use_global_device_ids=true | all-gather | bytes 993280 | tf_op jit(solution)/shard_map/all_gather | solution.py:270
  472.7 1.8 reshape.406
  478.5 3.1 copy.90
  481.7 4.5 broadcast_in_dim_reshape.20
  491.2 1.9 add_bitcast_fusion
  (203 shorter events, 45.8 us)
Async XLA Ops:
  7.2 6.1 %copy-start = (bf16[1,128,1024]{2,1,0:T(8,128)(2,1)S(1)}, bf16[1,128,1024]{2,1,0:T(8,128)(2,1)}, u32[]{:S(2)}) copy-start(bf16[1,128,1024]{2,1,0:T(8,128)(2,1)} %param.16) | copy-start | bytes 786436
  7.2 6.7 %copy-start.22 = (bf16[1,128]{1,0:T(2,128)(2,1)S(1)}, bf16[1,128]{1,0:T(2,128)(2,1)}, u32[]{:S(2)}) copy-start(bf16[1,128]{1,0:T(2,128)(2,1)} %param.19) | copy-start | bytes 772
  7.2 7.4 %copy-start.21 = (bf16[1,6,32]{2,1,0:T(8,128)(2,1)S(1)}, bf16[1,6,32]{2,1,0:T(8,128)(2,1)}, u32[]{:S(2)}) copy-start(bf16[1,6,32]{2,1,0:T(8,128)(2,1)} %param.17) | copy-start | bytes 1156
  7.2 7.5 %copy-start.23 = (bf16[1,2,32]{2,1,0:T(2,128)(2,1)S(1)}, bf16[1,2,32]{2,1,0:T(2,128)(2,1)}, u32[]{:S(2)}) copy-start(bf16[1,2,32]{2,1,0:T(2,128)(2,1)} %param.18) | copy-start | bytes 388
  7.2 115.5 %all-gather.4.cloned.1.call-start = ((), (), s32[]{:S(2)}) async-start(), calls=%async_computation.10 | async-start | bytes 8177664 | tf_op jit(solution)/shard_map/all_gather | solution.py:142
  8.7 7.5 %copy-start.24 = (s32[1,128]{1,0:T(1,128)S(1)}, s32[1,128]{1,0:T(1,128)}, u32[]{:S(2)}) copy-start(s32[1,128]{1,0:T(1,128)} %param.11) | copy-start | bytes 1540
  8.7 7.6 %copy-start.10 = (f32[1,128,1024]{2,1,0:T(8,128)S(1)}, f32[1,128,1024]{2,1,0:T(8,128)}, u32[]{:S(2)}) copy-start(f32[1,128,1024]{2,1,0:T(8,128)} %param.10) | copy-start | bytes 1572868
  16.2 169.8 %reduce-scatter.5.cloned.1.call-start = ((), (), s32[]{:S(2)}) async-start(), calls=%async_computation.6 | async-start | bytes 2621440 | tf_op jit(solution)/shard_map/reduce_scatter | solution.py:118
  131.9 5.9 %slice-start = ((bf16[32,123904]{1,0:T(8,128)(2,1)}), bf16[32,24576]{1,0:T(8,128)(2,1)S(1)}, s32[]{:S(2)}) async-start(bf16[32,123904]{1,0:T(8,128)(2,1)} %reshape.404), calls=%async_computation.11 | async-start | bytes 3145728 | tf_op jit(solution)/shard_map/slice | solution.py:143
  143.3 5.7 %copy-start.3 = (bf16[32,32768]{1,0:T(8,128)(2,1)S(1)}, bf16[32,32768]{1,0:T(8,128)(2,1)}, u32[]{:S(2)}) copy-start(bf16[32,32768]{1,0:T(8,128)(2,1)} %get-tuple-element.35) | copy-start | bytes 6291460
  148.9 2.4 copy-start.18
  148.9 2.4 copy-start.16
  153.6 2.0 copy-start.28
  155.6 0.7 copy-start.14
  159.2 81.9 %reduce-scatter.7.cloned.1.call-start = ((), (), s32[]{:S(2)}) async-start(), calls=%async_computation.7 | async-start | bytes 2621440 | tf_op jit(solution)/shard_map/reduce_scatter | solution.py:118
  161.6 4.4 copy-start.2
  168.3 36.0 %copy-start.7 = (bf16[1024,1024]{1,0:T(8,128)(2,1)S(1)}, bf16[1024,1024]{1,0:T(8,128)(2,1)}, u32[]{:S(2)}) copy-start(bf16[1024,1024]{1,0:T(8,128)(2,1)} %reshape.378) | copy-start | bytes 6291460
  204.4 5.0 %copy-start.9 = (bf16[1024,1024]{1,0:T(8,128)(2,1)S(1)}, bf16[1024,1024]{1,0:T(8,128)(2,1)}, u32[]{:S(2)}) copy-start(bf16[1024,1024]{1,0:T(8,128)(2,1)} %reshape.379) | copy-start | bytes 6291460
  208.4 1.0 copy-start.30
  212.0 30.7 %copy-start.5 = (f32[1,128,1024]{2,1,0:T(8,128)S(1)}, f32[1,128,1024]{2,1,0:T(8,128)}, u32[]{:S(2)}) copy-start(f32[1,128,1024]{2,1,0:T(8,128)} %param.12) | copy-start | bytes 1572868
  212.0 112.1 %reduce-scatter.9.cloned.1.call-start = ((), (), s32[]{:S(2)}) async-start(), calls=%async_computation.8 | async-start | bytes 2621440 | tf_op jit(solution)/shard_map/reduce_scatter | solution.py:118
  260.8 5.6 %copy-start.8 = (bf16[1024,1024]{1,0:T(8,128)(2,1)S(1)}, bf16[1024,1024]{1,0:T(8,128)(2,1)}, u32[]{:S(2)}) copy-start(bf16[1024,1024]{1,0:T(8,128)(2,1)} %reshape.378) | copy-start | bytes 6291460
  265.4 1.0 copy-start.32
  268.9 0.9 copy-start.15
  269.0 25.9 %copy-start.13 = (bf16[512,1024]{1,0:T(8,128)(2,1)S(1)}, bf16[512,1024]{1,0:T(8,128)(2,1)}, u32[]{:S(2)}) copy-start(bf16[512,1024]{1,0:T(8,128)(2,1)} %shard_map.171) | copy-start | bytes 3145732
  270.7 24.2 %copy-start.31 = (bf16[512,1024]{1,0:T(8,128)(2,1)S(1)}, bf16[512,1024]{1,0:T(8,128)(2,1)}, u32[]{:S(2)}) copy-start(bf16[512,1024]{1,0:T(8,128)(2,1)} %copy-done.30) | copy-start | bytes 3145732
  314.2 101.0 %all-to-all-start.1 = ((bf16[32,8,8192]{2,1,0:T(8,128)(2,1)}), bf16[32,8,8192]{2,1,0:T(8,128)(2,1)}, u32[]{:S(2)}, u32[]{:S(2)}) async-start(bf16[32,8,8192]{2,1,0:T(8,128)(2,1)} %pad_maximum_fusion), calls=%async_computation.5 | async-start | bytes 8388608 | tf_op jit(solution)/shard_map/all_to_all | solution.py:207
  380.7 2.9 copy-start.17
  380.7 3.6 copy-start.29
  384.4 1.1 copy-start.20
  385.5 17.3 %copy-start.25 = (bf16[1,512,4,64]{1,3,2,0:T(8,128)(2,1)}, bf16[1,512,4,64]{1,3,2,0:T(8,128)(2,1)S(1)}, u32[]{:S(2)}) copy-start(bf16[1,512,4,64]{1,3,2,0:T(8,128)(2,1)S(1)} %get-tuple-element.42) | copy-start | bytes 786436
  385.5 7.7 %copy-start.19 = (bf16[512,256]{0,1:T(8,128)(2,1)S(1)}, bf16[512,256]{0,1:T(8,128)(2,1)}, u32[]{:S(2)}) copy-start(bf16[512,256]{0,1:T(8,128)(2,1)} %copy-done.18) | copy-start | bytes 786436
  393.2 9.6 %copy-start.27 = (bf16[4,64,512]{2,1,0:T(8,128)(2,1)}, bf16[4,64,512]{2,1,0:T(8,128)(2,1)S(1)}, u32[]{:S(2)}) copy-start(bf16[4,64,512]{2,1,0:T(8,128)(2,1)S(1)} %fusion.28) | copy-start | bytes 786436
  393.2 9.6 %copy-start.12 = (bf16[512,1152]{1,0:T(8,128)(2,1)S(1)}, bf16[512,1152]{1,0:T(8,128)(2,1)}, u32[]{:S(2)}) copy-start(bf16[512,1152]{1,0:T(8,128)(2,1)} %shard_map.169) | copy-start | bytes 3538948
  405.9 2.8 copy-start.6
  415.2 42.9 %all-to-all-start = ((bf16[32,8,4224]{2,1,0:T(8,128)(2,1)}), bf16[32,8,4224]{2,1,0:T(8,128)(2,1)S(1)}, u32[]{:S(2)}, u32[]{:S(2)}) async-start(bf16[32,8,4224]{2,1,0:T(8,128)(2,1)} %bitcast.48), calls=%async_computation.4 | async-start | bytes 4325376 | tf_op jit(solution)/shard_map/all_to_all | solution.py:267
  427.5 3.1 copy-start.26
  427.5 63.7 %reduce-scatter.11.cloned.1.call-start = ((), (), s32[]{:S(2)}) async-start(), calls=%async_computation.9 | async-start | bytes 2621440 | tf_op jit(solution)/shard_map/reduce_scatter | solution.py:118
  474.6 3.2 copy-start.4
  481.7 4.5 copy-start.11
  481.7 11.5 %copy-start.1 = (bf16[1,128,1024]{2,1,0:T(8,128)(2,1)S(1)}, bf16[1,128,1024]{2,1,0:T(8,128)(2,1)}, u32[]{:S(2)}) copy-start(bf16[1,128,1024]{2,1,0:T(8,128)(2,1)} %param.16) | copy-start | bytes 786436
Sparse Core Ops, SparseCore 0:
  16.3 106.3 all-gather.3
  159.3 26.6 reduce-scatter.4
  212.1 28.9 reduce-scatter.6
  269.1 34.5 reduce-scatter.8
  434.7 42.0 reduce-scatter.10

commit v9 on v8

--- a/solution.py
+++ b/solution.py
@@ -134,21 +134,24 @@
     up_piece = pick(w_up[0].reshape(k_rows, parts, reps, ff_piece), r, 2).reshape(k_rows, -1)
     down_piece = pick(w_down[0].reshape(reps, ff_piece, D), r, 0)
     upb_piece = pick(up_bias[0].reshape(reps, ff_piece), r, 0)
-    pieces = (qkv_piece, out_piece, up_piece, down_piece, upb_piece, biases[0], norm_gains[0])
-    sizes = [piece.size for piece in pieces]
-    offsets = [sum(sizes[:i]) for i in range(len(sizes) + 1)]
-    packed = jnp.concatenate([piece.reshape(-1) for piece in pieces])
-    packed = jnp.pad(packed, (0, -(-packed.size // 1024) * 1024 - packed.size))
-    gathered = lax.all_gather(packed, "shard", axis=0, tiled=False)
-    got = [gathered[:, offsets[i] : offsets[i + 1]] for i in range(len(sizes))]
+    first = (qkv_piece, out_piece, biases[0], norm_gains[0])
+    second = (up_piece, down_piece, upb_piece)
+    got = []
+    for group in (first, second):
+        sizes = [piece.size for piece in group]
+        offsets = [sum(sizes[:i]) for i in range(len(sizes) + 1)]
+        packed = jnp.concatenate([piece.reshape(-1) for piece in group])
+        packed = jnp.pad(packed, (0, -(-packed.size // 1024) * 1024 - packed.size))
+        gathered = lax.all_gather(packed, "shard", axis=0, tiled=False)
+        got += [gathered[:, offsets[i] : offsets[i + 1]] for i in range(len(sizes))]
     w_qkv_r = got[0].reshape(D, 3 * head_cols)
     w_out_all = got[1].reshape(D, D)
     w_out_r = lax.dynamic_slice_in_dim(w_out_all, r * head_cols, head_cols, axis=0)
-    w_up_r = got[2].reshape(D, -1)
-    w_down_r = got[3].reshape(-1, D)
-    up_bias_r = got[4].reshape(-1)
-    bias_all = unpack_cols(got[5], parts, biases.shape[1])
-    gain_all = unpack_cols(got[6], parts, norm_gains.shape[1])
+    bias_all = unpack_cols(got[2], parts, biases.shape[1])
+    gain_all = unpack_cols(got[3], parts, norm_gains.shape[1])
+    w_up_r = got[4].reshape(D, -1)
+    w_down_r = got[5].reshape(-1, D)
+    up_bias_r = got[6].reshape(-1)
     bias_q = lax.dynamic_slice_in_dim(bias_all[0], r * head_cols, head_cols)
     bias_v = lax.dynamic_slice_in_dim(bias_all[1], r * head_cols, head_cols)
 

time: 509 us -> 530 us (1.041)
  waiting for transfers between devices: 153 us -> 175 us
    all_gather x1 -> x2, waiting for transfers between devices: 82.7 us -> 110 us  [local(): gathered = lax.all_gather(packed, 'shard', axis=0, tiled=False)]
    all_gather x1 -> x2, local copies, waits for them, and re-layouts: 8.34 us -> 10.8 us  [local(): gathered = lax.all_gather(packed, 'shard', axis=0, tiled=False)]
  transfers between devices with their start and end apart: 7 -> 8, of which waited for: 4 -> 5; matrix products, arithmetic and copies ran while one was open for 20% -> 26% of each run, Pallas kernels for 19% -> 18%
where the time goes in v9:
time: 530 us; the launch traced here: 521 us
  waiting for transfers between devices  175 us (33%)
  Pallas kernels  126 us (24%)
  local copies, waits for them, and re-layouts  80.6 us (15%)
  matrix products  60.9 us (11%)
  other arithmetic  25.9 us (5%)
  starting transfers between devices  22.2 us (4%)
  between operations  15.3 us (3%)
  blocking collectives  14.2 us (3%)
    pallas_call x5, Pallas kernels, gather_rep(): pl.pallas_call(rep_gather_kernel, out_shape=jax.ShapeDtypeStruct((n * row...  126 us
    all_gather x2, waiting for transfers between devices, local(): gathered = lax.all_gather(packed, 'shard', axis=0, tiled=False)  110 us
    reduce_scatter x4, waiting for transfers between devices, scatter_rep(): return lax.psum_scatter(tensor, 'rep', scatter_dimension=0, tiled=True)  41.5 us
    all_to_all x1, waiting for transfers between devices, local(): received = lax.all_to_all(grad_pack, 'shard', 0, 0, tiled=True)  23.1 us
    all_gather x1, blocking collectives, local(): lax.all_gather(all_shares, 'rep', axis=0, tiled=False).astype(jnp.float32)  14.2 us
    dot_general x4, matrix products, matmul_rt(): lax.dot_general(first_op, second_op, (((1,), (1,)), ((), ())), preferred_...  13 us
    all_to_all x1, starting transfers between devices, local(): received = lax.all_to_all(grad_pack, 'shard', 0, 0, tiled=True)  12.3 us
    dot_general x4, matrix products, matmul(): return jnp.dot(first_op, second_op, preferred_element_type=jnp.float32)  12.2 us
  transfers between devices with their start and end apart: 8, of which 5 were waited for; matrix products, arithmetic and copies ran while one was open for 26% of the time, Pallas kernels for 18%

profile of v9, /device:TPU:1, one launch (start us, length us, event | category | flops | bytes accessed | tf_op | source)
XLA Modules:
  0.0 520.5 jit_solution(1166667899588943728)
XLA Ops:
  14.2 1.7 reshape_squeeze.25
  15.9 1.7 dynamic-slice_reduce_fusion
  19.5 20.0 %shard_map.169 = bf16[512,1152]{1,0:T(8,128)(2,1)} custom-call(bf16[128,1152]{1,0:T(8,128)(2,1)} %pad_maximum_fusion.4.x_ref), custom_call_target="tpu_custom_call" | custom-call | tf_op jit(solution)/shard_map/pallas_call | solution.py:107
  41.5 52.7 %all-gather.6.cloned.1.call-done = bf16[1867776]{0:T(1024)(128)(2,1)} async-done(((bf16[58368]{0:T(1024)(128)(2,1)}), bf16[1867776]{0:T(1024)(128)(2,1)}) %all-gather.6.cloned.1.call-update) | async-done | bytes 3735568 | tf_op jit(solution)/shard_map/all_gather | solution.py:145
  94.2 5.2 reshape.404
  101.6 1.6 reshape.369
  103.5 2.7 fusion.32
  109.3 2.4 reshape.375
  111.8 2.3 fusion.2
  116.7 2.8 fusion.44
  119.8 57.7 %all-gather.8.cloned.1.call-done = bf16[2129920]{0:T(1024)(128)(2,1)} async-done(((bf16[66560]{0:T(1024)(128)(2,1)}), bf16[2129920]{0:T(1024)(128)(2,1)}) %all-gather.8.cloned.1.call-update) | async-done | bytes 4259856 | tf_op jit(solution)/shard_map/all_gather | solution.py:145
  177.4 5.6 %reshape.405 = bf16[32,66560]{1,0:T(8,128)(2,1)} reshape(bf16[2129920]{0:T(1024)(128)(2,1)} %all-gather.8.cloned.1.call-done) | data formatting | bytes 8519680 | tf_op jit(solution)/shard_map/all_gather | solution.py:145
  183.8 3.8 fusion.82
  187.6 4.2 reshape.378
  191.8 2.4 reshape.379
  194.2 12.6 %reduce-scatter.5.cloned.1.call-done = f32[128,1024]{1,0:T(8,128)} async-done(((f32[512,1024]{1,0:T(8,128)}), f32[128,1024]{1,0:T(8,128)}) %reduce-scatter.5.cloned.1.call-update) | async-done | bytes 524304 | tf_op jit(solution)/shard_map/reduce_scatter | solution.py:118
  209.1 16.0 %shard_map.170 = bf16[512,1024]{1,0:T(8,128)(2,1)} custom-call(bf16[128,1024]{1,0:T(8,128)(2,1)} %fusion.41.x_ref), custom_call_target="tpu_custom_call" | custom-call | tf_op jit(solution)/shard_map/pallas_call | solution.py:107
  225.1 4.1 multiply_convert_fusion.1
  230.2 2.6 fusion.89
  233.1 28.9 %reduce-scatter.7.cloned.1.call-done = f32[128,1024]{1,0:T(8,128)} async-done(((f32[512,1024]{1,0:T(8,128)}), f32[128,1024]{1,0:T(8,128)}) %reduce-scatter.7.cloned.1.call-update) | async-done | bytes 524304 | tf_op jit(solution)/shard_map/reduce_scatter | solution.py:118
  265.6 16.0 %shard_map.171 = bf16[512,1024]{1,0:T(8,128)(2,1)} custom-call(bf16[128,1024]{1,0:T(8,128)(2,1)} %convert_element_type.197.x_ref), custom_call_target="tpu_custom_call" | custom-call | tf_op jit(solution)/shard_map/pallas_call | solution.py:107
  281.6 4.6 fusion.88
  287.2 2.6 fusion.39
  291.6 21.9 %shard_map.173 = bf16[2048,256]{1,0:T(8,128)(2,1)} custom-call(bf16[512,256]{1,0:T(8,128)(2,1)} %copy.72.x_ref), custom_call_target="tpu_custom_call" | custom-call | tf_op jit(solution)/shard_map/pallas_call | solution.py:107
  313.5 2.3 copy.73
  315.7 2.6 convolution_convert_fusion
  318.4 3.3 concatenate.37
  321.7 4.2 convolution_convert_fusion.1
  325.9 4.5 concatenate.36
  330.4 4.6 pad_maximum_fusion
  335.0 9.3 %all-to-all-start.1 = ((bf16[32,8,8192]{2,1,0:T(8,128)(2,1)}), bf16[32,8,8192]{2,1,0:T(8,128)(2,1)}, u32[]{:S(2)}, u32[]{:S(2)}) async-start(bf16[32,8,8192]{2,1,0:T(8,128)(2,1)} %pad_maximum_fusion), calls=%async_computation.5 | async-start | bytes 8388608 | tf_op jit(solution)/shard_map/all_to_all | solution.py:210
  347.2 52.4 %shard_map.172 = bf16[512,1024]{1,0:T(8,128)(2,1)} custom-call(bf16[128,1024]{1,0:T(8,128)(2,1)} %convert_element_type.199.x_ref), custom_call_target="tpu_custom_call" | custom-call | tf_op jit(solution)/shard_map/pallas_call | solution.py:107
  399.6 1.8 convolution_convert_fusion.4
  401.5 2.8 fusion.90
  406.3 7.4 %fusion.28 = bf16[4,64,512]{2,1,0:T(8,128)(2,1)S(1)} fusion(bf16[512,4,64]{0,2,1:T(8,128)(2,1)S(1)} %bitcast.123, f32[4,512,512]{1,2,0:T(8,128)} %fusion.90, f32[4,512,512]{1,2,0:T(8,128)} %copy-done.23, f32[4,512]{1,0:T(4,128)S(1)} %log.8, pred[512,512]{0,1:T(8,128)(4,1)S(1)} %copy-done.15), kind=kOutput, calls=%fused_computation.32 | convolution fusion | flops 145885696 | bytes 9183232 | tf_op jit(solution)/shard_map/shqk,sqhe->skhe/dot_general | solution.py:237
  413.8 9.5 %fusion.85 = (bf16[4,64]{1,0:T(4,128)(2,1)S(1)}, bf16[1,512,4,64]{1,3,2,0:T(8,128)(2,1)}) fusion(bf16[512,4,64]{0,2,1:T(8,128)(2,1)S(1)} %bitcast.121, f32[4,512,512]{1,2,0:T(8,128)} %fusion.90, f32[4,512]{1,0:T(4,128)S(1)} %log.8, f32[4,512,512]{1,2,0:T(8,128)} %copy-done.23, pred[512,512]{0,1:T(8,128)(4,1)S(1)} %copy-done.15), kind=kOutput, calls=%fused_computation.151 | convolution fusion | flops 146016512 | bytes 9183744 | tf_op jit(solution)/shard_map/shqk,skhe->sqhe/dot_general | solution.py:234
  423.2 3.1 convolution_convert_fusion.2
  426.4 2.8 reshape.384
  434.1 1.6 copy.87
  435.7 12.3 %all-to-all-start = ((bf16[32,8,4224]{2,1,0:T(8,128)(2,1)}), bf16[32,8,4224]{2,1,0:T(8,128)(2,1)S(1)}, u32[]{:S(2)}, u32[]{:S(2)}) async-start(bf16[32,8,4224]{2,1,0:T(8,128)(2,1)} %bitcast.48), calls=%async_computation.4 | async-start | bytes 4325376 | tf_op jit(solution)/shard_map/all_to_all | solution.py:270
  448.3 2.8 reduce_sum.242
  451.2 4.0 fusion.46
  455.1 23.1 %all-to-all-done = bf16[32,8,4224]{2,1,0:T(8,128)(2,1)S(1)} async-done(((bf16[32,8,4224]{2,1,0:T(8,128)(2,1)}), bf16[32,8,4224]{2,1,0:T(8,128)(2,1)S(1)}, u32[]{:S(2)}, u32[]{:S(2)}) %all-to-all-start) | async-done | bytes 2162720 | tf_op jit(solution)/shard_map/all_to_all | solution.py:270
  478.7 14.2 %all-gather.2 = bf16[397312]{0:T(1024)(128)(2,1)} all-gather(bf16[99328]{0:T(1024)(128)(2,1)S(1)} %pad_maximum_fusion.5), channel_id=4, replica_groups=mesh['rep'=4,'shard'=32] {'rep'}, dimensions={0}, use_global_device_ids=true | all-gather | bytes 993280 | tf_op jit(solution)/shard_map/all_gather | solution.py:273
  492.9 1.8 reshape.407
  498.7 3.1 copy.90
  501.8 4.5 broadcast_in_dim_reshape.20
  511.3 1.9 add_bitcast_fusion
  (201 shorter events, 49.3 us)
Async XLA Ops:
  7.2 7.0 %copy-start = (bf16[1,128,1024]{2,1,0:T(8,128)(2,1)S(1)}, bf16[1,128,1024]{2,1,0:T(8,128)(2,1)}, u32[]{:S(2)}) copy-start(bf16[1,128,1024]{2,1,0:T(8,128)(2,1)} %param.16) | copy-start | bytes 786436
  7.2 87.0 %all-gather.6.cloned.1.call-start = ((), (), s32[]{:S(2)}) async-start(), calls=%async_computation.10 | async-start | bytes 3852288 | tf_op jit(solution)/shard_map/all_gather | solution.py:145
  8.3 10.3 %copy-start.19 = (s32[1,128]{1,0:T(1,128)S(1)}, s32[1,128]{1,0:T(1,128)}, u32[]{:S(2)}) copy-start(s32[1,128]{1,0:T(1,128)} %param.11) | copy-start | bytes 1540
  8.4 10.3 %copy-start.8 = (f32[1,128,1024]{2,1,0:T(8,128)S(1)}, f32[1,128,1024]{2,1,0:T(8,128)}, u32[]{:S(2)}) copy-start(f32[1,128,1024]{2,1,0:T(8,128)} %param.10) | copy-start | bytes 1572868
  12.2 165.2 %all-gather.8.cloned.1.call-start = ((), (), s32[]{:S(2)}) async-start(), calls=%async_computation.11 | async-start | bytes 4392960 | tf_op jit(solution)/shard_map/all_gather | solution.py:145
  18.5 188.3 %reduce-scatter.5.cloned.1.call-start = ((), (), s32[]{:S(2)}) async-start(), calls=%async_computation.6 | async-start | bytes 2621440 | tf_op jit(solution)/shard_map/reduce_scatter | solution.py:118
  100.2 0.7 slice-start
  100.2 1.4 slice-start.1
  106.2 3.0 slice-start.2
  109.2 2.5 copy-start.16
  109.2 2.5 copy-start.14
  114.0 2.0 copy-start.23
  116.0 0.7 copy-start.12
  119.6 142.4 %reduce-scatter.7.cloned.1.call-start = ((), (), s32[]{:S(2)}) async-start(), calls=%async_computation.7 | async-start | bytes 2621440 | tf_op jit(solution)/shard_map/reduce_scatter | solution.py:118
  194.2 30.9 %copy-start.5 = (bf16[1024,1024]{1,0:T(8,128)(2,1)S(1)}, bf16[1024,1024]{1,0:T(8,128)(2,1)}, u32[]{:S(2)}) copy-start(bf16[1024,1024]{1,0:T(8,128)(2,1)} %reshape.378) | copy-start | bytes 6291460
  225.1 5.1 copy-start.7
  229.2 1.0 copy-start.25
  232.8 30.7 %copy-start.3 = (f32[1,128,1024]{2,1,0:T(8,128)S(1)}, f32[1,128,1024]{2,1,0:T(8,128)}, u32[]{:S(2)}) copy-start(f32[1,128,1024]{2,1,0:T(8,128)} %param.12) | copy-start | bytes 1572868
  232.8 112.1 %reduce-scatter.9.cloned.1.call-start = ((), (), s32[]{:S(2)}) async-start(), calls=%async_computation.8 | async-start | bytes 2621440 | tf_op jit(solution)/shard_map/reduce_scatter | solution.py:118
  281.6 5.6 %copy-start.6 = (bf16[1024,1024]{1,0:T(8,128)(2,1)S(1)}, bf16[1024,1024]{1,0:T(8,128)(2,1)}, u32[]{:S(2)}) copy-start(bf16[1024,1024]{1,0:T(8,128)(2,1)} %reshape.378) | copy-start | bytes 6291460
  286.2 1.0 copy-start.27
  289.8 0.9 copy-start.13
  289.9 25.9 %copy-start.11 = (bf16[512,1024]{1,0:T(8,128)(2,1)S(1)}, bf16[512,1024]{1,0:T(8,128)(2,1)}, u32[]{:S(2)}) copy-start(bf16[512,1024]{1,0:T(8,128)(2,1)} %shard_map.171) | copy-start | bytes 3145732
  291.6 24.2 %copy-start.26 = (bf16[512,1024]{1,0:T(8,128)(2,1)S(1)}, bf16[512,1024]{1,0:T(8,128)(2,1)}, u32[]{:S(2)}) copy-start(bf16[512,1024]{1,0:T(8,128)(2,1)} %copy-done.25) | copy-start | bytes 3145732
  335.0 100.7 %all-to-all-start.1 = ((bf16[32,8,8192]{2,1,0:T(8,128)(2,1)}), bf16[32,8,8192]{2,1,0:T(8,128)(2,1)}, u32[]{:S(2)}, u32[]{:S(2)}) async-start(bf16[32,8,8192]{2,1,0:T(8,128)(2,1)} %pad_maximum_fusion), calls=%async_computation.5 | async-start | bytes 8388608 | tf_op jit(solution)/shard_map/all_to_all | solution.py:210
  401.5 2.9 copy-start.15
  401.5 3.6 copy-start.24
  405.1 1.1 copy-start.18
  406.3 17.0 %copy-start.20 = (bf16[1,512,4,64]{1,3,2,0:T(8,128)(2,1)}, bf16[1,512,4,64]{1,3,2,0:T(8,128)(2,1)S(1)}, u32[]{:S(2)}) copy-start(bf16[1,512,4,64]{1,3,2,0:T(8,128)(2,1)S(1)} %get-tuple-element.41) | copy-start | bytes 786436
  406.3 7.5 %copy-start.17 = (bf16[512,256]{0,1:T(8,128)(2,1)S(1)}, bf16[512,256]{0,1:T(8,128)(2,1)}, u32[]{:S(2)}) copy-start(bf16[512,256]{0,1:T(8,128)(2,1)} %copy-done.16) | copy-start | bytes 786436
  413.7 9.5 %copy-start.22 = (bf16[4,64,512]{2,1,0:T(8,128)(2,1)}, bf16[4,64,512]{2,1,0:T(8,128)(2,1)S(1)}, u32[]{:S(2)}) copy-start(bf16[4,64,512]{2,1,0:T(8,128)(2,1)S(1)} %fusion.28) | copy-start | bytes 786436
  413.7 9.5 %copy-start.10 = (bf16[512,1152]{1,0:T(8,128)(2,1)S(1)}, bf16[512,1152]{1,0:T(8,128)(2,1)}, u32[]{:S(2)}) copy-start(bf16[512,1152]{1,0:T(8,128)(2,1)} %shard_map.169) | copy-start | bytes 3538948
  426.4 2.8 copy-start.4
  435.7 42.6 %all-to-all-start = ((bf16[32,8,4224]{2,1,0:T(8,128)(2,1)}), bf16[32,8,4224]{2,1,0:T(8,128)(2,1)S(1)}, u32[]{:S(2)}, u32[]{:S(2)}) async-start(bf16[32,8,4224]{2,1,0:T(8,128)(2,1)} %bitcast.48), calls=%async_computation.4 | async-start | bytes 4325376 | tf_op jit(solution)/shard_map/all_to_all | solution.py:270
  448.0 3.1 copy-start.21
  448.0 63.3 %reduce-scatter.11.cloned.1.call-start = ((), (), s32[]{:S(2)}) async-start(), calls=%async_computation.9 | async-start | bytes 2621440 | tf_op jit(solution)/shard_map/reduce_scatter | solution.py:118
  494.8 3.2 copy-start.2
  501.8 4.5 copy-start.9
  501.8 11.5 %copy-start.1 = (bf16[1,128,1024]{2,1,0:T(8,128)(2,1)S(1)}, bf16[1,128,1024]{2,1,0:T(8,128)(2,1)}, u32[]{:S(2)}) copy-start(bf16[1,128,1024]{2,1,0:T(8,128)(2,1)} %param.16) | copy-start | bytes 786436
Sparse Core Ops, SparseCore 0:
  12.3 81.8 all-gather.5
  97.7 79.6 all-gather.7
  179.8 26.9 reduce-scatter.4
  233.0 28.9 reduce-scatter.6
  289.9 34.5 reduce-scatter.8
  455.3 41.9 reduce-scatter.10

commit v10 on v8

--- a/solution.py
+++ b/solution.py
@@ -75,30 +75,45 @@
 
 
 def rep_gather_kernel(x_ref, o_ref, send_sem, recv_sem):
-    n = lax.axis_size("rep")
     me = lax.axis_index("rep")
     rows = x_ref.shape[0]
+    other_chip = lax.rem(me + 2, 4)
+    other_core = me + 1 - 2 * lax.rem(me, 2)
     o_ref[pl.ds(me * rows, rows), :] = x_ref[...]
     barrier = pltpu.get_barrier_semaphore()
-    for k in range(1, n):
-        pl.semaphore_signal(
-            barrier, inc=1, device_id={"rep": lax.rem(me + k, n)}, device_id_type=pl.DeviceIdType.MESH
-        )
-    pl.semaphore_wait(barrier, n - 1)
-    copies = []
-    for k in range(1, n):
-        copy = pltpu.make_async_remote_copy(
-            src_ref=x_ref,
-            dst_ref=o_ref.at[pl.ds(me * rows, rows)],
-            send_sem=send_sem.at[k - 1],
-            recv_sem=recv_sem.at[k - 1],
-            device_id={"rep": lax.rem(me + k, n)},
-            device_id_type=pl.DeviceIdType.MESH,
-        )
-        copy.start()
-        copies.append(copy)
-    for copy in copies:
-        copy.wait()
+    for peer in (other_chip, other_core):
+        pl.semaphore_signal(barrier, inc=1, device_id={"rep": peer}, device_id_type=pl.DeviceIdType.MESH)
+    pl.semaphore_wait(barrier, 2)
+    cross = pltpu.make_async_remote_copy(
+        src_ref=x_ref,
+        dst_ref=o_ref.at[pl.ds(me * rows, rows)],
+        send_sem=send_sem.at[0],
+        recv_sem=recv_sem.at[0],
+        device_id={"rep": other_chip},
+        device_id_type=pl.DeviceIdType.MESH,
+    )
+    cross.start()
+    own = pltpu.make_async_remote_copy(
+        src_ref=x_ref,
+        dst_ref=o_ref.at[pl.ds(me * rows, rows)],
+        send_sem=send_sem.at[1],
+        recv_sem=recv_sem.at[1],
+        device_id={"rep": other_core},
+        device_id_type=pl.DeviceIdType.MESH,
+    )
+    own.start()
+    cross.wait()
+    relay = pltpu.make_async_remote_copy(
+        src_ref=o_ref.at[pl.ds(other_chip * rows, rows)],
+        dst_ref=o_ref.at[pl.ds(other_chip * rows, rows)],
+        send_sem=send_sem.at[2],
+        recv_sem=recv_sem.at[2],
+        device_id={"rep": other_core},
+        device_id_type=pl.DeviceIdType.MESH,
+    )
+    relay.start()
+    own.wait()
+    relay.wait()
 
 
 def gather_rep(tensor, cid=1):

time: 509 us -> 486 us (0.955)
  Pallas kernels: 127 us -> 97.6 us
    pallas_call x5, Pallas kernels: 127 us -> 97.6 us  [gather_rep(): pl.pallas_call(rep_gather_kernel, out_shape=jax.ShapeDtypeStruct((n * row...]
    all_gather x1, waiting for transfers between devices: 82.7 us -> 88.2 us  [local(): gathered = lax.all_gather(packed, 'shard', axis=0, tiled=False)]
  transfers between devices with their start and end apart: 7 -> 7, of which waited for: 4 -> 4; matrix products, arithmetic and copies ran while one was open for 20% -> 21% of each run, Pallas kernels for 19% -> 16%
where the time goes in v10:
time: 486 us; the launch traced here: 477 us
  waiting for transfers between devices  157 us (32%)
  Pallas kernels  97.6 us (20%)
  local copies, waits for them, and re-layouts  80.5 us (17%)
  matrix products  62.4 us (13%)
  other arithmetic  25.9 us (5%)
  starting transfers between devices  22.9 us (5%)
  blocking collectives  15.4 us (3%)
  between operations  14.9 us (3%)
    pallas_call x5, Pallas kernels, gather_rep(): pl.pallas_call(rep_gather_kernel, out_shape=jax.ShapeDtypeStruct((n * row...  97.6 us
    all_gather x1, waiting for transfers between devices, local(): gathered = lax.all_gather(packed, 'shard', axis=0, tiled=False)  88.2 us
    reduce_scatter x4, waiting for transfers between devices, scatter_rep(): return lax.psum_scatter(tensor, 'rep', scatter_dimension=0, tiled=True)  46.6 us
    all_to_all x1, waiting for transfers between devices, local(): received = lax.all_to_all(grad_pack, 'shard', 0, 0, tiled=True)  22.1 us
    all_gather x1, blocking collectives, local(): lax.all_gather(all_shares, 'rep', axis=0, tiled=False).astype(jnp.float32)  15.4 us
    dot_general x4, matrix products, matmul(): return jnp.dot(first_op, second_op, preferred_element_type=jnp.float32)  13.4 us
    all_to_all x1, starting transfers between devices, local(): received = lax.all_to_all(grad_pack, 'shard', 0, 0, tiled=True)  13.1 us
    dot_general x4, matrix products, matmul_rt(): lax.dot_general(first_op, second_op, (((1,), (1,)), ((), ())), preferred_...  13 us
  transfers between devices with their start and end apart: 7, of which 4 were waited for; matrix products, arithmetic and copies ran while one was open for 21% of the time, Pallas kernels for 16%

profile of v10, /device:TPU:1, one launch (start us, length us, event | category | flops | bytes accessed | tf_op | source)
XLA Modules:
  0.0 476.7 jit_solution(4557733945616586200)
XLA Ops:
  9.7 1.7 reshape_squeeze.23
  11.4 1.7 dynamic-slice_reduce_fusion
  17.1 14.2 %shard_map.169 = bf16[512,1152]{1,0:T(8,128)(2,1)} custom-call(bf16[128,1152]{1,0:T(8,128)(2,1)} %pad_maximum_fusion.4.x_ref), custom_call_target="tpu_custom_call" | custom-call | tf_op jit(solution)/shard_map/pallas_call | solution.py:122
  33.3 88.2 %all-gather.4.cloned.1.call-done = bf16[3964928]{0:T(1024)(128)(2,1)} async-done(((bf16[123904]{0:T(1024)(128)(2,1)}), bf16[3964928]{0:T(1024)(128)(2,1)}) %all-gather.4.cloned.1.call-update) | async-done | bytes 7929872 | tf_op jit(solution)/shard_map/all_gather | solution.py:157
  121.6 8.3 %reshape.404 = bf16[32,123904]{1,0:T(8,128)(2,1)} reshape(bf16[3964928]{0:T(1024)(128)(2,1)} %all-gather.4.cloned.1.call-done) | data formatting | bytes 15859712 | tf_op jit(solution)/shard_map/all_gather | solution.py:157
  130.7 5.7 %fusion.77 = (bf16[32,32768]{1,0:T(8,128)(2,1)}, bf16[32,32768]{1,0:T(8,128)(2,1)}, bf16[32,32768]{1,0:T(8,128)(2,1)}) fusion(bf16[32,123904]{1,0:T(8,128)(2,1)} %reshape.404), kind=kLoop, calls=%fused_computation.142 | loop fusion | bytes 12582912 | tf_op jit(solution)/shard_map/slice | solution.py:158
  136.6 1.7 reshape.370
  138.3 3.9 fusion.32
  143.7 2.0 fusion.34
  147.8 2.4 reshape.376
  150.2 2.3 fusion.2
  155.2 2.9 fusion.44
  160.5 4.4 reshape.378
  164.9 2.3 reshape.379
  167.2 17.7 %reduce-scatter.5.cloned.1.call-done = f32[128,1024]{1,0:T(8,128)} async-done(((f32[512,1024]{1,0:T(8,128)}), f32[128,1024]{1,0:T(8,128)}) %reduce-scatter.5.cloned.1.call-update) | async-done | bytes 524304 | tf_op jit(solution)/shard_map/reduce_scatter | solution.py:133
  187.2 11.8 %shard_map.170 = bf16[512,1024]{1,0:T(8,128)(2,1)} custom-call(bf16[128,1024]{1,0:T(8,128)(2,1)} %fusion.41.x_ref), custom_call_target="tpu_custom_call" | custom-call | tf_op jit(solution)/shard_map/pallas_call | solution.py:122
  199.0 4.0 multiply_convert_fusion.1
  204.0 2.6 fusion.84
  206.9 28.9 %reduce-scatter.7.cloned.1.call-done = f32[128,1024]{1,0:T(8,128)} async-done(((f32[512,1024]{1,0:T(8,128)}), f32[128,1024]{1,0:T(8,128)}) %reduce-scatter.7.cloned.1.call-update) | async-done | bytes 524304 | tf_op jit(solution)/shard_map/reduce_scatter | solution.py:133
  239.4 11.8 %shard_map.171 = bf16[512,1024]{1,0:T(8,128)(2,1)} custom-call(bf16[128,1024]{1,0:T(8,128)(2,1)} %convert_element_type.195.x_ref), custom_call_target="tpu_custom_call" | custom-call | tf_op jit(solution)/shard_map/pallas_call | solution.py:122
  251.2 4.6 fusion.83
  256.8 2.6 fusion.39
  261.2 11.8 %shard_map.173 = bf16[2048,256]{1,0:T(8,128)(2,1)} custom-call(bf16[512,256]{1,0:T(8,128)(2,1)} %copy.72.x_ref), custom_call_target="tpu_custom_call" | custom-call | tf_op jit(solution)/shard_map/pallas_call | solution.py:122
  273.0 2.3 copy.73
  275.3 2.7 convolution_convert_fusion
  278.0 3.3 concatenate.33
  281.3 4.2 convolution_convert_fusion.1
  285.6 4.5 concatenate.32
  290.1 4.6 pad_maximum_fusion
  294.7 9.2 %all-to-all-start.1 = ((bf16[32,8,8192]{2,1,0:T(8,128)(2,1)}), bf16[32,8,8192]{2,1,0:T(8,128)(2,1)}, u32[]{:S(2)}, u32[]{:S(2)}) async-start(bf16[32,8,8192]{2,1,0:T(8,128)(2,1)} %pad_maximum_fusion), calls=%async_computation.5 | async-start | bytes 8388608 | tf_op jit(solution)/shard_map/all_to_all | solution.py:222
  306.9 47.9 %shard_map.172 = bf16[512,1024]{1,0:T(8,128)(2,1)} custom-call(bf16[128,1024]{1,0:T(8,128)(2,1)} %convert_element_type.197.x_ref), custom_call_target="tpu_custom_call" | custom-call | tf_op jit(solution)/shard_map/pallas_call | solution.py:122
  354.8 1.8 convolution_convert_fusion.4
  356.7 2.8 fusion.85
  361.5 7.7 %fusion.28 = bf16[4,64,512]{2,1,0:T(8,128)(2,1)S(1)} fusion(bf16[512,4,64]{0,2,1:T(8,128)(2,1)S(1)} %bitcast.124, f32[4,512,512]{1,2,0:T(8,128)} %fusion.85, f32[4,512,512]{1,2,0:T(8,128)} %copy-done.28, f32[4,512]{1,0:T(4,128)S(1)} %log.8, pred[512,512]{0,1:T(8,128)(4,1)S(1)} %copy-done.17), kind=kOutput, calls=%fused_computation.32 | convolution fusion | flops 145885696 | bytes 9183232 | tf_op jit(solution)/shard_map/shqk,sqhe->skhe/dot_general | solution.py:249
  369.2 9.5 %fusion.80 = (bf16[4,64]{1,0:T(4,128)(2,1)S(1)}, bf16[1,512,4,64]{1,3,2,0:T(8,128)(2,1)}) fusion(bf16[512,4,64]{0,2,1:T(8,128)(2,1)S(1)} %bitcast.122, f32[4,512,512]{1,2,0:T(8,128)} %fusion.85, f32[4,512]{1,0:T(4,128)S(1)} %log.8, f32[4,512,512]{1,2,0:T(8,128)} %copy-done.28, pred[512,512]{0,1:T(8,128)(4,1)S(1)} %copy-done.17), kind=kOutput, calls=%fused_computation.145 | convolution fusion | flops 146016512 | bytes 9183744 | tf_op jit(solution)/shard_map/shqk,skhe->sqhe/dot_general | solution.py:246
  378.8 3.1 convolution_convert_fusion.2
  381.9 2.8 reshape.384
  387.3 1.5 constant_dynamic-update-slice_fusion.8
  389.6 1.6 copy.87
  391.2 13.1 %all-to-all-start = ((bf16[32,8,4224]{2,1,0:T(8,128)(2,1)}), bf16[32,8,4224]{2,1,0:T(8,128)(2,1)S(1)}, u32[]{:S(2)}, u32[]{:S(2)}) async-start(bf16[32,8,4224]{2,1,0:T(8,128)(2,1)} %bitcast.48), calls=%async_computation.4 | async-start | bytes 4325376 | tf_op jit(solution)/shard_map/all_to_all | solution.py:282
  404.6 2.8 reduce_sum.242
  407.4 3.9 fusion.46
  411.4 22.1 %all-to-all-done = bf16[32,8,4224]{2,1,0:T(8,128)(2,1)S(1)} async-done(((bf16[32,8,4224]{2,1,0:T(8,128)(2,1)}), bf16[32,8,4224]{2,1,0:T(8,128)(2,1)S(1)}, u32[]{:S(2)}, u32[]{:S(2)}) %all-to-all-start) | async-done | bytes 2162720 | tf_op jit(solution)/shard_map/all_to_all | solution.py:282
  433.9 15.4 %all-gather.1 = bf16[397312]{0:T(1024)(128)(2,1)} all-gather(bf16[99328]{0:T(1024)(128)(2,1)S(1)} %pad_maximum_fusion.5), channel_id=3, replica_groups=mesh['rep'=4,'shard'=32] {'rep'}, dimensions={0}, use_global_device_ids=true | all-gather | bytes 993280 | tf_op jit(solution)/shard_map/all_gather | solution.py:285
  449.3 1.8 reshape.406
  455.0 3.1 copy.90
  458.2 4.5 broadcast_in_dim_reshape.20
  467.8 1.9 add_bitcast_fusion
  (203 shorter events, 45.8 us)
Async XLA Ops:
  7.2 6.1 %copy-start = (bf16[1,128,1024]{2,1,0:T(8,128)(2,1)S(1)}, bf16[1,128,1024]{2,1,0:T(8,128)(2,1)}, u32[]{:S(2)}) copy-start(bf16[1,128,1024]{2,1,0:T(8,128)(2,1)} %param.16) | copy-start | bytes 786436
  7.2 6.7 %copy-start.22 = (bf16[1,128]{1,0:T(2,128)(2,1)S(1)}, bf16[1,128]{1,0:T(2,128)(2,1)}, u32[]{:S(2)}) copy-start(bf16[1,128]{1,0:T(2,128)(2,1)} %param.19) | copy-start | bytes 772
  7.2 7.4 %copy-start.21 = (bf16[1,6,32]{2,1,0:T(8,128)(2,1)S(1)}, bf16[1,6,32]{2,1,0:T(8,128)(2,1)}, u32[]{:S(2)}) copy-start(bf16[1,6,32]{2,1,0:T(8,128)(2,1)} %param.17) | copy-start | bytes 1156
  7.2 7.5 %copy-start.23 = (bf16[1,2,32]{2,1,0:T(2,128)(2,1)S(1)}, bf16[1,2,32]{2,1,0:T(2,128)(2,1)}, u32[]{:S(2)}) copy-start(bf16[1,2,32]{2,1,0:T(2,128)(2,1)} %param.18) | copy-start | bytes 388
  7.2 114.4 %all-gather.4.cloned.1.call-start = ((), (), s32[]{:S(2)}) async-start(), calls=%async_computation.10 | async-start | bytes 8177664 | tf_op jit(solution)/shard_map/all_gather | solution.py:157
  8.7 7.5 %copy-start.24 = (s32[1,128]{1,0:T(1,128)S(1)}, s32[1,128]{1,0:T(1,128)}, u32[]{:S(2)}) copy-start(s32[1,128]{1,0:T(1,128)} %param.11) | copy-start | bytes 1540
  8.7 7.6 %copy-start.10 = (f32[1,128,1024]{2,1,0:T(8,128)S(1)}, f32[1,128,1024]{2,1,0:T(8,128)}, u32[]{:S(2)}) copy-start(f32[1,128,1024]{2,1,0:T(8,128)} %param.10) | copy-start | bytes 1572868
  16.2 168.7 %reduce-scatter.5.cloned.1.call-start = ((), (), s32[]{:S(2)}) async-start(), calls=%async_computation.6 | async-start | bytes 2621440 | tf_op jit(solution)/shard_map/reduce_scatter | solution.py:133
  130.7 5.9 %slice-start = ((bf16[32,123904]{1,0:T(8,128)(2,1)}), bf16[32,24576]{1,0:T(8,128)(2,1)S(1)}, s32[]{:S(2)}) async-start(bf16[32,123904]{1,0:T(8,128)(2,1)} %reshape.404), calls=%async_computation.11 | async-start | bytes 3145728 | tf_op jit(solution)/shard_map/slice | solution.py:158
  142.1 5.7 %copy-start.3 = (bf16[32,32768]{1,0:T(8,128)(2,1)S(1)}, bf16[32,32768]{1,0:T(8,128)(2,1)}, u32[]{:S(2)}) copy-start(bf16[32,32768]{1,0:T(8,128)(2,1)} %get-tuple-element.35) | copy-start | bytes 6291460
  147.8 2.4 copy-start.18
  147.8 2.4 copy-start.16
  152.5 2.0 copy-start.28
  154.5 0.7 copy-start.14
  158.1 77.7 %reduce-scatter.7.cloned.1.call-start = ((), (), s32[]{:S(2)}) async-start(), calls=%async_computation.7 | async-start | bytes 2621440 | tf_op jit(solution)/shard_map/reduce_scatter | solution.py:133
  160.5 4.4 copy-start.2
  167.2 31.8 %copy-start.7 = (bf16[1024,1024]{1,0:T(8,128)(2,1)S(1)}, bf16[1024,1024]{1,0:T(8,128)(2,1)}, u32[]{:S(2)}) copy-start(bf16[1024,1024]{1,0:T(8,128)(2,1)} %reshape.378) | copy-start | bytes 6291460
  199.0 5.0 %copy-start.9 = (bf16[1024,1024]{1,0:T(8,128)(2,1)S(1)}, bf16[1024,1024]{1,0:T(8,128)(2,1)}, u32[]{:S(2)}) copy-start(bf16[1024,1024]{1,0:T(8,128)(2,1)} %reshape.379) | copy-start | bytes 6291460
  203.1 1.0 copy-start.30
  206.6 30.8 %copy-start.5 = (f32[1,128,1024]{2,1,0:T(8,128)S(1)}, f32[1,128,1024]{2,1,0:T(8,128)}, u32[]{:S(2)}) copy-start(f32[1,128,1024]{2,1,0:T(8,128)} %param.12) | copy-start | bytes 1572868
  206.6 98.0 %reduce-scatter.9.cloned.1.call-start = ((), (), s32[]{:S(2)}) async-start(), calls=%async_computation.8 | async-start | bytes 2621440 | tf_op jit(solution)/shard_map/reduce_scatter | solution.py:133
  251.2 5.6 %copy-start.8 = (bf16[1024,1024]{1,0:T(8,128)(2,1)S(1)}, bf16[1024,1024]{1,0:T(8,128)(2,1)}, u32[]{:S(2)}) copy-start(bf16[1024,1024]{1,0:T(8,128)(2,1)} %reshape.378) | copy-start | bytes 6291460
  255.8 1.0 copy-start.32
  259.4 0.9 copy-start.15
  259.5 15.8 %copy-start.13 = (bf16[512,1024]{1,0:T(8,128)(2,1)S(1)}, bf16[512,1024]{1,0:T(8,128)(2,1)}, u32[]{:S(2)}) copy-start(bf16[512,1024]{1,0:T(8,128)(2,1)} %shard_map.171) | copy-start | bytes 3145732
  261.2 14.1 %copy-start.31 = (bf16[512,1024]{1,0:T(8,128)(2,1)S(1)}, bf16[512,1024]{1,0:T(8,128)(2,1)}, u32[]{:S(2)}) copy-start(bf16[512,1024]{1,0:T(8,128)(2,1)} %copy-done.30) | copy-start | bytes 3145732
  294.7 96.5 %all-to-all-start.1 = ((bf16[32,8,8192]{2,1,0:T(8,128)(2,1)}), bf16[32,8,8192]{2,1,0:T(8,128)(2,1)}, u32[]{:S(2)}, u32[]{:S(2)}) async-start(bf16[32,8,8192]{2,1,0:T(8,128)(2,1)} %pad_maximum_fusion), calls=%async_computation.5 | async-start | bytes 8388608 | tf_op jit(solution)/shard_map/all_to_all | solution.py:222
  356.7 2.9 copy-start.17
  356.7 3.6 copy-start.29
  360.4 1.1 copy-start.20
  361.5 17.3 %copy-start.25 = (bf16[1,512,4,64]{1,3,2,0:T(8,128)(2,1)}, bf16[1,512,4,64]{1,3,2,0:T(8,128)(2,1)S(1)}, u32[]{:S(2)}) copy-start(bf16[1,512,4,64]{1,3,2,0:T(8,128)(2,1)S(1)} %get-tuple-element.42) | copy-start | bytes 786436
  361.5 7.7 %copy-start.19 = (bf16[512,256]{0,1:T(8,128)(2,1)S(1)}, bf16[512,256]{0,1:T(8,128)(2,1)}, u32[]{:S(2)}) copy-start(bf16[512,256]{0,1:T(8,128)(2,1)} %copy-done.18) | copy-start | bytes 786436
  369.2 9.6 %copy-start.27 = (bf16[4,64,512]{2,1,0:T(8,128)(2,1)}, bf16[4,64,512]{2,1,0:T(8,128)(2,1)S(1)}, u32[]{:S(2)}) copy-start(bf16[4,64,512]{2,1,0:T(8,128)(2,1)S(1)} %fusion.28) | copy-start | bytes 786436
  369.2 9.6 %copy-start.12 = (bf16[512,1152]{1,0:T(8,128)(2,1)S(1)}, bf16[512,1152]{1,0:T(8,128)(2,1)}, u32[]{:S(2)}) copy-start(bf16[512,1152]{1,0:T(8,128)(2,1)} %shard_map.169) | copy-start | bytes 3538948
  381.9 2.8 copy-start.6
  391.2 42.3 %all-to-all-start = ((bf16[32,8,4224]{2,1,0:T(8,128)(2,1)}), bf16[32,8,4224]{2,1,0:T(8,128)(2,1)S(1)}, u32[]{:S(2)}, u32[]{:S(2)}) async-start(bf16[32,8,4224]{2,1,0:T(8,128)(2,1)} %bitcast.48), calls=%async_computation.4 | async-start | bytes 4325376 | tf_op jit(solution)/shard_map/all_to_all | solution.py:282
  404.3 3.1 copy-start.26
  404.3 63.5 %reduce-scatter.11.cloned.1.call-start = ((), (), s32[]{:S(2)}) async-start(), calls=%async_computation.9 | async-start | bytes 2621440 | tf_op jit(solution)/shard_map/reduce_scatter | solution.py:133
  451.1 3.2 copy-start.4
  458.2 4.5 copy-start.11
  458.2 11.5 %copy-start.1 = (bf16[1,128,1024]{2,1,0:T(8,128)(2,1)S(1)}, bf16[1,128,1024]{2,1,0:T(8,128)(2,1)}, u32[]{:S(2)}) copy-start(bf16[1,128,1024]{2,1,0:T(8,128)(2,1)} %param.16) | copy-start | bytes 786436
Sparse Core Ops, SparseCore 0:
  16.3 105.2 all-gather.3
  158.2 26.6 reduce-scatter.4
  206.7 29.0 reduce-scatter.6
  259.6 28.9 reduce-scatter.8
  411.5 40.7 reduce-scatter.10

commit v11 on v10

--- a/solution.py
+++ b/solution.py
@@ -129,8 +129,61 @@
     )(tensor)
 
 
-def scatter_rep(tensor):
-    return lax.psum_scatter(tensor, "rep", scatter_dimension=0, tiled=True)
+def rep_scatter_kernel(p_ref, o_ref, onchip_buf, cross_buf, partial, send_sem, recv_sem):
+    me = lax.axis_index("rep")
+    rows = o_ref.shape[0]
+    other_chip = lax.rem(me + 2, 4)
+    other_core = me + 1 - 2 * lax.rem(me, 2)
+    diagonal = lax.rem(other_core + 2, 4)
+    barrier = pltpu.get_barrier_semaphore()
+    for peer in (other_chip, other_core):
+        pl.semaphore_signal(barrier, inc=1, device_id={"rep": peer}, device_id_type=pl.DeviceIdType.MESH)
+    pl.semaphore_wait(barrier, 2)
+    near = []
+    for slot, block in ((0, other_core), (1, diagonal)):
+        copy = pltpu.make_async_remote_copy(
+            src_ref=p_ref.at[pl.ds(block * rows, rows)],
+            dst_ref=onchip_buf.at[slot],
+            send_sem=send_sem.at[slot],
+            recv_sem=recv_sem.at[slot],
+            device_id={"rep": other_core},
+            device_id_type=pl.DeviceIdType.MESH,
+        )
+        copy.start()
+        near.append(copy)
+    for copy in near:
+        copy.wait()
+    partial[...] = p_ref[pl.ds(other_chip * rows, rows), :] + onchip_buf[1]
+    far = pltpu.make_async_remote_copy(
+        src_ref=partial,
+        dst_ref=cross_buf,
+        send_sem=send_sem.at[2],
+        recv_sem=recv_sem.at[2],
+        device_id={"rep": other_chip},
+        device_id_type=pl.DeviceIdType.MESH,
+    )
+    far.start()
+    far.wait()
+    o_ref[...] = p_ref[pl.ds(me * rows, rows), :] + onchip_buf[0] + cross_buf[...]
+
+
+def scatter_rep(tensor, cid=4):
+    n = lax.axis_size("rep")
+    rows, cols = tensor.shape[0] // n, tensor.shape[1]
+    return pl.pallas_call(
+        rep_scatter_kernel,
+        out_shape=jax.ShapeDtypeStruct((rows, cols), tensor.dtype),
+        in_specs=[pl.BlockSpec(memory_space=pltpu.VMEM)],
+        out_specs=pl.BlockSpec(memory_space=pltpu.VMEM),
+        scratch_shapes=[
+            pltpu.VMEM((2, rows, cols), tensor.dtype),
+            pltpu.VMEM((rows, cols), tensor.dtype),
+            pltpu.VMEM((rows, cols), tensor.dtype),
+            pltpu.SemaphoreType.DMA((3,)),
+            pltpu.SemaphoreType.DMA((3,)),
+        ],
+        compiler_params=pltpu.CompilerParams(collective_id=cid, has_side_effects=True),
+    )(tensor)
 
 
 def local(inputs, segment_ids, cotangent, w_qkv, w_out, w_up, w_down, biases, norm_gains, up_bias):

time: 486 us -> 479 us (0.986)
  Pallas kernels: 97.6 us -> 172 us
  waiting for transfers between devices: 157 us -> 95 us
  starting transfers between devices: 22.9 us -> 12.1 us
  blocking collectives: 15.4 us -> 10.2 us
    pallas_call x0 -> x4, Pallas kernels: none -> 111 us  [scatter_rep(): pl.pallas_call(rep_scatter_kernel, out_shape=jax.ShapeDtypeStruct((rows,...]
    reduce_scatter x4 -> x0, waiting for transfers between devices: 46.6 us -> none  [scatter_rep(): return lax.psum_scatter(tensor, 'rep', scatter_dimension=0, tiled=True)]
    pallas_call x5, Pallas kernels: 97.6 us -> 61.4 us  [gather_rep(): pl.pallas_call(rep_gather_kernel, out_shape=jax.ShapeDtypeStruct((n * row...]
    all_to_all x1, waiting for transfers between devices: 22.1 us -> 6.82 us  [local(): received = lax.all_to_all(grad_pack, 'shard', 0, 0, tiled=True)]
    all_to_all x1, starting transfers between devices: 13.1 us -> 6.28 us  [local(): received = lax.all_to_all(grad_pack, 'shard', 0, 0, tiled=True)]
    all_gather x1, blocking collectives: 15.4 us -> 10.2 us  [local(): lax.all_gather(all_shares, 'rep', axis=0, tiled=False).astype(jnp.float32)]
    unnamed x81 -> x73, local copies, waits for them, and re-layouts: 9.99 us -> 7.4 us
  transfers between devices with their start and end apart: 7 -> 3, of which waited for: 4 -> 2; matrix products, arithmetic and copies ran while one was open for 21% -> 7% of each run, Pallas kernels for 16% -> 14%
where the time goes in v11:
time: 479 us; the launch traced here: 473 us
  Pallas kernels  172 us (36%)
  waiting for transfers between devices  95 us (20%)
  local copies, waits for them, and re-layouts  79.7 us (17%)
  matrix products  64.2 us (13%)
  other arithmetic  24.3 us (5%)
  between operations  15.1 us (3%)
  starting transfers between devices  12.1 us (3%)
  blocking collectives  10.2 us (2%)
    pallas_call x4, Pallas kernels, scatter_rep(): pl.pallas_call(rep_scatter_kernel, out_shape=jax.ShapeDtypeStruct((rows,...  111 us
    all_gather x1, waiting for transfers between devices, local(): gathered = lax.all_gather(packed, 'shard', axis=0, tiled=False)  88.2 us
    pallas_call x5, Pallas kernels, gather_rep(): pl.pallas_call(rep_gather_kernel, out_shape=jax.ShapeDtypeStruct((n * row...  61.4 us
    dot_general x4, matrix products, matmul(): return jnp.dot(first_op, second_op, preferred_element_type=jnp.float32)  14.1 us
    dot_general x4, matrix products, matmul_rt(): lax.dot_general(first_op, second_op, (((1,), (1,)), ((), ())), preferred_...  12.9 us
    dot_general x3, matrix products, matmul_lt(): lax.dot_general(first_op, second_op, (((0,), (0,)), ((), ())), preferred_...  10.6 us
    all_gather x1, blocking collectives, local(): lax.all_gather(all_shares, 'rep', axis=0, tiled=False).astype(jnp.float32)  10.2 us
  transfers between devices with their start and end apart: 3, of which 2 were waited for; matrix products, arithmetic and copies ran while one was open for 7% of the time, Pallas kernels for 14%

profile of v11, /device:TPU:1, one launch (start us, length us, event | category | flops | bytes accessed | tf_op | source)
XLA Modules:
  0.0 472.9 jit_solution(16734956575529471735)
XLA Ops:
  9.7 1.7 reshape_squeeze.23
  11.4 1.7 dynamic-slice_reduce_fusion
  17.7 14.2 %shard_map.169 = bf16[512,1152]{1,0:T(8,128)(2,1)} custom-call(bf16[128,1152]{1,0:T(8,128)(2,1)} %pad_maximum_fusion.4.x_ref), custom_call_target="tpu_custom_call" | custom-call | tf_op jit(solution)/shard_map/pallas_call | solution.py:122
  34.0 88.2 %all-gather.4.cloned.1.call-done = bf16[3964928]{0:T(1024)(128)(2,1)} async-done(((bf16[123904]{0:T(1024)(128)(2,1)}), bf16[3964928]{0:T(1024)(128)(2,1)}) %all-gather.4.cloned.1.call-update) | async-done | bytes 7929872 | tf_op jit(solution)/shard_map/all_gather | solution.py:210
  122.2 8.3 %reshape.404 = bf16[32,123904]{1,0:T(8,128)(2,1)} reshape(bf16[3964928]{0:T(1024)(128)(2,1)} %all-gather.4.cloned.1.call-done) | data formatting | bytes 15859712 | tf_op jit(solution)/shard_map/all_gather | solution.py:210
  132.8 5.7 %fusion.77 = (bf16[32,32768]{1,0:T(8,128)(2,1)}, bf16[32,32768]{1,0:T(8,128)(2,1)}, bf16[32,32768]{1,0:T(8,128)(2,1)}) fusion(bf16[32,123904]{1,0:T(8,128)(2,1)} %reshape.404), kind=kLoop, calls=%fused_computation.142 | loop fusion | bytes 12582912 | tf_op jit(solution)/shard_map/slice | solution.py:211
  140.9 3.9 fusion.32
  146.3 2.1 fusion.34
  148.3 1.8 copy.65
  150.1 1.8 copy.66
  152.8 2.4 reshape.376
  155.1 2.4 fusion.2
  159.5 2.8 fusion.44.p_ref
  162.3 19.7 %shard_map.170 = f32[128,1024]{1,0:T(8,128)} custom-call(f32[512,1024]{1,0:T(8,128)} %fusion.44.p_ref), custom_call_target="tpu_custom_call" | custom-call | tf_op jit(solution)/shard_map/pallas_call | solution.py:173
  184.5 11.8 %shard_map.171 = bf16[512,1024]{1,0:T(8,128)(2,1)} custom-call(bf16[128,1024]{1,0:T(8,128)(2,1)} %fusion.41.x_ref), custom_call_target="tpu_custom_call" | custom-call | tf_op jit(solution)/shard_map/pallas_call | solution.py:122
  196.3 4.4 reshape.378
  200.6 2.5 reshape.379
  203.2 4.8 %multiply_convert_fusion.1 = (bf16[512,1024]{1,0:T(8,128)(2,1)S(1)}, f32[512,1024]{1,0:T(8,128)}) fusion(f32[1024]{0:T(1024)S(1)} %reshape.400, bf16[512,1024]{1,0:T(8,128)(2,1)} %shard_map.171, bf16[1024,1024]{1,0:T(8,128)(2,1)} %reshape.378), kind=kOutput, calls=%fused_computation.20 | convolution fusion | flops 1076887552 | bytes 6295552 | tf_op jit(solution)/shard_map/dot_general | solution.py:41
  209.0 2.6 fusion.84.p_ref
  211.6 18.8 %shard_map.172 = f32[128,1024]{1,0:T(8,128)} custom-call(f32[512,1024]{1,0:T(8,128)} %fusion.84.p_ref), custom_call_target="tpu_custom_call" | custom-call | tf_op jit(solution)/shard_map/pallas_call | solution.py:173
  234.1 11.8 %shard_map.173 = bf16[512,1024]{1,0:T(8,128)(2,1)} custom-call(bf16[128,1024]{1,0:T(8,128)(2,1)} %convert_element_type.195.x_ref), custom_call_target="tpu_custom_call" | custom-call | tf_op jit(solution)/shard_map/pallas_call | solution.py:122
  246.0 4.6 fusion.83
  250.6 2.6 fusion.39.p_ref
  253.2 18.8 %shard_map.174 = f32[128,1024]{1,0:T(8,128)} custom-call(f32[512,1024]{1,0:T(8,128)} %fusion.39.p_ref), custom_call_target="tpu_custom_call" | custom-call | tf_op jit(solution)/shard_map/pallas_call | solution.py:173
  274.3 11.7 %shard_map.175 = bf16[512,1024]{1,0:T(8,128)(2,1)} custom-call(bf16[128,1024]{1,0:T(8,128)(2,1)} %convert_element_type.197.x_ref), custom_call_target="tpu_custom_call" | custom-call | tf_op jit(solution)/shard_map/pallas_call | solution.py:122
  286.0 1.8 convolution_convert_fusion.4
  287.9 2.8 fusion.85
  292.7 7.7 %fusion.28 = bf16[4,64,512]{2,1,0:T(8,128)(2,1)S(1)} fusion(bf16[512,4,64]{0,2,1:T(8,128)(2,1)S(1)} %bitcast.125, f32[4,512,512]{1,2,0:T(8,128)} %fusion.85, f32[4,512,512]{1,2,0:T(8,128)} %copy-done.25, f32[4,512]{1,0:T(4,128)S(1)} %log.8, pred[512,512]{0,1:T(8,128)(4,1)S(1)} %copy-done.12), kind=kOutput, calls=%fused_computation.32 | convolution fusion | flops 145885696 | bytes 9183232 | tf_op jit(solution)/shard_map/shqk,sqhe->skhe/dot_general | solution.py:302
  300.4 8.8 %fusion.80 = (bf16[4,64]{1,0:T(4,128)(2,1)S(1)}, bf16[1,512,4,64]{1,3,2,0:T(8,128)(2,1)S(1)}) fusion(bf16[512,4,64]{0,2,1:T(8,128)(2,1)S(1)} %bitcast.123, f32[4,512,512]{1,2,0:T(8,128)} %fusion.85, f32[4,512]{1,0:T(4,128)S(1)} %log.8, f32[4,512,512]{1,2,0:T(8,128)} %copy-done.25, pred[512,512]{0,1:T(8,128)(4,1)S(1)} %copy-done.12), kind=kOutput, calls=%fused_computation.145 | convolution fusion | flops 146016512 | bytes 9183744 | tf_op jit(solution)/shard_map/shqk,skhe->sqhe/dot_general | solution.py:299
  310.0 2.3 convolution_convert_fusion.2
  315.5 11.8 %shard_map.177 = bf16[2048,256]{1,0:T(8,128)(2,1)} custom-call(bf16[512,256]{1,0:T(8,128)(2,1)} %copy.72.x_ref), custom_call_target="tpu_custom_call" | custom-call | tf_op jit(solution)/shard_map/pallas_call | solution.py:122
  327.3 2.3 copy.73
  329.6 2.5 convolution_convert_fusion.3
  337.1 6.3 %all-to-all-start = ((bf16[32,8,4224]{2,1,0:T(8,128)(2,1)}), bf16[32,8,4224]{2,1,0:T(8,128)(2,1)S(1)}, u32[]{:S(2)}, u32[]{:S(2)}) async-start(bf16[32,8,4224]{2,1,0:T(8,128)(2,1)} %bitcast.103), calls=%async_computation | async-start | bytes 4325376 | tf_op jit(solution)/shard_map/all_to_all | solution.py:335
  343.3 4.2 convolution_convert_fusion
  347.5 4.5 concatenate.33
  352.1 4.2 convolution_convert_fusion.1
  356.2 4.5 concatenate.32
  360.8 4.9 %pad_maximum_fusion = bf16[32,8,8192]{2,1,0:T(8,128)(2,1)} fusion(bf16[32,4,8192]{2,1,0:T(4,128)(2,1)} %concatenate.33, bf16[32,4,8192]{2,1,0:T(4,128)(2,1)} %concatenate.32), kind=kLoop, calls=%fused_computation.1 | loop fusion | flops 8388608 | bytes 8388608 | tf_op jit(solution)/shard_map/concatenate | solution.py:271
  365.7 6.8 %all-to-all-done = bf16[32,8,4224]{2,1,0:T(8,128)(2,1)S(1)} async-done(((bf16[32,8,4224]{2,1,0:T(8,128)(2,1)}), bf16[32,8,4224]{2,1,0:T(8,128)(2,1)S(1)}, u32[]{:S(2)}, u32[]{:S(2)}) %all-to-all-start) | async-done | bytes 2162720 | tf_op jit(solution)/shard_map/all_to_all | solution.py:335
  372.5 5.8 %all-to-all-start.1 = ((bf16[32,8,8192]{2,1,0:T(8,128)(2,1)}), bf16[32,8,8192]{2,1,0:T(8,128)(2,1)}, u32[]{:S(2)}, u32[]{:S(2)}) async-start(bf16[32,8,8192]{2,1,0:T(8,128)(2,1)} %pad_maximum_fusion), calls=%async_computation.1 | async-start | bytes 8388608 | tf_op jit(solution)/shard_map/all_to_all | solution.py:275
  378.3 3.8 fusion.46.p_ref
  382.2 53.8 %shard_map.176 = f32[128,1024]{1,0:T(8,128)} custom-call(f32[512,1024]{1,0:T(8,128)} %fusion.46.p_ref), custom_call_target="tpu_custom_call" | custom-call | tf_op jit(solution)/shard_map/pallas_call | solution.py:173
  436.0 1.9 add_bitcast_fusion
  438.3 2.8 reduce_sum.242
  441.2 10.2 %all-gather.1 = bf16[397312]{0:T(1024)(128)(2,1)S(1)} all-gather(bf16[99328]{0:T(1024)(128)(2,1)S(1)} %pad_maximum_fusion.5), channel_id=3, replica_groups=mesh['rep'=4,'shard'=32] {'rep'}, dimensions={0}, use_global_device_ids=true | all-gather | bytes 993280 | tf_op jit(solution)/shard_map/all_gather | solution.py:338
  455.8 3.1 copy.90
  459.0 4.4 broadcast_in_dim_reshape.20
  (187 shorter events, 45.5 us)
Async XLA Ops:
  7.2 6.1 %copy-start = (bf16[1,128,1024]{2,1,0:T(8,128)(2,1)S(1)}, bf16[1,128,1024]{2,1,0:T(8,128)(2,1)}, u32[]{:S(2)}) copy-start(bf16[1,128,1024]{2,1,0:T(8,128)(2,1)} %param.16) | copy-start | bytes 786436
  7.2 6.7 %copy-start.16 = (bf16[1,128]{1,0:T(2,128)(2,1)S(1)}, bf16[1,128]{1,0:T(2,128)(2,1)}, u32[]{:S(2)}) copy-start(bf16[1,128]{1,0:T(2,128)(2,1)} %param.19) | copy-start | bytes 772
  7.2 7.4 %copy-start.15 = (bf16[1,6,32]{2,1,0:T(8,128)(2,1)S(1)}, bf16[1,6,32]{2,1,0:T(8,128)(2,1)}, u32[]{:S(2)}) copy-start(bf16[1,6,32]{2,1,0:T(8,128)(2,1)} %param.17) | copy-start | bytes 1156
  7.2 7.5 %copy-start.17 = (bf16[1,2,32]{2,1,0:T(2,128)(2,1)S(1)}, bf16[1,2,32]{2,1,0:T(2,128)(2,1)}, u32[]{:S(2)}) copy-start(bf16[1,2,32]{2,1,0:T(2,128)(2,1)} %param.18) | copy-start | bytes 388
  7.2 114.9 %all-gather.4.cloned.1.call-start = ((), (), s32[]{:S(2)}) async-start(), calls=%async_computation.2 | async-start | bytes 8177664 | tf_op jit(solution)/shard_map/all_gather | solution.py:210
  8.7 8.1 %copy-start.18 = (s32[1,128]{1,0:T(1,128)S(1)}, s32[1,128]{1,0:T(1,128)}, u32[]{:S(2)}) copy-start(s32[1,128]{1,0:T(1,128)} %param.11) | copy-start | bytes 1540
  8.7 8.1 %copy-start.7 = (f32[1,128,1024]{2,1,0:T(8,128)S(1)}, f32[1,128,1024]{2,1,0:T(8,128)}, u32[]{:S(2)}) copy-start(f32[1,128,1024]{2,1,0:T(8,128)} %param.10) | copy-start | bytes 1572868
  13.4 18.5 %copy-start.4 = (f32[1,128,1024]{2,1,0:T(8,128)S(1)}, f32[1,128,1024]{2,1,0:T(8,128)}, u32[]{:S(2)}) copy-start(f32[1,128,1024]{2,1,0:T(8,128)} %param.12) | copy-start | bytes 1572868
  132.8 6.5 %slice-start = ((bf16[32,123904]{1,0:T(8,128)(2,1)}), bf16[32,24576]{1,0:T(8,128)(2,1)S(1)}, s32[]{:S(2)}) async-start(bf16[32,123904]{1,0:T(8,128)(2,1)} %reshape.404), calls=%async_computation.3 | async-start | bytes 3145728 | tf_op jit(solution)/shard_map/slice | solution.py:211
  144.8 8.0 %copy-start.3 = (bf16[32,32768]{1,0:T(8,128)(2,1)S(1)}, bf16[32,32768]{1,0:T(8,128)(2,1)}, u32[]{:S(2)}) copy-start(bf16[32,32768]{1,0:T(8,128)(2,1)} %get-tuple-element.35) | copy-start | bytes 6291460
  152.8 2.4 copy-start.10
  155.1 2.4 copy-start.8
  155.1 2.4 copy-start.11
  157.5 1.9 copy-start.25
  196.2 4.4 copy-start.2
  203.2 5.8 %copy-start.6 = (bf16[1024,1024]{1,0:T(8,128)(2,1)S(1)}, bf16[1024,1024]{1,0:T(8,128)(2,1)}, u32[]{:S(2)}) copy-start(bf16[1024,1024]{1,0:T(8,128)(2,1)} %reshape.379) | copy-start | bytes 6291460
  208.0 1.0 copy-start.27
  246.0 4.6 copy-start.5
  250.6 2.7 copy-start.28
  273.5 14.4 %copy-start.9 = (bf16[512,256]{0,1:T(8,128)(2,1)S(1)}, bf16[512,256]{0,1:T(8,128)(2,1)}, u32[]{:S(2)}) copy-start(bf16[512,256]{0,1:T(8,128)(2,1)} %copy.65) | copy-start | bytes 786436
  287.9 2.9 copy-start.12
  287.9 3.6 copy-start.26
  291.6 1.1 copy-start.14
  292.7 17.4 %copy-start.19 = (bf16[1,512,4,64]{1,3,2,0:T(8,128)(2,1)}, bf16[1,512,4,64]{1,3,2,0:T(8,128)(2,1)S(1)}, u32[]{:S(2)}) copy-start(bf16[1,512,4,64]{1,3,2,0:T(8,128)(2,1)S(1)} %get-tuple-element.42) | copy-start | bytes 786436
  292.7 7.7 %copy-start.13 = (bf16[512,256]{0,1:T(8,128)(2,1)S(1)}, bf16[512,256]{0,1:T(8,128)(2,1)}, u32[]{:S(2)}) copy-start(bf16[512,256]{0,1:T(8,128)(2,1)} %copy.67) | copy-start | bytes 786436
  300.4 9.7 %copy-start.21 = (bf16[4,64,512]{2,1,0:T(8,128)(2,1)}, bf16[4,64,512]{2,1,0:T(8,128)(2,1)S(1)}, u32[]{:S(2)}) copy-start(bf16[4,64,512]{2,1,0:T(8,128)(2,1)S(1)} %fusion.28) | copy-start | bytes 786436
  309.2 3.1 copy-start.23
  337.1 35.4 %all-to-all-start = ((bf16[32,8,4224]{2,1,0:T(8,128)(2,1)}), bf16[32,8,4224]{2,1,0:T(8,128)(2,1)S(1)}, u32[]{:S(2)}, u32[]{:S(2)}) async-start(bf16[32,8,4224]{2,1,0:T(8,128)(2,1)} %bitcast.103), calls=%async_computation | async-start | bytes 4325376 | tf_op jit(solution)/shard_map/all_to_all | solution.py:335
  365.7 12.6 %copy-start.20 = (bf16[1,512,4,64]{1,3,2,0:T(8,128)(2,1)S(1)}, bf16[1,512,4,64]{1,3,2,0:T(8,128)(2,1)}, u32[]{:S(2)}) copy-start(bf16[1,512,4,64]{1,3,2,0:T(8,128)(2,1)} %copy-done.19) | copy-start | bytes 786436
  365.7 12.7 %copy-start.22 = (bf16[4,64,512]{2,1,0:T(8,128)(2,1)S(1)}, bf16[4,64,512]{2,1,0:T(8,128)(2,1)}, u32[]{:S(2)}) copy-start(bf16[4,64,512]{2,1,0:T(8,128)(2,1)} %copy-done.21) | copy-start | bytes 786436
  365.7 12.7 %copy-start.24 = (bf16[1,512,4,64]{1,3,2,0:T(8,128)(2,1)S(1)}, bf16[1,512,4,64]{1,3,2,0:T(8,128)(2,1)}, u32[]{:S(2)}) copy-start(bf16[1,512,4,64]{1,3,2,0:T(8,128)(2,1)} %copy-done.23) | copy-start | bytes 786436
  372.5 65.8 %all-to-all-start.1 = ((bf16[32,8,8192]{2,1,0:T(8,128)(2,1)}), bf16[32,8,8192]{2,1,0:T(8,128)(2,1)}, u32[]{:S(2)}, u32[]{:S(2)}) async-start(bf16[32,8,8192]{2,1,0:T(8,128)(2,1)} %pad_maximum_fusion), calls=%async_computation.1 | async-start | bytes 8388608 | tf_op jit(solution)/shard_map/all_to_all | solution.py:275
  455.8 10.0 %copy-start.1 = (bf16[1,128,1024]{2,1,0:T(8,128)(2,1)S(1)}, bf16[1,128,1024]{2,1,0:T(8,128)(2,1)}, u32[]{:S(2)}) copy-start(bf16[1,128,1024]{2,1,0:T(8,128)(2,1)} %param.16) | copy-start | bytes 786436
Sparse Core Ops, SparseCore 0:
  16.9 105.2 all-gather.3
